TPU v7x, 32 devices: a whole 2x2x4 slice. The times are simulated.
32 devices in a mesh: dp: 4 (over y, x), seq: 8 (over z, core).
Axes of the slice: x: 2, y: 2, z: 4, core: 2. Of those that a mesh axis runs over, the one named last changes fastest.
Arguments:
- inputs: bfloat16 [2, 4, 1024, 768], P(None, 'dp', 'seq'), may hold values from -6 to 6
- segments: int32 [2, 4, 1024], P(None, 'dp'), may hold values from 0 to 2, never falling along the last dimension, each value on 1 to 512 neighbouring positions
- w_query: float32 [768, 768], P(('dp', 'seq')), may hold values from -0.21875 to 0.21875
- b_query: float32 [768], P(('dp', 'seq')), may hold values from -3 to 3
- w_key: float32 [768, 768], P(('dp', 'seq')), may hold values from -0.21875 to 0.21875
- w_value: float32 [768, 768], P(('dp', 'seq')), may hold values from -0.21875 to 0.21875
- b_value: float32 [768], P(('dp', 'seq')), may hold values from -0.3125 to 0.3125
- w_output: float32 [768, 768], P(('dp', 'seq')), may hold values from -1.75 to 1.75
- b_output: float32 [768], P(('dp', 'seq')), may hold values from -1.75 to 1.75
- gain_first: float32 [768], P(('dp', 'seq')), may hold values from 0.5 to 1.5
- shift_first: float32 [768], P(('dp', 'seq')), may hold values from -1.75 to 1.75
- w_inner: float32 [768, 3072], P(('dp', 'seq')), may hold values from -0.21875 to 0.21875
- b_inner: float32 [3072], P(('dp', 'seq')), may hold values from -1.75 to 1.75
- w_outer: float32 [3072, 768], P(('dp', 'seq')), may hold values from -0.109375 to 0.109375
- b_outer: float32 [768], P(('dp', 'seq')), may hold values from -1.75 to 1.75
- gain_second: float32 [768], P(('dp', 'seq')), may hold values from 0.5 to 1.5
- shift_second: float32 [768], P(('dp', 'seq')), may hold values from -1.75 to 1.75
- cotangent: bfloat16 [2, 4, 1024, 768], P(None, 'dp', 'seq'), may hold values from -6 to 6
Outputs:
- outputs: bfloat16 [2, 4, 1024, 768], P(None, 'dp', 'seq')
- grad_inputs: bfloat16 [2, 4, 1024, 768], P(None, 'dp', 'seq')
- grad_w_query: float32 [768, 768], P(('dp', 'seq'))
- grad_b_query: float32 [768], P(('dp', 'seq'))
- grad_w_key: float32 [768, 768], P(('dp', 'seq'))
- grad_w_value: float32 [768, 768], P(('dp', 'seq'))
- grad_b_value: float32 [768], P(('dp', 'seq'))
- grad_w_output: float32 [768, 768], P(('dp', 'seq'))
- grad_b_output: float32 [768], P(('dp', 'seq'))
- grad_gain_first: float32 [768], P(('dp', 'seq'))
- grad_shift_first: float32 [768], P(('dp', 'seq'))
- grad_w_inner: float32 [768, 3072], P(('dp', 'seq'))
- grad_b_inner: float32 [3072], P(('dp', 'seq'))
- grad_w_outer: float32 [3072, 768], P(('dp', 'seq'))
- grad_b_outer: float32 [768], P(('dp', 'seq'))
- grad_gain_second: float32 [768], P(('dp', 'seq'))
- grad_shift_second: float32 [768], P(('dp', 'seq'))
Inputs may be any that keep to these rules, and one draw needn't show every extreme that they name: `segments`: segment numbers never fall along a sequence; a document has 1 to 512 tokens and one has exactly 512.
All inputs are finite; a program needn't handle non-finite values.
Results may differ from a plain program's by a relative error of at most 0.017.
Values may be sent and summed in bfloat16 or wider, within the bound.
No kernel may reach another device: no remote copies, remote signals or barrier semaphores. Data moves between devices by JAX's collectives and lax.ppermute only.
A program may use at most 256 MiB of HBM per device.

v0:
```python
import math

import jax
import jax.numpy as jnp
from jax import lax
from jax.sharding import PartitionSpec as P

HEADS = 12
HEAD_DIM = 64


def narrow(masters):
    return tuple((item.astype(jnp.bfloat16) for item in masters))


def fetch_forward(masters):
    lowered = narrow(masters)
    return (
        lax.all_gather(lowered[0], ("dp", "seq"), axis=0, tiled=True),
        lax.all_gather(lowered[1], ("dp", "seq"), axis=0, tiled=True),
        lax.all_gather(lowered[2], ("dp", "seq"), axis=0, tiled=True),
        lax.all_gather(lowered[3], ("dp", "seq"), axis=0, tiled=True),
        lax.all_gather(lowered[4], ("dp", "seq"), axis=0, tiled=True),
        lax.all_gather(lowered[5], ("dp", "seq"), axis=0, tiled=True),
        lax.all_gather(lowered[6], ("dp", "seq"), axis=0, tiled=True),
        lax.all_gather(lowered[7], ("dp", "seq"), axis=0, tiled=True),
        lax.all_gather(lowered[8], ("dp", "seq"), axis=0, tiled=True),
        lax.all_gather(lowered[9], ("dp", "seq"), axis=0, tiled=True),
        lax.all_gather(lowered[10], ("dp", "seq"), axis=0, tiled=True),
        lax.all_gather(lowered[11], ("dp", "seq"), axis=0, tiled=True),
        lax.all_gather(lowered[12], ("dp", "seq"), axis=0, tiled=True),
        lax.all_gather(lowered[13], ("dp", "seq"), axis=0, tiled=True),
        lax.all_gather(lowered[14], ("dp", "seq"), axis=0, tiled=True),
    )


def fetch_backward(masters):
    lowered = narrow(masters)
    return (
        lax.all_gather(lowered[0], ("dp", "seq"), axis=0, tiled=True),
        lax.all_gather(lowered[1], ("dp", "seq"), axis=0, tiled=True),
        lax.all_gather(lowered[2], ("dp", "seq"), axis=0, tiled=True),
        lax.all_gather(lowered[3], ("dp", "seq"), axis=0, tiled=True),
        lax.all_gather(lowered[4], ("dp", "seq"), axis=0, tiled=True),
        lax.all_gather(lowered[5], ("dp", "seq"), axis=0, tiled=True),
        lax.all_gather(lowered[6], ("dp", "seq"), axis=0, tiled=True),
        lax.all_gather(lowered[7], ("dp", "seq"), axis=0, tiled=True),
        lax.all_gather(lowered[8], ("dp", "seq"), axis=0, tiled=True),
        lax.all_gather(lowered[9], ("dp", "seq"), axis=0, tiled=True),
        lax.all_gather(lowered[10], ("dp", "seq"), axis=0, tiled=True),
        lax.all_gather(lowered[11], ("dp", "seq"), axis=0, tiled=True),
        lax.all_gather(lowered[12], ("dp", "seq"), axis=0, tiled=True),
        lax.all_gather(lowered[13], ("dp", "seq"), axis=0, tiled=True),
        lax.all_gather(lowered[14], ("dp", "seq"), axis=0, tiled=True),
    )


def sum_owners(terms):
    return (
        lax.psum_scatter(terms[0], ("dp", "seq"), scatter_dimension=0, tiled=True),
        lax.psum_scatter(terms[1], ("dp", "seq"), scatter_dimension=0, tiled=True),
        lax.psum_scatter(terms[2], ("dp", "seq"), scatter_dimension=0, tiled=True),
        lax.psum_scatter(terms[3], ("dp", "seq"), scatter_dimension=0, tiled=True),
        lax.psum_scatter(terms[4], ("dp", "seq"), scatter_dimension=0, tiled=True),
        lax.psum_scatter(terms[5], ("dp", "seq"), scatter_dimension=0, tiled=True),
        lax.psum_scatter(terms[6], ("dp", "seq"), scatter_dimension=0, tiled=True),
        lax.psum_scatter(terms[7], ("dp", "seq"), scatter_dimension=0, tiled=True),
        lax.psum_scatter(terms[8], ("dp", "seq"), scatter_dimension=0, tiled=True),
        lax.psum_scatter(terms[9], ("dp", "seq"), scatter_dimension=0, tiled=True),
        lax.psum_scatter(terms[10], ("dp", "seq"), scatter_dimension=0, tiled=True),
        lax.psum_scatter(terms[11], ("dp", "seq"), scatter_dimension=0, tiled=True),
        lax.psum_scatter(terms[12], ("dp", "seq"), scatter_dimension=0, tiled=True),
        lax.psum_scatter(terms[13], ("dp", "seq"), scatter_dimension=0, tiled=True),
        lax.psum_scatter(terms[14], ("dp", "seq"), scatter_dimension=0, tiled=True),
    )


def layer_norm(z, gain, shift):
    mean = jnp.mean(z, axis=-1, keepdims=True)
    centered = z - mean
    rstd = lax.rsqrt(jnp.mean(centered * centered, axis=-1, keepdims=True) + 1e-05)
    normed = centered * rstd
    return (normed * gain + shift, normed, rstd)


def norm_back(grad, normed, rstd, gain):
    scaled = grad * gain
    inner = (
        scaled
        - jnp.mean(scaled, axis=-1, keepdims=True)
        - normed * jnp.mean(scaled * normed, axis=-1, keepdims=True)
    )
    return (rstd * inner, jnp.sum(grad * normed, axis=0), jnp.sum(grad, axis=0))


def gelu_exact(value):
    return jax.nn.gelu(value, approximate=False)


def key_blocks(keys_all, values_all, seg_row):
    length = keys_all.shape[0]
    width = math.gcd(length, 1024)
    count = length // width
    keys_split = keys_all.reshape(count, width, HEADS, HEAD_DIM)
    values_split = values_all.reshape(count, width, HEADS, HEAD_DIM)
    return (keys_split, values_split, seg_row.reshape(count, width))


def block_scores(queries, keys, query_seg, key_seg):
    scores = jnp.einsum("qhd,khd->hqk", queries, keys, preferred_element_type=jnp.float32) * 0.125
    same = (query_seg[:, None] == key_seg[None, :])[None]
    return jnp.where(same, scores, -1e30)


def attend(queries, keys_all, values_all, seg_row, query_seg):
    rows = queries.shape[0]
    query_h = queries.reshape(rows, HEADS, HEAD_DIM)
    keys_split, values_split, seg_split = key_blocks(keys_all, values_all, seg_row)

    def first_pass(carry, block):
        top, total = carry
        keys, key_seg = block
        scores = block_scores(query_h, keys, query_seg, key_seg)
        new_top = jnp.maximum(top, jnp.max(scores, axis=-1))
        total = total * jnp.exp(top - new_top) + jnp.sum(
            jnp.exp(scores - new_top[..., None]), axis=-1
        )
        return ((new_top, total), None)

    start = (jnp.full((HEADS, rows), -1e30, jnp.float32), jnp.zeros((HEADS, rows), jnp.float32))
    (top, total), _ = lax.scan(first_pass, start, (keys_split, seg_split))
    lse = top + jnp.log(total)

    def second_pass(acc, block):
        keys, values, key_seg = block
        scores = block_scores(query_h, keys, query_seg, key_seg)
        probs = jnp.exp(scores - lse[..., None]).astype(jnp.bfloat16)
        return (
            acc + jnp.einsum("hqk,khd->qhd", probs, values, preferred_element_type=jnp.float32),
            None,
        )

    mixed, _ = lax.scan(
        second_pass,
        jnp.zeros((rows, HEADS, HEAD_DIM), jnp.float32),
        (keys_split, values_split, seg_split),
    )
    return (lse, mixed.reshape(rows, HEADS * HEAD_DIM))


def attend_back(queries, grad_mixed, lse, delta, keys_all, values_all, seg_row, query_seg):
    rows = queries.shape[0]
    query_h = queries.reshape(rows, HEADS, HEAD_DIM)
    grad_h = grad_mixed.reshape(rows, HEADS, HEAD_DIM)
    keys_split, values_split, seg_split = key_blocks(keys_all, values_all, seg_row)

    def step(grad_query, block):
        keys, values, key_seg = block
        scores = block_scores(query_h, keys, query_seg, key_seg)
        probs = jnp.exp(scores - lse[..., None])
        grad_probs = jnp.einsum("qhd,khd->hqk", grad_h, values, preferred_element_type=jnp.float32)
        grad_scores = (probs * (grad_probs - delta[..., None])).astype(jnp.bfloat16)
        grad_query = grad_query + jnp.einsum(
            "hqk,khd->qhd", grad_scores, keys, preferred_element_type=jnp.float32
        )
        grad_keys = (
            jnp.einsum("hqk,qhd->khd", grad_scores, query_h, preferred_element_type=jnp.float32)
            * 0.125
        )
        grad_values = jnp.einsum(
            "hqk,qhd->khd", probs.astype(jnp.bfloat16), grad_h, preferred_element_type=jnp.float32
        )
        width = keys.shape[0]
        joined = jnp.concatenate(
            [
                grad_keys.reshape(width, HEADS * HEAD_DIM),
                grad_values.reshape(width, HEADS * HEAD_DIM),
            ],
            axis=-1,
        )
        return (grad_query, joined)

    grad_query, joined = lax.scan(
        step, jnp.zeros((rows, HEADS, HEAD_DIM), jnp.float32), (keys_split, values_split, seg_split)
    )
    grad_query = (grad_query * 0.125).reshape(rows, HEADS * HEAD_DIM)
    return (grad_query, joined.reshape(keys_all.shape[0], 2 * HEADS * HEAD_DIM))


def outer_sum(left, right):
    return jnp.einsum("tf,tg->fg", left, right, preferred_element_type=jnp.float32)


def times_transposed(left, weight):
    return jnp.einsum("tg,fg->tf", left, weight, preferred_element_type=jnp.float32)


def column_sum(value):
    return jnp.sum(value.astype(jnp.float32), axis=0)


def per_device(
    inputs,
    segments,
    w_query,
    b_query,
    w_key,
    w_value,
    b_value,
    w_output,
    b_output,
    gain_first,
    shift_first,
    w_inner,
    b_inner,
    w_outer,
    b_outer,
    gain_second,
    shift_second,
    cotangent,
):
    masters = (
        w_query,
        b_query,
        w_key,
        w_value,
        b_value,
        w_output,
        b_output,
        gain_first,
        shift_first,
        w_inner,
        b_inner,
        w_outer,
        b_outer,
        gain_second,
        shift_second,
    )
    rows = inputs.shape[2]
    offset = lax.axis_index("seq") * rows
    results = []
    grad_rows = []
    totals = None
    for micro in range(inputs.shape[0]):
        tokens = inputs[micro, 0]
        seg_row = segments[micro, 0]
        query_seg = lax.dynamic_slice_in_dim(seg_row, offset, rows)
        full = fetch_forward(masters)
        wq, bq, wk, wv, bv, wo, bo, g1, s1, w1, b1, w2, b2, g2, s2 = full
        g1f, s1f, g2f, s2f = (
            g1.astype(jnp.float32),
            s1.astype(jnp.float32),
            g2.astype(jnp.float32),
            s2.astype(jnp.float32),
        )
        queries = (
            jnp.dot(tokens, wq, preferred_element_type=jnp.float32) + bq.astype(jnp.float32)
        ).astype(jnp.bfloat16)
        keys = jnp.dot(tokens, wk, preferred_element_type=jnp.float32).astype(jnp.bfloat16)
        values = (
            jnp.dot(tokens, wv, preferred_element_type=jnp.float32) + bv.astype(jnp.float32)
        ).astype(jnp.bfloat16)
        keys_all, values_all = (
            lax.all_gather(keys, "seq", axis=0, tiled=True),
            lax.all_gather(values, "seq", axis=0, tiled=True),
        )
        lse, mixed = attend(queries, keys_all, values_all, seg_row, query_seg)
        mixed_low = mixed.astype(jnp.bfloat16)
        branch = jnp.dot(mixed_low, wo, preferred_element_type=jnp.float32) + bo.astype(jnp.float32)
        hidden, normed_first, rstd_first = layer_norm(tokens.astype(jnp.float32) + branch, g1f, s1f)
        hidden_low = hidden.astype(jnp.bfloat16)
        inner = jnp.dot(hidden_low, w1, preferred_element_type=jnp.float32) + b1.astype(jnp.float32)
        active, gelu_pull = jax.vjp(gelu_exact, inner)
        active_low = active.astype(jnp.bfloat16)
        outer = jnp.dot(active_low, w2, preferred_element_type=jnp.float32) + b2.astype(jnp.float32)
        result, normed_second, rstd_second = layer_norm(hidden + outer, g2f, s2f)
        results.append(result.astype(jnp.bfloat16))
        wq, bq, wk, wv, bv, wo, bo, g1, s1, w1, b1, w2, b2, g2, s2 = fetch_backward(masters)
        keys_all, values_all = (
            lax.all_gather(keys, "seq", axis=0, tiled=True),
            lax.all_gather(values, "seq", axis=0, tiled=True),
        )
        grad_out = cotangent[micro, 0].astype(jnp.float32)
        grad_z2, grad_g2, grad_s2 = norm_back(grad_out, normed_second, rstd_second, g2f)
        grad_outer = grad_z2.astype(jnp.bfloat16)
        grad_w2 = outer_sum(active_low, grad_outer)
        grad_b2 = column_sum(grad_outer)
        grad_active = times_transposed(grad_outer, w2)
        grad_inner = gelu_pull(grad_active)[0].astype(jnp.bfloat16)
        grad_w1 = outer_sum(hidden_low, grad_inner)
        grad_b1 = column_sum(grad_inner)
        grad_hidden = times_transposed(grad_inner, w1) + grad_z2
        grad_z1, grad_g1, grad_s1 = norm_back(grad_hidden, normed_first, rstd_first, g1f)
        grad_branch = grad_z1.astype(jnp.bfloat16)
        grad_wo = outer_sum(mixed_low, grad_branch)
        grad_bo = column_sum(grad_branch)
        grad_mixed = times_transposed(grad_branch, wo).astype(jnp.bfloat16)
        delta = jnp.sum(
            (grad_mixed.astype(jnp.float32) * mixed).reshape(rows, HEADS, HEAD_DIM), axis=-1
        ).T
        grad_query, joined = attend_back(
            queries, grad_mixed, lse, delta, keys_all, values_all, seg_row, query_seg
        )
        summed = lax.psum_scatter(
            joined.astype(jnp.bfloat16), "seq", scatter_dimension=0, tiled=True
        ).astype(jnp.float32)
        width = summed.shape[1] // 2
        grad_keys = summed[:, :width].astype(jnp.bfloat16)
        grad_values = summed[:, width:].astype(jnp.bfloat16)
        grad_query = grad_query.astype(jnp.bfloat16)
        grad_wq = outer_sum(tokens, grad_query)
        grad_wk = outer_sum(tokens, grad_keys)
        grad_wv = outer_sum(tokens, grad_values)
        grad_bq = column_sum(grad_query)
        grad_bv = column_sum(grad_values)
        grad_tokens = (
            times_transposed(grad_query, wq)
            + times_transposed(grad_keys, wk)
            + times_transposed(grad_values, wv)
            + grad_z1
        )
        grad_rows.append(grad_tokens.astype(jnp.bfloat16))
        terms = (
            grad_wq,
            grad_bq,
            grad_wk,
            grad_wv,
            grad_bv,
            grad_wo,
            grad_bo,
            grad_g1,
            grad_s1,
            grad_w1,
            grad_b1,
            grad_w2,
            grad_b2,
            grad_g2,
            grad_s2,
        )
        totals = terms if totals is None else tuple((old + new for old, new in zip(totals, terms)))
    owned = sum_owners(totals)
    outputs = jnp.stack(results)[:, None]
    grad_inputs = jnp.stack(grad_rows)[:, None]
    return (
        outputs,
        grad_inputs,
        owned[0],
        owned[1],
        owned[2],
        owned[3],
        owned[4],
        owned[5],
        owned[6],
        owned[7],
        owned[8],
        owned[9],
        owned[10],
        owned[11],
        owned[12],
        owned[13],
        owned[14],
    )


def solution(mesh):
    in_specs = (
        P(None, "dp", "seq", None),
        P(None, "dp", None),
        P(("dp", "seq"), None),
        P(("dp", "seq")),
        P(("dp", "seq"), None),
        P(("dp", "seq"), None),
        P(("dp", "seq")),
        P(("dp", "seq"), None),
        P(("dp", "seq")),
        P(("dp", "seq")),
        P(("dp", "seq")),
        P(("dp", "seq"), None),
        P(("dp", "seq")),
        P(("dp", "seq"), None),
        P(("dp", "seq")),
        P(("dp", "seq")),
        P(("dp", "seq")),
        P(None, "dp", "seq", None),
    )
    out_specs = (
        P(None, "dp", "seq", None),
        P(None, "dp", "seq", None),
        P(("dp", "seq"), None),
        P(("dp", "seq")),
        P(("dp", "seq"), None),
        P(("dp", "seq"), None),
        P(("dp", "seq")),
        P(("dp", "seq"), None),
        P(("dp", "seq")),
        P(("dp", "seq")),
        P(("dp", "seq")),
        P(("dp", "seq"), None),
        P(("dp", "seq")),
        P(("dp", "seq"), None),
        P(("dp", "seq")),
        P(("dp", "seq")),
        P(("dp", "seq")),
    )
    return jax.shard_map(
        per_device, mesh=mesh, in_specs=in_specs, out_specs=out_specs, check_vma=False
    )
```

profile of v0, /device:TPU:0, one launch (start us, length us, event | category | flops | bytes accessed | tf_op | source)
XLA Modules:
  0.0 1312.7 jit_solution(14285759591236713342)
XLA Ops:
  19.8 42.4 %all-reduce.19 = (bf16[3072]{0:T(1024)(128)(2,1)S(1)}, bf16[768]{0:T(1024)(128)(2,1)S(1)}, bf16[768]{0:T(1024)(128)(2,1)S(1)}, bf16[768]{0:T(1024)(128)(2,1)S(1)...) all-reduce(bf16[3072]{0:T(1024)(128)(2,1)S(1)} %dynamic-update-slic, ...), channel_id=1, replica_groups=mesh['dp'=4,'seq'=8] {'dp','seq'}, use_global_device_ids=true, to_apply=%add.5 | all-reduce | flops 9216 | bytes 36864
  62.2 6.6 all-gather.11.cloned.1.call-done
  71.3 54.4 %all-gather.17.cloned.1.call-done = bf16[768,768]{1,0:T(8,128)(2,1)} async-done(((bf16[24,768]{1,0:T(8,128)(2,1)}), bf16[768,768]{1,0:T(8,128)(2,1)}) %all-gather.17.cloned.1.call-update) | async-done | bytes 1179664 | tf_op jit(solution)/shard_map/all_gather | solution.py:21
  134.2 48.2 %all-gather.15.cloned.1.call-done = bf16[768,768]{1,0:T(8,128)(2,1)} async-done(((bf16[24,768]{1,0:T(8,128)(2,1)}), bf16[768,768]{1,0:T(8,128)(2,1)}) %all-gather.15.cloned.1.call-update) | async-done | bytes 1179664 | tf_op jit(solution)/shard_map/all_gather | solution.py:19
  184.8 23.7 %all-gather.13.cloned.1.call-done = bf16[1024,768]{1,0:T(8,128)(2,1)} async-done(((bf16[128,768]{1,0:T(8,128)(2,1)}), bf16[1024,768]{1,0:T(8,128)(2,1)}) %all-gather.13.cloned.1.call-update) | async-done | bytes 1572880 | tf_op jit(solution)/shard_map/all_gather | solution.py:265
  211.6 23.6 %all-gather.19.cloned.1.call-done = bf16[1024,768]{1,0:T(8,128)(2,1)} async-done(((bf16[128,768]{1,0:T(8,128)(2,1)}), bf16[1024,768]{1,0:T(8,128)(2,1)}) %all-gather.19.cloned.1.call-update) | async-done | bytes 1572880 | tf_op jit(solution)/shard_map/all_gather | solution.py:264
  243.4 18.4 %all-gather.27.cloned.1.call-done = bf16[1024,768]{1,0:T(8,128)(2,1)} async-done(((bf16[128,768]{1,0:T(8,128)(2,1)}), bf16[1024,768]{1,0:T(8,128)(2,1)}) %all-gather.27.cloned.1.call-update) | async-done | bytes 1572880 | tf_op jit(solution)/shard_map/all_gather | solution.py:265
  264.5 23.6 %all-gather.29.cloned.1.call-done = bf16[1024,768]{1,0:T(8,128)(2,1)} async-done(((bf16[128,768]{1,0:T(8,128)(2,1)}), bf16[1024,768]{1,0:T(8,128)(2,1)}) %all-gather.29.cloned.1.call-update) | async-done | bytes 1572880 | tf_op jit(solution)/shard_map/all_gather | solution.py:264
  289.9 55.6 %all-gather.21.cloned.1.call-done = bf16[768,768]{1,0:T(8,128)(2,1)} async-done(((bf16[24,768]{1,0:T(8,128)(2,1)}), bf16[768,768]{1,0:T(8,128)(2,1)}) %all-gather.21.cloned.1.call-update) | async-done | bytes 1179664 | tf_op jit(solution)/shard_map/all_gather | solution.py:24
  353.7 57.4 %all-gather.23.cloned.1.call-done = bf16[768,3072]{1,0:T(8,128)(2,1)} async-done(((bf16[24,3072]{1,0:T(8,128)(2,1)}), bf16[768,3072]{1,0:T(8,128)(2,1)}) %all-gather.23.cloned.1.call-update) | async-done | bytes 4718608 | tf_op jit(solution)/shard_map/all_gather | solution.py:28
  411.1 8.6 multiply_convert_fusion.5
  419.8 56.7 %all-gather.25.cloned.1.call-done = bf16[3072,768]{1,0:T(8,128)(2,1)} async-done(((bf16[96,768]{1,0:T(8,128)(2,1)}), bf16[3072,768]{1,0:T(8,128)(2,1)}) %all-gather.25.cloned.1.call-update) | async-done | bytes 4718608 | tf_op jit(solution)/shard_map/all_gather | solution.py:30
  502.4 6.0 convolution_convert_fusion.1
  510.0 5.2 multiply_convert_fusion.1
  534.9 6.0 multiply_convert_fusion
  570.8 34.6 %reduce-scatter.27.cloned.1.call-done = bf16[128,1536]{1,0:T(8,128)(2,1)} async-done(((bf16[1024,1536]{1,0:T(8,128)(2,1)}), bf16[128,1536]{1,0:T(8,128)(2,1)}) %reduce-scatter.27.cloned.1.call-update) | async-done | bytes 393232
  621.4 5.2 convolution_add_fusion.1
  644.8 39.4 %all-reduce.18 = (f32[768]{0:T(1024)S(1)}, f32[768]{0:T(1024)S(1)}, f32[768]{0:T(1024)S(1)}, f32[768]{0:T(1024)S(1)}, f32[768]{0:T(1024)S(1)}, /*index=5*/f32[30...) all-reduce(f32[768]{0:T(1024)} %add.356, ...), channel_id=5, replica_groups=mesh['dp'=4,'seq'=8] {'dp','seq'}, use_global_device_ids=true, to_apply=%region_27.28.clone | all-reduce | flops 9216 | bytes 73728
  694.5 15.0 %reduce-scatter.29.cloned.1.call-done = f32[24,768]{1,0:T(8,128)} async-done(((f32[768,768]{1,0:T(8,128)}), f32[24,768]{1,0:T(8,128)}) %reduce-scatter.29.cloned.1.call-update) | async-done | bytes 73744
  709.6 104.7 %reduce-scatter.19.cloned.1.call-done = f32[24,768]{1,0:T(8,128)} async-done(((f32[768,768]{1,0:T(8,128)}), f32[24,768]{1,0:T(8,128)}) %reduce-scatter.19.cloned.1.call-update) | async-done | bytes 73744 | tf_op jit(solution)/shard_map/reduce_scatter | solution.py:65
  814.3 103.8 %reduce-scatter.31.cloned.1.call-done = f32[24,768]{1,0:T(8,128)} async-done(((f32[768,768]{1,0:T(8,128)}), f32[24,768]{1,0:T(8,128)}) %reduce-scatter.31.cloned.1.call-update) | async-done | bytes 73744
  918.1 104.7 %reduce-scatter.33.cloned.1.call-done = f32[24,768]{1,0:T(8,128)} async-done(((f32[768,768]{1,0:T(8,128)}), f32[24,768]{1,0:T(8,128)}) %reduce-scatter.33.cloned.1.call-update) | async-done | bytes 73744
  1022.8 141.0 %reduce-scatter.21.cloned.1.call-done = f32[24,3072]{1,0:T(8,128)} async-done(((f32[768,3072]{1,0:T(8,128)}), f32[24,3072]{1,0:T(8,128)}) %reduce-scatter.21.cloned.1.call-update) | async-done | bytes 294928 | tf_op jit(solution)/shard_map/reduce_scatter | solution.py:69
  1163.8 141.9 %reduce-scatter.23.cloned.1.call-done = f32[96,768]{1,0:T(8,128)} async-done(((f32[3072,768]{1,0:T(8,128)}), f32[96,768]{1,0:T(8,128)}) %reduce-scatter.23.cloned.1.call-update) | async-done | bytes 294928 | tf_op jit(solution)/shard_map/reduce_scatter | solution.py:71
  (361 shorter events, 170.2 us)
Async XLA Ops:
  7.2 118.5 %copy-start.2 = (bf16[2,1,128,768]{3,2,1,0:T(8,128)(2,1)S(1)}, bf16[2,1,128,768]{3,2,1,0:T(8,128)(2,1)}, u32[]{:S(2)}) copy-start(bf16[2,1,128,768]{3,2,1,0:T(8,128)(2,1)} %param.18) | copy-start | bytes 1179652
  7.2 61.5 %all-gather.11.cloned.1.call-start = ((), (), s32[]{:S(2)}) async-start(), calls=%async_computation.8 | async-start | bytes 1216512 | tf_op jit(solution)/shard_map/all_gather | solution.py:22
  8.8 116.8 %all-gather.17.cloned.1.call-start = ((), (), s32[]{:S(2)}) async-start(), calls=%async_computation.11 | async-start | bytes 1216512 | tf_op jit(solution)/shard_map/all_gather | solution.py:21
  10.4 172.0 %all-gather.15.cloned.1.call-start = ((), (), s32[]{:S(2)}) async-start(), calls=%async_computation.10 | async-start | bytes 1216512 | tf_op jit(solution)/shard_map/all_gather | solution.py:19
  12.0 196.5 %all-gather.13.cloned.1.call-start = ((), (), s32[]{:S(2)}) async-start(), calls=%async_computation.9 | async-start | bytes 1769472 | tf_op jit(solution)/shard_map/all_gather | solution.py:265
  68.7 59.3 %copy-start.5 = (bf16[768,768]{1,0:T(8,128)(2,1)S(1)}, bf16[768,768]{1,0:T(8,128)(2,1)}, u32[]{:S(2)}) copy-start(bf16[768,768]{1,0:T(8,128)(2,1)} %all-gather.11.cloned.1.call-done) | copy-start | bytes 3538948
  71.2 163.9 %all-gather.19.cloned.1.call-start = ((), (), s32[]{:S(2)}) async-start(), calls=%async_computation.12 | async-start | bytes 1769472 | tf_op jit(solution)/shard_map/all_gather | solution.py:264
  128.0 133.9 %all-gather.27.cloned.1.call-start = ((), (), s32[]{:S(2)}) async-start(), calls=%async_computation.16 | async-start | bytes 1769472 | tf_op jit(solution)/shard_map/all_gather | solution.py:265
  129.1 159.0 %all-gather.29.cloned.1.call-start = ((), (), s32[]{:S(2)}) async-start(), calls=%async_computation.17 | async-start | bytes 1769472 | tf_op jit(solution)/shard_map/all_gather | solution.py:264
  131.4 214.0 %all-gather.21.cloned.1.call-start = ((), (), s32[]{:S(2)}) async-start(), calls=%async_computation.13 | async-start | bytes 1216512 | tf_op jit(solution)/shard_map/all_gather | solution.py:24
  132.2 278.9 %all-gather.23.cloned.1.call-start = ((), (), s32[]{:S(2)}) async-start(), calls=%async_computation.14 | async-start | bytes 4866048 | tf_op jit(solution)/shard_map/all_gather | solution.py:28
  132.9 343.6 %all-gather.25.cloned.1.call-start = ((), (), s32[]{:S(2)}) async-start(), calls=%async_computation.15 | async-start | bytes 4866048 | tf_op jit(solution)/shard_map/all_gather | solution.py:30
  133.7 434.2 %reduce-scatter.25.cloned.1.call-start = ((), (), s32[]{:S(2)}) async-start(), calls=%async_computation.21 | async-start | bytes 3538944
  134.1 105.8 %copy-start.59 = (pred[128,1024]{1,0:T(8,128)(4,1)}, pred[128,1024]{1,0:T(8,128)(4,1)S(1)}, u32[]{:S(2)}) copy-start(pred[128,1024]{1,0:T(8,128)(4,1)S(1)} %broadcast_compare_fusion.1) | copy-start | bytes 393220
  134.2 216.2 %copy-start.57 = (pred[128,1024]{1,0:T(8,128)(4,1)}, pred[128,1024]{1,0:T(8,128)(4,1)S(1)}, u32[]{:S(2)}) copy-start(pred[128,1024]{1,0:T(8,128)(4,1)S(1)} %broadcast_compare_fusion) | copy-start | bytes 393220
  242.5 103.0 %copy-start.28 = (f32[12,64,128]{2,1,0:T(8,128)}, f32[12,64,128]{2,1,0:T(8,128)S(1)}, u32[]{:S(2)}) copy-start(f32[12,64,128]{2,1,0:T(8,128)S(1)} %fusion.94) | copy-start | bytes 1179652
  353.0 66.8 %copy-start.32 = (f32[12,64,128]{2,1,0:T(8,128)}, f32[12,64,128]{2,1,0:T(8,128)S(1)}, u32[]{:S(2)}) copy-start(f32[12,64,128]{2,1,0:T(8,128)S(1)} %fusion.91) | copy-start | bytes 1179652
  524.6 80.9 %reduce-scatter.27.cloned.1.call-start = ((), (), s32[]{:S(2)}) async-start(), calls=%async_computation.22 | async-start | bytes 3538944
  551.1 158.5 %reduce-scatter.29.cloned.1.call-start = ((), (), s32[]{:S(2)}) async-start(), calls=%async_computation.23 | async-start | bytes 2433024
  564.4 249.9 %reduce-scatter.19.cloned.1.call-start = ((), (), s32[]{:S(2)}) async-start(), calls=%async_computation.18 | async-start | bytes 2433024 | tf_op jit(solution)/shard_map/reduce_scatter | solution.py:65
  567.8 350.3 %reduce-scatter.31.cloned.1.call-start = ((), (), s32[]{:S(2)}) async-start(), calls=%async_computation.24 | async-start | bytes 2433024
  612.3 410.4 %reduce-scatter.33.cloned.1.call-start = ((), (), s32[]{:S(2)}) async-start(), calls=%async_computation.25 | async-start | bytes 2433024
  618.8 545.0 %reduce-scatter.21.cloned.1.call-start = ((), (), s32[]{:S(2)}) async-start(), calls=%async_computation.19 | async-start | bytes 9732096 | tf_op jit(solution)/shard_map/reduce_scatter | solution.py:69
  626.7 679.0 %reduce-scatter.23.cloned.1.call-start = ((), (), s32[]{:S(2)}) async-start(), calls=%async_computation.20 | async-start | bytes 9732096 | tf_op jit(solution)/shard_map/reduce_scatter | solution.py:71
  (73 other events, 503.8 us)
Sparse Core Ops, SparseCore 0:
  11.6 57.0 all-gather.10
  72.3 53.2 all-gather.16
  129.2 53.1 all-gather.14
  184.5 23.9 all-gather.12
  210.6 24.5 all-gather.18
  237.2 24.5 all-gather.26
  263.5 24.5 all-gather.28
  291.7 53.7 all-gather.20
  348.5 62.5 all-gather.22
  414.0 62.4 all-gather.24
  524.7 39.1 reduce-scatter.24
  566.0 39.3 reduce-scatter.26
  611.3 98.2 reduce-scatter.28
  716.1 98.0 reduce-scatter.18
  820.0 98.0 reduce-scatter.30
  924.7 98.0 reduce-scatter.32
  1029.1 134.6 reduce-scatter.20
  1171.1 134.5 reduce-scatter.22
where the time goes:
time: 1320 us; the launch traced here: 1310 us
  waiting for transfers between devices  1010 us (77%)
  matrix products  106 us (8%)
  blocking collectives  81.8 us (6%)
  local copies, waits for them, and re-layouts  62.1 us (5%)
  other arithmetic  31.1 us (2%)
  between operations  15.6 us (1%)
    unnamed x23, waiting for transfers between devices  259 us
    reduce_scatter x1, waiting for transfers between devices, sum_owners(): lax.psum_scatter(terms[11], ('dp', 'seq'), scatter_dimension=0, tiled=True)  142 us
    reduce_scatter x1, waiting for transfers between devices, sum_owners(): lax.psum_scatter(terms[9], ('dp', 'seq'), scatter_dimension=0, tiled=True)  141 us
    reduce_scatter x1, waiting for transfers between devices, sum_owners(): lax.psum_scatter(terms[5], ('dp', 'seq'), scatter_dimension=0, tiled=True)  105 us
    unnamed x2, blocking collectives  81.8 us
    all_gather x1, waiting for transfers between devices, fetch_forward(): lax.all_gather(lowered[9], ('dp', 'seq'), axis=0, tiled=True)  57.4 us
    all_gather x1, waiting for transfers between devices, fetch_forward(): lax.all_gather(lowered[11], ('dp', 'seq'), axis=0, tiled=True)  56.7 us
    all_gather x1, waiting for transfers between devices, fetch_forward(): lax.all_gather(lowered[5], ('dp', 'seq'), axis=0, tiled=True)  55.6 us
  transfers between devices with their start and end apart: 18, of which 17 were waited for; matrix products, arithmetic and copies ran while one was open for 10% of the time, Pallas kernels for 0%

commit v1 on v0

--- a/solution.py
+++ b/solution.py
@@ -3,6 +3,8 @@
 import jax
 import jax.numpy as jnp
 from jax import lax
+from jax.experimental import pallas as pl
+from jax.experimental.pallas import tpu as pltpu
 from jax.sharding import PartitionSpec as P
 
 HEADS = 12
@@ -362,6 +364,660 @@
     )
 
 
+BOTH = ("dp", "seq")
+CHIPS = 16
+BAND = 128
+F32 = jnp.float32
+BF16 = jnp.bfloat16
+IN_VMEM = pl.BlockSpec(memory_space=pltpu.VMEM)
+IN_PLACE = pl.BlockSpec(memory_space=pl.ANY)
+
+
+def pairs(dp_bits, seq_bits, keep=lambda dp, seq: True):
+    return [
+        (dp * 8 + seq, (dp ^ dp_bits) * 8 + (seq ^ seq_bits))
+        for dp in range(4)
+        for seq in range(8)
+        if keep(dp, seq)
+    ]
+
+
+CORE, Z1, Z2, Z3 = pairs(0, 1), pairs(0, 2), pairs(0, 4), pairs(0, 6)
+Z3_INNER = pairs(0, 6, lambda dp, seq: seq // 2 in (1, 2))
+X, Y = pairs(1, 0), pairs(2, 0)
+
+
+def send(value, route):
+    return lax.ppermute(value, BOTH, route)
+
+
+def after(value, *events):
+    return lax.optimization_barrier((value, *events))[0]
+
+
+def my_chip():
+    return lax.axis_index("dp") * 4 + lax.axis_index("seq") // 2
+
+
+def my_core():
+    return lax.axis_index("seq") % 2
+
+
+def dot_nn(a, b):
+    return lax.dot_general(a, b, (((1,), (0,)), ((), ())), preferred_element_type=F32)
+
+
+def dot_nt(a, b):
+    return lax.dot_general(a, b, (((1,), (1,)), ((), ())), preferred_element_type=F32)
+
+
+def dot_tn(a, b):
+    return lax.dot_general(a, b, (((0,), (0,)), ((), ())), preferred_element_type=F32)
+
+
+def call(body, outs, n_in, in_specs=None, out_specs=None, scratch=(), grid=None, cost=None):
+    kwargs = {} if grid is None else {"grid": grid}
+    return pl.pallas_call(
+        body,
+        out_shape=[jax.ShapeDtypeStruct(s, d) for s, d in outs],
+        in_specs=in_specs or [IN_VMEM] * n_in,
+        out_specs=out_specs or [IN_VMEM] * len(outs),
+        scratch_shapes=list(scratch),
+        cost_estimate=pl.CostEstimate(flops=cost[0], bytes_accessed=cost[1], transcendentals=0)
+        if cost
+        else None,
+        **kwargs,
+    )
+
+
+def gather_z(block):
+    parts = [block, send(block, Z1), send(block, Z2), send(block, Z3)]
+    half = block.shape[1] // 2
+    return (
+        jnp.concatenate([p[:, :half] for p in parts], axis=0),
+        jnp.concatenate([p[:, half:] for p in parts], axis=0),
+    )
+
+
+def gather_xy(first, second):
+    first_x, second_y = send(first, X), send(second, Y)
+    first_y, second_x = send(first, Y), send(second, X)
+    return (
+        (first, first_x, first_y, send(first_x, Y)),
+        (second, second_x, second_y, send(second_y, X)),
+    )
+
+
+def placed(groups, rows, target, cols, sems, base):
+    me = my_chip()
+    half = groups[0].shape[1]
+    copies = []
+    for g in range(4):
+        for z in range(4):
+            at = pl.multiple_of(((g * 4 + z) ^ me) * rows, 16)
+            copies.append(
+                pltpu.make_async_copy(
+                    groups[g].at[pl.ds(z * rows, rows), :],
+                    target.at[pl.ds(at, rows), pl.ds(cols, half)],
+                    sems.at[base + g * 4 + z],
+                )
+            )
+    return copies
+
+
+def project_kernel(*refs):
+    xs, first, second = refs[0:8], refs[8:12], refs[12:16]
+    bq_ref, bv_ref = refs[16:18]
+    q_ref, k_ref, v_ref, w_ref, x_ref, sems = refs[18:]
+    loads = [pltpu.make_async_copy(xs[s], x_ref.at[s], sems.at[32 + s]) for s in range(8)]
+    loads += placed(first, 48, w_ref, 0, sems, 0) + placed(second, 48, w_ref, 768, sems, 16)
+    for c in loads:
+        c.start()
+    for c in loads:
+        c.wait()
+    bq, bv = bq_ref[...], bv_ref[...]
+
+    def queries(s, _):
+        x = x_ref[s].reshape(2 * BAND, 768)
+        q = (dot_nn(x, w_ref[:, 0:384]) + bq).astype(BF16) * jnp.asarray(0.125, BF16)
+        q_ref[s] = q.reshape(2, BAND, 384)
+        return 0
+
+    lax.fori_loop(0, 2, queries, 0)
+
+    def slot(s, _):
+        x = x_ref[s].reshape(2 * BAND, 768)
+        k_ref[s] = dot_nn(x, w_ref[:, 384:768]).astype(BF16).reshape(2, BAND, 384)
+        v_ref[s] = (dot_nn(x, w_ref[:, 768:1152]) + bv).astype(BF16).reshape(2, BAND, 384)
+        return 0
+
+    lax.fori_loop(0, 8, slot, 0)
+
+
+def attend_kernel(q_ref, k_ref, v_ref, kseg_ref, qseg_ref, mix_ref, low_ref, lse_ref):
+    mask = jnp.where(kseg_ref[0] == qseg_ref[0], 0.0, -1e30)
+    q = q_ref[:, 0].reshape(2 * BAND, 384)
+    for h in range(6):
+        cols = slice(64 * h, 64 * h + 64)
+        k = k_ref[:, 0, :, cols].reshape(8 * BAND, 64)
+        v = v_ref[:, 0, :, cols].reshape(8 * BAND, 64)
+        s = dot_nt(k, q[:, cols]) + mask
+        top = jnp.max(s, axis=0, keepdims=True)
+        e = jnp.exp(s - top)
+        total = jnp.sum(e, axis=0, keepdims=True)
+        mixed = dot_tn(v, e.astype(BF16)) * (1.0 / total)
+        mix_ref[0, cols] = mixed
+        low_ref[0, cols] = mixed.astype(BF16)
+        lse_ref[0, h : h + 1] = top + jnp.log(total)
+
+
+def norm(z):
+    mean = jnp.mean(z, axis=-1, keepdims=True)
+    centered = z - mean
+    rstd = lax.rsqrt(jnp.mean(centered * centered, axis=-1, keepdims=True) + 1e-05)
+    return (centered * rstd, rstd)
+
+
+def norm_grad(grad, normed, rstd, gain):
+    scaled = grad * gain
+    return rstd * (
+        scaled
+        - jnp.mean(scaled, axis=-1, keepdims=True)
+        - normed * jnp.mean(scaled * normed, axis=-1, keepdims=True)
+    )
+
+
+def forward_kernel(*refs):
+    x_ref, own_ref, other_ref, vec_ref, b1_ref = refs[0:5]
+    wa, wb, va, vb = refs[5:9], refs[9:13], refs[13:17], refs[17:21]
+    n1_ref, r1_ref, low_ref, act_ref, slope_ref, f_ref, w1_ref, w2_ref, tok_ref, sems = refs[21:]
+    loads1 = placed(wa, 48, w1_ref, 0, sems, 0) + placed(wb, 48, w1_ref, 768, sems, 16)
+    loads2 = placed(va, 96, w2_ref, 0, sems, 32) + placed(vb, 96, w2_ref, 384, sems, 48)
+    tokens = pltpu.make_async_copy(x_ref.at[pl.ds(0, 2)], tok_ref, sems.at[64])
+    for c in [tokens] + loads1 + loads2:
+        c.start()
+    tokens.wait()
+    bo, g1, s1 = vec_ref[2:3], vec_ref[3:4], vec_ref[4:5]
+
+    def rows(i, _):
+        r = pl.ds(i * 128, 128)
+        o = pl.ds((i ^ 2) * 128, 128)
+        z = tok_ref[i // 2, i % 2].astype(F32) + (own_ref[r].astype(F32) + other_ref[o].astype(F32)) + bo
+        n, rstd = norm(z)
+        n1_ref[r] = n
+        r1_ref[r] = rstd
+        low_ref[r] = (n * g1 + s1).astype(BF16)
+        return 0
+
+    lax.fori_loop(0, 4, rows, 0)
+    for c in loads1:
+        c.wait()
+
+    def inner(j, _):
+        cols = pl.ds(pl.multiple_of(j * 256, 256), 256)
+        u = dot_nn(low_ref[...], w1_ref[:, cols]) + b1_ref[:, cols]
+        cdf = 0.5 * (1.0 + lax.erf(u * (1.0 / math.sqrt(2.0))))
+        act_ref[:, cols] = (u * cdf).astype(BF16)
+        slope = cdf + u * (jnp.exp(-0.5 * u * u) * (1.0 / math.sqrt(2.0 * math.pi)))
+        slope_ref[:, cols] = slope.astype(BF16)
+        return 0
+
+    lax.fori_loop(0, 6, inner, 0)
+    for c in loads2:
+        c.wait()
+
+    def outer(j, _):
+        cols = pl.ds(pl.multiple_of(j * 256, 256), 256)
+        f_ref[:, cols] = dot_nn(act_ref[...], w2_ref[:, cols]).astype(BF16)
+        return 0
+
+    lax.fori_loop(0, 3, outer, 0)
+
+
+def middle_kernel(
+    n1_ref, own_ref, other_ref, cot_ref, pcot_ref, vec_ref, slope_ref, w1_ref, w2_ref,
+    out_ref, df_ref, dz_ref, du_ref, dh_ref, sums_ref, db1_ref,
+):
+    g1, s1, b2, g2, s2 = (vec_ref[i : i + 1] for i in (3, 4, 5, 6, 7))
+
+    def rows(i, which):
+        ref, base = which
+        r, o = pl.ds(base + i * 128, 128), pl.ds(256 - base + i * 128, 128)
+        z = n1_ref[r] * g1 + s1 + (own_ref[r].astype(F32) + other_ref[o].astype(F32)) + b2
+        n, rstd = norm(z)
+        grad = ref[pl.ds(i * 128, 128)].astype(F32)
+        dz = norm_grad(grad, n, rstd, g2)
+        dz_ref[r] = dz
+        df_ref[r] = dz.astype(BF16)
+        return (r, n, grad, dz)
+
+    sums_ref[...] = jnp.zeros_like(sums_ref)
+
+    def own_rows(i, _):
+        r, n, grad, dz = rows(i, (cot_ref, 0))
+        out_ref[r] = (n * g2 + s2).astype(BF16)
+        sums_ref[0:1] += jnp.sum(grad * n, axis=0, keepdims=True)
+        sums_ref[1:2] += jnp.sum(grad, axis=0, keepdims=True)
+        sums_ref[2:3] += jnp.sum(dz.astype(BF16).astype(F32), axis=0, keepdims=True)
+        return 0
+
+    def other_rows(i, _):
+        rows(i, (pcot_ref, 256))
+        return 0
+
+    lax.fori_loop(0, 2, own_rows, 0)
+    lax.fori_loop(0, 2, other_rows, 0)
+
+    def hidden(j, _):
+        cols = pl.ds(pl.multiple_of(j * 256, 256), 256)
+        du = (dot_nt(df_ref[...], w2_ref[cols, :]) * slope_ref[:, cols].astype(F32)).astype(BF16)
+        du_ref[:, cols] = du
+        db1_ref[:, cols] = jnp.sum(du.astype(F32), axis=0, keepdims=True)
+        return 0
+
+    lax.fori_loop(0, 6, hidden, 0)
+
+    def back(j, _):
+        cols = pl.ds(pl.multiple_of(j * 256, 256), 256)
+        dh_ref[:, cols] = dot_nt(du_ref[...], w1_ref[cols, :]).astype(BF16)
+        return 0
+
+    lax.fori_loop(0, 3, back, 0)
+
+
+def first_kernel(dz_ref, own_ref, other_ref, n1_ref, r1_ref, vec_ref, wo_ref, dz1_ref, do_ref, half_ref, da_ref, sums_ref):
+    g1 = vec_ref[3:4]
+    core = my_core()
+    sums_ref[...] = jnp.zeros_like(sums_ref)
+
+    def rows(i):
+        r, o = pl.ds(i * 128, 128), pl.ds((i ^ 2) * 128, 128)
+        grad = dz_ref[r] + (own_ref[r].astype(F32) + other_ref[o].astype(F32))
+        n = n1_ref[r]
+        dz = norm_grad(grad, n, r1_ref[r], g1)
+        low = dz.astype(BF16)
+        do_ref[r] = low
+        half_ref[r] = jnp.where(core == 0, low[:, :384], low[:, 384:])
+        return (r, n, grad, dz, low)
+
+    def own_rows(i, _):
+        r, n, grad, dz, low = rows(i)
+        dz1_ref[r] = dz
+        sums_ref[0:1] += jnp.sum(grad * n, axis=0, keepdims=True)
+        sums_ref[1:2] += jnp.sum(grad, axis=0, keepdims=True)
+        sums_ref[2:3] += jnp.sum(low.astype(F32), axis=0, keepdims=True)
+        return 0
+
+    def other_rows(i, _):
+        rows(i)
+        return 0
+
+    lax.fori_loop(0, 2, own_rows, 0)
+    lax.fori_loop(2, 4, other_rows, 0)
+    for m in range(2):
+        for c in range(2):
+            part = do_ref[pl.ds((c * 2 + m) * BAND, BAND), :]
+            da_ref[m, :, c * BAND : (c + 1) * BAND] = dot_nt(wo_ref[...], part).astype(BF16)
+
+
+def attend_back_kernel(q_ref, k_ref, v_ref, mix_ref, da_ref, lse_ref, kseg_ref, qseg_ref, dq_ref, dk_ref, dv_ref):
+    mask = jnp.where(kseg_ref[0] == qseg_ref[0], 0.0, -1e30)
+    q = q_ref[:, 0].reshape(2 * BAND, 384)
+    for pair in range(3):
+        dks, dvs, dqs = [], [], []
+        for h in (2 * pair, 2 * pair + 1):
+            cols = slice(64 * h, 64 * h + 64)
+            k = k_ref[:, 0, :, cols].reshape(8 * BAND, 64)
+            v = v_ref[:, 0, :, cols].reshape(8 * BAND, 64)
+            qh, da = q[:, cols], da_ref[0, cols]
+            p = jnp.exp(dot_nt(k, qh) + mask - lse_ref[0, h : h + 1])
+            delta = jnp.sum(da.astype(F32) * mix_ref[0, cols], axis=0, keepdims=True)
+            ds = (p * (dot_nn(v, da) - delta)).astype(BF16)
+            dvs.append(dot_nt(p.astype(BF16), da))
+            dks.append(dot_nn(ds, qh))
+            dqs.append(dot_tn(k, ds))
+        both = slice(128 * pair, 128 * pair + 128)
+        dk_ref[:, 0, :, both] = jnp.concatenate(dks, axis=1).astype(BF16).reshape(8, BAND, 128)
+        dv_ref[:, 0, :, both] = jnp.concatenate(dvs, axis=1).astype(BF16).reshape(8, BAND, 128)
+        dq = jnp.transpose(jnp.concatenate(dqs, axis=0) * 0.125)
+        dq_ref[:, 0, :, both] = dq.astype(BF16).reshape(2, BAND, 128)
+
+
+def token_grad_kernel(dq_ref, dk_ref, dv_ref, w_ref, own_ref, send_ref):
+    z = pl.program_id(0)
+    for c, ref in enumerate((own_ref, send_ref)):
+        dk = dk_ref[c].reshape(2 * BAND, 384)
+        dv = dv_ref[c].reshape(2 * BAND, 384)
+        ref[0] = (dot_nt(dk, w_ref[:, 384:768]) + dot_nt(dv, w_ref[:, 768:1152])).astype(BF16).reshape(2, BAND, 768)
+
+        @pl.when(z == 0)
+        def _():
+            dq = dq_ref[c].reshape(2 * BAND, 384)
+            dx = dot_nt(dk, w_ref[:, 384:768]) + dot_nt(dv, w_ref[:, 768:1152]) + dot_nt(dq, w_ref[:, 0:384])
+            ref[0] = dx.astype(BF16).reshape(2, BAND, 768)
+
+
+def place_rows(scratch, value, first_block, rows, cols):
+    me = my_chip()
+    for i in range(value.shape[0] // rows):
+        at = pl.multiple_of(((first_block + i) ^ me) * rows, 16)
+        scratch[pl.ds(at, rows), cols] = value[i * rows : (i + 1) * rows].astype(BF16)
+
+
+def flush(scratch, outs, sems):
+    rows, half = outs[0].shape
+    copies = []
+    for i, out in enumerate(outs):
+        src = scratch.at[pl.ds((i % 4) * rows, rows), pl.ds((i // 4) * half, half)]
+        copies.append(pltpu.make_async_copy(src, out, sems.at[i]))
+    for c in copies:
+        c.start()
+    for c in copies:
+        c.wait()
+
+
+def outer_grad_kernel(act_ref, df_ref, *refs):
+    outs, scratch, sems = refs[:8], refs[8], refs[9]
+
+    def step(j, _):
+        cols = pl.ds(pl.multiple_of(j * 384, 384), 384)
+        place_rows(scratch, dot_tn(act_ref[:, cols], df_ref[...]), j * 4, 96, slice(0, 768))
+        return 0
+
+    lax.fori_loop(0, 4, step, 0)
+    flush(scratch, outs, sems)
+
+
+def inner_grad_kernel(low_ref, du_ref, *refs):
+    outs, scratch, sems = refs[:8], refs[8], refs[9]
+
+    def step(j, _):
+        cols = pl.ds(pl.multiple_of(j * 384, 384), 384)
+        place_rows(scratch, dot_tn(low_ref[:, cols], du_ref[...]), j * 8, 48, slice(0, 1536))
+        return 0
+
+    lax.fori_loop(0, 2, step, 0)
+    flush(scratch, outs, sems)
+
+
+def projection_grad_kernel(x_ref, dq_ref, dk_ref, dv_ref, mix0_ref, mix1_ref, half_ref, *refs):
+    outs, sums_ref, scratch, sems = refs[:8], refs[8], refs[9], refs[10]
+    dq = dq_ref[...].reshape(4 * BAND, 384)
+    sums_ref[0:1] = jnp.sum(dq.astype(F32), axis=0, keepdims=True)
+
+    def count(s, acc):
+        return acc + jnp.sum(dv_ref[s].reshape(2 * BAND, 384).astype(F32), axis=0, keepdims=True)
+
+    sums_ref[1:2] = lax.fori_loop(0, 8, count, jnp.zeros((1, 384), F32))
+    half = half_ref[...].reshape(2, 2, BAND, 384)
+
+    def step(j, _):
+        cols = pl.ds(pl.multiple_of(j * 384, 384), 384)
+        x = x_ref[:, :, :, cols].reshape(16 * BAND, 384)
+        place_rows(scratch, dot_tn(x[: 4 * BAND], dq), j * 8, 48, slice(0, 384))
+        place_rows(scratch, dot_tn(x, dk_ref[...].reshape(16 * BAND, 384)), j * 8, 48, slice(384, 768))
+        place_rows(scratch, dot_tn(x, dv_ref[...].reshape(16 * BAND, 384)), j * 8, 48, slice(768, 1152))
+        rows = pl.ds(pl.multiple_of(j * 384, 384), 384)
+        dwo = dot_nn(mix0_ref[rows], half[:, 0].reshape(2 * BAND, 384))
+        dwo += dot_nn(mix1_ref[rows], half[:, 1].reshape(2 * BAND, 384))
+        place_rows(scratch, dwo, j * 8, 48, slice(1152, 1536))
+        return 0
+
+    lax.fori_loop(0, 2, step, 0)
+    flush(scratch, outs, sems)
+
+
+def add(*terms):
+    total = terms[0].astype(F32)
+    for t in terms[1:]:
+        total = total + t.astype(F32)
+    return total
+
+
+def scatter_groups(groups, first_route, second_route, near, far, both):
+    from_both = send(groups[both], first_route)
+    from_far = send(groups[far], first_route)
+    passed = add(groups[near], from_both).astype(BF16)
+    return add(groups[0], from_far, send(passed, second_route)).astype(BF16)
+
+
+def scatter_z(block):
+    rows = block.shape[0] // 4
+    part = [block[i * rows : (i + 1) * rows] for i in range(4)]
+    return add(part[0], send(part[1], Z1), send(part[2], Z2), send(part[3], Z3))
+
+
+def scatter_sum(outs):
+    first = scatter_groups(outs[:4], Y, X, 1, 2, 3)
+    second = scatter_groups(outs[4:], X, Y, 2, 1, 3)
+    return (scatter_z(first), scatter_z(second))
+
+
+def flip(values, axis, index, bits):
+    for bit in range(bits):
+        shape = values.shape
+        n = shape[axis]
+        split = shape[:axis] + (n >> (bit + 1), 2, 1 << bit) + shape[axis + 1 :]
+        swapped = jnp.flip(values.reshape(split), axis + 1).reshape(shape)
+        values = jnp.where((index >> bit) & 1 == 1, swapped, values)
+    return values
+
+
+def per_device_paired(
+    inputs, segments, w_query, b_query, w_key, w_value, b_value, w_output, b_output, gain_first,
+    shift_first, w_inner, b_inner, w_outer, b_outer, gain_second, shift_second, cotangent,
+):
+    seq = lax.axis_index("seq")
+    me, core = my_chip(), my_core()
+    even = core == 0
+
+    four = jnp.stack([w_query, w_key, w_value, w_output], axis=1).astype(BF16).reshape(24, 4, 2, 384)
+    mine, theirs = (
+        jnp.where(even, four[:, :, 0], four[:, :, 1]).reshape(24, 1536),
+        jnp.where(even, four[:, :, 1], four[:, :, 0]).reshape(24, 1536),
+    )
+    got = send(theirs, CORE)
+    square = jnp.where(even, jnp.concatenate([mine, got], 0), jnp.concatenate([got, mine], 0))
+    wide = w_inner.astype(BF16).reshape(24, CHIPS, 2, 96)
+    mine, theirs = (
+        jnp.where(even, wide[:, :, 0], wide[:, :, 1]).reshape(24, 1536),
+        jnp.where(even, wide[:, :, 1], wide[:, :, 0]).reshape(24, 1536),
+    )
+    got = send(theirs, CORE)
+    inner_rows = jnp.where(even, jnp.concatenate([mine, got], 0), jnp.concatenate([got, mine], 0))
+    outer_rows = w_outer.astype(BF16)
+
+    own_vec = jnp.concatenate(
+        [b_query, b_value, b_output, gain_first, shift_first, b_outer, gain_second, shift_second, b_inner]
+    ).astype(BF16)
+    spot = (jnp.arange(CHIPS)[:, None, None] == me) & (jnp.arange(2)[None, :, None] == core)
+    vecs = jnp.where(spot, own_vec[None, None, :], jnp.zeros((), BF16))
+    for route in (CORE, Z1, Z2, X, Y):
+        vecs = vecs + send(vecs, route)
+    vecs = vecs.astype(F32)
+    vec8 = vecs[:, :, :192].reshape(CHIPS, 2, 8, 24).transpose(2, 0, 1, 3).reshape(8, 768)
+    b1 = jnp.where(even, vecs[:, 0, 192:], vecs[:, 1, 192:]).reshape(1, 1536)
+    bq = jnp.where(even, vec8[0:1, :384], vec8[0:1, 384:])
+    bv = jnp.where(even, vec8[1:2, :384], vec8[1:2, 384:])
+
+    tokens, cot = inputs[:, 0], cotangent[:, 0]
+    square_a, square_d = gather_z(square)
+    tokens_z = after(tokens, square_a)
+    near = [tokens, send(tokens_z, Z1), send(tokens_z, Z2), send(tokens_z, Z3_INNER)]
+    slots = []
+    for part in near:
+        slots += [part, send(part, CORE)]
+    other_cot = send(cot, CORE)
+    square_a, square_d = gather_xy(square_a, square_d)
+    inner_a, inner_d = gather_z(after(inner_rows, near[1], near[2], near[3]))
+    inner_a, inner_d = gather_xy(after(inner_a, *square_a), after(inner_d, *square_d))
+    outer_a, outer_d = gather_z(after(outer_rows, near[1], near[2], near[3]))
+    outer_a, outer_d = gather_xy(after(outer_a, *inner_a), after(outer_d, *inner_d))
+
+    segs = segments[:, 0]
+    segs = flip(segs.reshape(2, 8, BAND), 1, seq, 3)
+    kseg = segs.reshape(2, 8 * BAND, 1)
+    qseg = segs[:, :2].reshape(2, 1, 2 * BAND)
+
+    slot_shape, head_shape = (2, BAND, 768), (2, BAND, 384)
+    q, k, v, w_abs, x_all = call(
+        project_kernel,
+        [((2, *head_shape), BF16), ((8, *head_shape), BF16), ((8, *head_shape), BF16), ((768, 1536), BF16), ((8, *slot_shape), BF16)],
+        18,
+        in_specs=[IN_PLACE] * 16 + [IN_VMEM] * 2,
+        scratch=[pltpu.SemaphoreType.DMA((40,))],
+        cost=(2_800_000_000, 16_000_000),
+    )(*slots, *square_a, *square_d, bq, bv)
+
+    wo_half = w_abs[:, 1152:]
+    wo_mine = jnp.where(even, wo_half[:384], wo_half[384:])
+    wo_got = send(jnp.where(even, wo_half[384:], wo_half[:384]), CORE)
+    wo = jnp.where(even, jnp.concatenate([wo_mine, wo_got], 1), jnp.concatenate([wo_got, wo_mine], 1))
+
+    q_spec = pl.BlockSpec((2, 1, BAND, 384), lambda m: (0, m, 0, 0))
+    k_spec = pl.BlockSpec((8, 1, BAND, 384), lambda m: (0, m, 0, 0))
+    seg_specs = [
+        pl.BlockSpec((1, 8 * BAND, 1), lambda m: (m, 0, 0)),
+        pl.BlockSpec((1, 1, 2 * BAND), lambda m: (m, 0, 0)),
+    ]
+    t_spec = pl.BlockSpec((1, 384, 2 * BAND), lambda m: (m, 0, 0))
+    lse_spec = pl.BlockSpec((1, 8, 2 * BAND), lambda m: (m, 0, 0))
+    mix, mix_low, lse = call(
+        attend_kernel,
+        [((2, 384, 256), F32), ((2, 384, 256), BF16), ((2, 8, 256), F32)],
+        5,
+        grid=(2,),
+        in_specs=[q_spec, k_spec, k_spec, *seg_specs],
+        out_specs=[t_spec, t_spec, lse_spec],
+        cost=(1_600_000_000, 8_000_000),
+    )(q, k, v, kseg, qseg)
+    mix_other = send(mix_low, CORE)
+
+    branch = [dot_tn(mix_low[m], wo).astype(BF16).reshape(2, 1, BAND, 768) for m in range(2)]
+    branch = jnp.concatenate(branch, axis=1).reshape(2, 2 * BAND, 768)
+    branch = branch.reshape(4 * BAND, 768)
+    branch_other = send(branch, CORE)
+    n1, r1, hid_low, act, slope, f_own, w1, w2 = call(
+        forward_kernel,
+        [((512, 768), F32), ((512, 1), F32), ((512, 768), BF16), ((512, 1536), BF16), ((512, 1536), BF16), ((512, 768), BF16), ((768, 1536), BF16), ((1536, 768), BF16)],
+        21,
+        in_specs=[IN_PLACE] + [IN_VMEM] * 4 + [IN_PLACE] * 16,
+        scratch=[pltpu.VMEM((2, *slot_shape), BF16), pltpu.SemaphoreType.DMA((65,))],
+        cost=(2_500_000_000, 16_000_000),
+    )(x_all, branch, branch_other, vec8, b1, *inner_a, *inner_d, *outer_a, *outer_d)
+
+    result, df, dz2, du, dh_own, sums2, db1 = call(
+        middle_kernel,
+        [((256, 768), BF16), ((512, 768), BF16), ((512, 768), F32), ((512, 1536), BF16), ((512, 768), BF16), ((8, 768), F32), ((1, 1536), F32)],
+        9,
+        cost=(2_500_000_000, 16_000_000),
+    )(n1, f_own, send(f_own, CORE), cot.reshape(256, 768), other_cot.reshape(256, 768), vec8, slope, w1, w2)
+    dh_other = send(dh_own, CORE)
+
+    piece = [pltpu.SemaphoreType.DMA((8,))]
+    outer_terms = call(
+        outer_grad_kernel,
+        [((384, 384), BF16)] * 8,
+        2,
+        out_specs=[IN_PLACE] * 8,
+        scratch=[pltpu.VMEM((1536, 768), BF16)] + piece,
+        cost=(1_200_000_000, 6_000_000),
+    )(act, df)
+    outer_sum_a, outer_sum_d = scatter_sum(outer_terms)
+    inner_terms = call(
+        inner_grad_kernel,
+        [((192, 768), BF16)] * 8,
+        2,
+        out_specs=[IN_PLACE] * 8,
+        scratch=[pltpu.VMEM((768, 1536), BF16)] + piece,
+        cost=(1_200_000_000, 6_000_000),
+    )(hid_low, du)
+    inner_sum_a, inner_sum_d = scatter_sum(inner_terms)
+
+    dz1, do, do_half, da, sums1 = call(
+        first_kernel,
+        [((256, 768), F32), ((512, 768), BF16), ((512, 384), BF16), ((2, 384, 256), BF16), ((8, 768), F32)],
+        7,
+        cost=(300_000_000, 10_000_000),
+    )(dz2, dh_own, dh_other, n1, r1, vec8, wo)
+
+    dq, dk, dv = call(
+        attend_back_kernel,
+        [((2, *head_shape), BF16), ((8, *head_shape), BF16), ((8, *head_shape), BF16)],
+        8,
+        grid=(2,),
+        in_specs=[q_spec, k_spec, k_spec, t_spec, t_spec, lse_spec, *seg_specs],
+        out_specs=[q_spec, k_spec, k_spec],
+        cost=(4_000_000_000, 12_000_000),
+    )(q, k, v, mix, da, lse, kseg, qseg)
+
+    by_z = pl.BlockSpec((1, *slot_shape), lambda z: (z, 0, 0, 0))
+    heads_by_z = pl.BlockSpec((2, *head_shape), lambda z: (z, 0, 0, 0))
+    dx_own, dx_send = call(
+        token_grad_kernel,
+        [((4, *slot_shape), BF16)] * 2,
+        4,
+        grid=(4,),
+        in_specs=[pl.BlockSpec((2, *head_shape), lambda z: (0, 0, 0, 0)), heads_by_z, heads_by_z, pl.BlockSpec((768, 1536), lambda z: (0, 0))],
+        out_specs=[by_z, by_z],
+        cost=(2_700_000_000, 10_000_000),
+    )(dq, dk, dv, w_abs)
+    dx_got = send(dx_send, CORE)
+    dx = [add(dx_own[z], dx_got[z]) for z in range(4)]
+    low_dx = [d.astype(BF16) for d in dx]
+    grad_tokens = add(
+        dx[0], dz1.reshape(slot_shape), send(low_dx[1], Z1), send(low_dx[2], Z2), send(low_dx[3], Z3_INNER)
+    ).astype(BF16)
+
+    mix_full = [
+        jnp.where(even, jnp.concatenate([mix_low[m], jnp.roll(mix_other[m], BAND, 1)], 0), jnp.concatenate([jnp.roll(mix_other[m], BAND, 1), mix_low[m]], 0))
+        for m in range(2)
+    ]
+    *square_terms, sums0 = call(
+        projection_grad_kernel,
+        [((192, 768), BF16)] * 8 + [((8, 384), F32)],
+        7,
+        out_specs=[IN_PLACE] * 8 + [IN_VMEM],
+        scratch=[pltpu.VMEM((768, 1536), BF16)] + piece,
+        cost=(3_300_000_000, 12_000_000),
+    )(x_all, dq, dk, dv, mix_full[0], mix_full[1], do_half)
+    square_sum_a, square_sum_d = scatter_sum(square_terms)
+
+    zero = jnp.zeros((1, 384), F32)
+    bq_g, bv_g = (
+        jnp.where(even, jnp.concatenate([sums0[i : i + 1], zero], 1), jnp.concatenate([zero, sums0[i : i + 1]], 1))
+        for i in (0, 1)
+    )
+    eight = jnp.concatenate(
+        [bq_g, bv_g, sums1[2:3], sums1[0:1], sums1[1:2], sums2[2:3], sums2[0:1], sums2[1:2]], 0
+    )
+    eight = eight.reshape(8, CHIPS, 2, 24).transpose(1, 2, 0, 3).reshape(CHIPS, 2, 192)
+    db1 = db1.reshape(CHIPS, 1, 96)
+    db1 = jnp.where(jnp.arange(2)[None, :, None] == core, db1, 0.0)
+    vec_grads = jnp.concatenate([eight, db1], axis=2)
+    for route in (CORE, Z1, Z2, X, Y):
+        vec_grads = vec_grads + send(vec_grads, route)
+    own = jnp.sum(jnp.where(spot, vec_grads, 0.0), axis=(0, 1))
+
+    def to_owner(first, second):
+        value = jnp.concatenate([first, second], axis=1)
+        keep = jnp.where(even, value[:24], value[24:])
+        other = jnp.where(even, value[24:], value[:24]).astype(BF16)
+        return (keep, send(other, CORE).astype(F32))
+
+    keep, got = (v.reshape(24, 4, 384) for v in to_owner(square_sum_a, square_sum_d))
+    squares = jnp.where(even, jnp.concatenate([keep, got], 2), jnp.concatenate([got, keep], 2))
+    keep, got = (v.reshape(24, CHIPS, 1, 96) for v in to_owner(inner_sum_a, inner_sum_d))
+    grad_inner = jnp.where(even, jnp.concatenate([keep, got], 2), jnp.concatenate([got, keep], 2)).reshape(24, 3072)
+    grad_outer = jnp.concatenate([outer_sum_a, outer_sum_d], axis=1)
+    small = [own[24 * i : 24 * i + 24] for i in range(8)]
+    return (
+        result.reshape(2, 1, BAND, 768), grad_tokens[:, None],
+        squares[:, 0], small[0], squares[:, 1], squares[:, 2], small[1], squares[:, 3], small[2],
+        small[3], small[4], grad_inner, own[192:], grad_outer, small[5], small[6], small[7],
+    )
+
+
 def solution(mesh):
     in_specs = (
         P(None, "dp", "seq", None),
@@ -402,6 +1058,7 @@
         P(("dp", "seq")),
         P(("dp", "seq")),
     )
+    paired = (mesh.shape["dp"], mesh.shape["seq"]) == (4, 8)
     return jax.shard_map(
-        per_device, mesh=mesh, in_specs=in_specs, out_specs=out_specs, check_vma=False
-    )
+        per_device_paired if paired else per_device, mesh=mesh, in_specs=in_specs, out_specs=out_specs, check_vma=False
+    )

time: 1320 us -> 398 us (0.30)
  waiting for transfers between devices: 1010 us -> 153 us
  matrix products: 106 us -> 1.92 us
  starting transfers between devices: 1.33 us -> 104 us
  Pallas kernels: 0 us -> 93.5 us
  blocking collectives: 81.8 us -> 0 us
  local copies, waits for them, and re-layouts: 62.1 us -> 18.9 us
  other arithmetic: 31.1 us -> 17.1 us
  between operations: 15.6 us -> 2.39 us
    reduce_scatter x3 -> x0, waiting for transfers between devices: 388 us -> none  [the longest x1 142 us: sum_owners(): lax.psum_scatter(terms[11], ('dp', 'seq'), scatter_dimension=0, tiled=True)]
    all_gather x10 -> x0, waiting for transfers between devices: 368 us -> none  [the longest x1 57.4 us: fetch_forward(): lax.all_gather(lowered[9], ('dp', 'seq'), axis=0, tiled=True)]
    unnamed x23 -> x0, waiting for transfers between devices: 259 us -> none
    ppermute x0 -> x94, waiting for transfers between devices: none -> 153 us  [send(): return lax.ppermute(value, BOTH, route)]
    ppermute x0 -> x94, starting transfers between devices: none -> 104 us  [send(): return lax.ppermute(value, BOTH, route)]
    dot_general x48 -> x2, matrix products: 106 us -> 1.92 us  [dot_tn(): lax.dot_general(a, b, (((0,), (0,)), ((), ())), preferred_element_type=F32)]
    pallas_call x0 -> x10, Pallas kernels: none -> 93.5 us  [the longest x1 12.6 us: per_device_paired(): call(forward_kernel, [((512, 768), F32), ((512, 1), F32), ((512, 768), BF...]
    unnamed x2 -> x0, blocking collectives: 81.8 us -> none
  transfers between devices with their start and end apart: 18 -> 94, of which waited for: 17 -> 41; matrix products, arithmetic and copies ran while one was open for 10% -> 7% of each run, Pallas kernels for 0% -> 20%
where the time goes in v1:
time: 398 us; the launch traced here: 391 us
  waiting for transfers between devices  153 us (38%)
  starting transfers between devices  104 us (26%)
  Pallas kernels  93.5 us (23%)
  local copies, waits for them, and re-layouts  18.9 us (5%)
  other arithmetic  17.1 us (4%)
    ppermute x94, waiting for transfers between devices, send(): return lax.ppermute(value, BOTH, route)  153 us
    ppermute x94, starting transfers between devices, send(): return lax.ppermute(value, BOTH, route)  104 us
    pallas_call x1, Pallas kernels, per_device_paired(): call(forward_kernel, [((512, 768), F32), ((512, 1), F32), ((512, 768), BF...  12.6 us
    pallas_call x1, Pallas kernels, per_device_paired(): call(project_kernel, [((2, *head_shape), BF16), ((8, *head_shape), BF16),...  11.8 us
    pallas_call x1, Pallas kernels, per_device_paired(): call(middle_kernel, [((256, 768), BF16), ((512, 768), BF16), ((512, 768),...  11.7 us
    pallas_call x1, Pallas kernels, per_device_paired(): call(attend_back_kernel, [((2, *head_shape), BF16), ((8, *head_shape), BF...  11.3 us
    pallas_call x1, Pallas kernels, per_device_paired(): call(attend_kernel, [((2, 384, 256), F32), ((2, 384, 256), BF16), ((2, 8,...  10.9 us
    pallas_call x1, Pallas kernels, per_device_paired(): call(projection_grad_kernel, [((192, 768), BF16)] * 8 + [((8, 384), F32)]...  10.2 us
  transfers between devices with their start and end apart: 94, of which 41 were waited for; matrix products, arithmetic and copies ran while one was open for 7% of the time, Pallas kernels for 20%

profile of v1, /device:TPU:0, one launch (start us, length us, event | category | flops | bytes accessed | tf_op | source)
XLA Modules:
  0.0 391.2 jit_solution(9170214755118129786)
XLA Ops:
  30.3 6.4 %collective-permute-done.3 = bf16[48,1536]{1,0:T(8,128)(2,1)S(1)} collective-permute-done((bf16[48,1536]{1,0:T(8,128)(2,1)S(1)}, bf16[48,1536]{1,0:T(8,128)(2,1)S(1)}, u32[]{:S(2)}, u32[]{:S(2)}) %collective-permute-start.3) | collective-permute-done | bytes 147488 | tf_op jit(solution)/shard_map/ppermute | solution.py:391
  54.4 6.0 %collective-permute-done.7.refs_4_ = bf16[2,128,768]{2,1,0:T(8,128)(2,1)S(1)} collective-permute-done((bf16[2,128,768]{2,1,0:T(8,128)(2,1)S(1)}, bf16[2,128,768]{2,1,0:T(8,128)(2,1)S(1)}, u32[]{:S(2)}, u32[]{:S(2)}) %collective-permute-start.7) | collective-permute-done | bytes 393248 | tf_op jit(solution)/shard_map/ppermute | solution.py:391
  61.7 5.1 %collective-permute-start.34 = (bf16[96,768]{1,0:T(8,128)(2,1)S(1)}, bf16[96,768]{1,0:T(8,128)(2,1)S(1)}, u32[]{:S(2)}, u32[]{:S(2)}) collective-permute-start(bf16[96,768]{1,0:T(8,128)(2,1)S(1)} %convert_element_type.294), channel_id=1, source_target_pairs={{0,2},{1,3},{2,0},{3,1},{4,6},{5,7},{6,4},{7,5},{8,10},{9,11},{10,... | collective-permute-start | bytes 442376 | tf_op jit(solution)/shard_map/ppermute | solution.py:391
  79.9 7.8 %collective-permute-done.26 = bf16[48,1536]{1,0:T(8,128)(2,1)S(1)} collective-permute-done((bf16[48,1536]{1,0:T(8,128)(2,1)S(1)}, bf16[48,1536]{1,0:T(8,128)(2,1)S(1)}, u32[]{:S(2)}, u32[]{:S(2)}) %collective-permute-start.26) | collective-permute-done | bytes 147488 | tf_op jit(solution)/shard_map/ppermute | solution.py:391
  89.9 4.7 %collective-permute-done.27 = bf16[48,1536]{1,0:T(8,128)(2,1)S(1)} collective-permute-done((bf16[48,1536]{1,0:T(8,128)(2,1)S(1)}, bf16[48,1536]{1,0:T(8,128)(2,1)S(1)}, u32[]{:S(2)}, u32[]{:S(2)}) %collective-permute-start.27) | collective-permute-done | bytes 147488 | tf_op jit(solution)/shard_map/ppermute | solution.py:391
  96.2 6.1 %collective-permute-done.35 = bf16[96,768]{1,0:T(8,128)(2,1)S(1)} collective-permute-done((bf16[96,768]{1,0:T(8,128)(2,1)S(1)}, bf16[96,768]{1,0:T(8,128)(2,1)S(1)}, u32[]{:S(2)}, u32[]{:S(2)}) %collective-permute-start.35) | collective-permute-done | bytes 147488 | tf_op jit(solution)/shard_map/ppermute | solution.py:391
  104.0 7.8 %collective-permute-done.13.refs_11_ = bf16[192,768]{1,0:T(8,128)(2,1)S(1)} collective-permute-done((bf16[192,768]{1,0:T(8,128)(2,1)S(1)}, bf16[192,768]{1,0:T(8,128)(2,1)S(1)}, u32[]{:S(2)}, u32[]{:S(2)}) %collective-permute-start.13) | collective-permute-done | bytes 294944 | tf_op jit(solution)/shard_map/ppermute | solution.py:391
  116.5 11.8 %shard_map.305 = (bf16[2,2,128,384]{3,2,1,0:T(8,128)(2,1)}, bf16[8,2,128,384]{3,2,1,0:T(8,128)(2,1)}, bf16[8,2,128,384]{3,2,1,0:T(8,128)(2,1)}, bf16[768,1536]{1,0:T(8,128)(2,1)}, bf16[8,2,128,768]{3,2,1,0:T(8,128)(2,1)}) custom-call(bf16[2,128,768]{2,1,0:T(8,128)(2,1)} %bitcast.150, bf16[2,128,768]{2,1,0:T(8,128)(2,1)} %copy-done.47, ...), custom_call_target="tpu_custom_call" | custom-call | flops 2800000000 | bytes 16000000 | tf_op jit(solution)/shard_map/pallas_call | solution.py:863
  131.7 10.9 %shard_map.306 = (f32[2,384,256]{2,1,0:T(8,128)}, bf16[2,384,256]{2,1,0:T(8,128)(2,1)}, f32[2,8,256]{2,1,0:T(8,128)}) custom-call(bf16[2,2,128,384]{3,2,1,0:T(8,128)(2,1)} %get-tuple-element.83.q_ref, bf16[8,2,128,384]{3,2,1,0:T(8,128)(2,1)} %get-tuple-element.84.k_ref, bf16[8,2,128,384]{3,2,1,0:T(8,128)(2,1)} %get-tuple-element.85.v_ref, ...), custom_call_target="tpu_custom_call" | custom-call | flops 1600000000 | bytes 8000000 | tf_op jit(solution)/shard_map/pallas_call | solution.py:885
  155.8 5.9 %collective-permute-done.41.refs_19_ = bf16[384,384]{1,0:T(8,128)(2,1)} collective-permute-done((bf16[384,384]{1,0:T(8,128)(2,1)S(1)}, bf16[384,384]{1,0:T(8,128)(2,1)}, u32[]{:S(2)}, u32[]{:S(2)}) %collective-permute-start.41) | collective-permute-done | bytes 294944 | tf_op jit(solution)/shard_map/ppermute | solution.py:391
  174.6 12.6 %shard_map.307 = (f32[512,768]{1,0:T(8,128)}, f32[512,1]{1,0:T(8,128)}, bf16[512,768]{1,0:T(8,128)(2,1)}, bf16[512,1536]{1,0:T(8,128)(2,1)}, bf16[512,1536]{1,0:...) custom-call(bf16[8,2,128,768]{3,2,1,0:T(8,128)(2,1)} %get-tuple-element.82.refs_0_.x_r, ...), custom_call_target="tpu_custom_call" | custom-call | flops 2500000000 | bytes 16000000 | tf_op jit(solution)/shard_map/pallas_call | solution.py:900
  190.7 11.7 %shard_map.308 = (bf16[256,768]{1,0:T(8,128)(2,1)}, bf16[512,768]{1,0:T(8,128)(2,1)}, f32[512,768]{1,0:T(8,128)}, bf16[512,1536]{1,0:T(8,128)(2,1)}, bf16[512,76...) custom-call(f32[512,768]{1,0:T(8,128)} %get-tuple-element.94.n1_ref, ...), custom_call_target="tpu_custom_call" | custom-call | flops 2500000000 | bytes 16000000 | tf_op jit(solution)/shard_map/pallas_call | solution.py:909
  202.4 5.2 %shard_map.314 = (bf16[384,384]{1,0:T(8,128)(2,1)}, bf16[384,384]{1,0:T(8,128)(2,1)}, bf16[384,384]{1,0:T(8,128)(2,1)}, bf16[384,384]{1,0:T(8,128)(2,1)}, bf16[3...) custom-call(bf16[512,1536]{1,0:T(8,128)(2,1)} %get-tuple-element.135.act_ref, ...), custom_call_target="tpu_custom_call" | custom-call | flops 1200000000 | bytes 6000000 | tf_op jit(solution)/shard_map/pallas_call | solution.py:918
  211.8 5.0 %shard_map.313 = (bf16[192,768]{1,0:T(8,128)(2,1)}, bf16[192,768]{1,0:T(8,128)(2,1)}, bf16[192,768]{1,0:T(8,128)(2,1)}, bf16[192,768]{1,0:T(8,128)(2,1)}, bf16[1...) custom-call(bf16[512,768]{1,0:T(8,128)(2,1)} %get-tuple-element.125.low_ref,, ...), custom_call_target="tpu_custom_call" | custom-call | flops 1200000000 | bytes 6000000 | tf_op jit(solution)/shard_map/pallas_call | solution.py:927
  221.4 9.0 %collective-permute-done.70 = bf16[192,768]{1,0:T(8,128)(2,1)S(1)} collective-permute-done((bf16[192,768]{1,0:T(8,128)(2,1)}, bf16[192,768]{1,0:T(8,128)(2,1)S(1)}, u32[]{:S(2)}, u32[]{:S(2)}) %collective-permute-start.70) | collective-permute-done | bytes 294944 | tf_op jit(solution)/shard_map/ppermute | solution.py:391
  233.4 6.9 %collective-permute-done.84 = bf16[384,384]{1,0:T(8,128)(2,1)S(1)} collective-permute-done((bf16[384,384]{1,0:T(8,128)(2,1)S(1)}, bf16[384,384]{1,0:T(8,128)(2,1)S(1)}, u32[]{:S(2)}, u32[]{:S(2)}) %collective-permute-start.84) | collective-permute-done | bytes 294944 | tf_op jit(solution)/shard_map/ppermute | solution.py:391
  241.1 5.6 %collective-permute-done.71 = bf16[192,768]{1,0:T(8,128)(2,1)S(1)} collective-permute-done((bf16[192,768]{1,0:T(8,128)(2,1)S(1)}, bf16[192,768]{1,0:T(8,128)(2,1)S(1)}, u32[]{:S(2)}, u32[]{:S(2)}) %collective-permute-start.71) | collective-permute-done | bytes 294944 | tf_op jit(solution)/shard_map/ppermute | solution.py:391
  278.9 5.3 %shard_map.309 = (f32[256,768]{1,0:T(8,128)}, bf16[512,768]{1,0:T(8,128)(2,1)}, bf16[512,384]{1,0:T(8,128)(2,1)}, bf16[2,384,256]{2,1,0:T(8,128)(2,1)}, f32[8,768]{1,0:T(8,128)}) custom-call(f32[512,768]{1,0:T(8,128)} %get-tuple-element.101.dz_ref, bf16[512,768]{1,0:T(8,128)(2,1)} %get-tuple-element.102.own_ref, bf16[512,768]{1,0:T(8,128)(2,1)} %copy-done.11, ...), custom_call_target="tpu_custom_call" | custom-call | flops 300000000 | bytes 10000000 | tf_op jit(solution)/shard_map/pallas_call | solution.py:937
  285.7 11.3 %shard_map.310 = (bf16[2,2,128,384]{3,2,1,0:T(8,128)(2,1)}, bf16[8,2,128,384]{3,2,1,0:T(8,128)(2,1)}, bf16[8,2,128,384]{3,2,1,0:T(8,128)(2,1)}) custom-call(bf16[2,2,128,384]{3,2,1,0:T(8,128)(2,1)} %get-tuple-element.83.q_ref, bf16[8,2,128,384]{3,2,1,0:T(8,128)(2,1)} %get-tuple-element.84.k_ref, bf16[8,2,128,384]{3,2,1,0:T(8,128)(2,1)} %get-tuple-element.85.v_ref, ...), custom_call_target="tpu_custom_call" | custom-call | flops 4000000000 | bytes 12000000 | tf_op jit(solution)/shard_map/pallas_call | solution.py:944
  297.0 10.2 %shard_map.312 = (bf16[192,768]{1,0:T(8,128)(2,1)}, bf16[192,768]{1,0:T(8,128)(2,1)}, bf16[192,768]{1,0:T(8,128)(2,1)}, bf16[192,768]{1,0:T(8,128)(2,1)}, bf16[1...) custom-call(bf16[8,2,128,768]{3,2,1,0:T(8,128)(2,1)} %get-tuple-elem, ...), custom_call_target="tpu_custom_call" | custom-call | flops 3300000000 | bytes 12000000 | tf_op jit(solution)/shard_map/pallas_call | solution.py:976
  325.3 9.5 %shard_map.311 = (bf16[4,2,128,768]{3,2,1,0:T(8,128)(2,1)}, bf16[4,2,128,768]{3,2,1,0:T(8,128)(2,1)}) custom-call(bf16[2,2,128,384]{3,2,1,0:T(8,128)(2,1)} %get-tuple-element.106.dq_ref, bf16[8,2,128,384]{3,2,1,0:T(8,128)(2,1)} %get-tuple-element.107.dk_ref, bf16[8,2,128,384]{3,2,1,0:T(8,128)(2,1)} %get-tuple-element.108.dv_ref, ...), custom_call_target="tpu_custom_call" | custom-call | flops 2700000000 | bytes 10000000 | tf_op jit(solution)/shard_map/pallas_call | solution.py:956
  340.4 4.7 %collective-permute-done.58 = bf16[192,768]{1,0:T(8,128)(2,1)S(1)} collective-permute-done((bf16[192,768]{1,0:T(8,128)(2,1)S(1)}, bf16[192,768]{1,0:T(8,128)(2,1)S(1)}, u32[]{:S(2)}, u32[]{:S(2)}) %collective-permute-start.58) | collective-permute-done | bytes 294944 | tf_op jit(solution)/shard_map/ppermute | solution.py:391
  347.0 6.6 %collective-permute-done.53 = bf16[192,768]{1,0:T(8,128)(2,1)S(1)} collective-permute-done((bf16[192,768]{1,0:T(8,128)(2,1)S(1)}, bf16[192,768]{1,0:T(8,128)(2,1)S(1)}, u32[]{:S(2)}, u32[]{:S(2)}) %collective-permute-start.53) | collective-permute-done | bytes 294944 | tf_op jit(solution)/shard_map/ppermute | solution.py:391
  373.3 14.8 %collective-permute-done.47 = bf16[2,128,768]{2,1,0:T(8,128)(2,1)S(1)} collective-permute-done((bf16[2,128,768]{2,1,0:T(8,128)(2,1)S(1)}, bf16[2,128,768]{2,1,0:T(8,128)(2,1)S(1)}, u32[]{:S(2)}, u32[]{:S(2)}) %collective-permute-start.47) | collective-permute-done | bytes 393248 | tf_op jit(solution)/shard_map/ppermute | solution.py:391
  (465 shorter events, 197.9 us)
Async XLA Ops:
  6.4 22.9 %collective-permute-start.24 = (bf16[24,1536]{1,0:T(8,128)(2,1)S(1)}, bf16[24,1536]{1,0:T(8,128)(2,1)}, u32[]{:S(2)}, u32[]{:S(2)}) collective-permute-start(bf16[24,1536]{1,0:T(8,128)(2,1)S(1)} %select_n.312), channel_id=1, source_target_pairs={{0,1},{1,0},{2,3},{3,2},{4,5},{5,4},{6,7},{7,6},{8,9},{9,8},{10,11... | collective-permute-start | bytes 221192 | tf_op jit(solution)/shard_map/ppermute | solution.py:391
  39.0 21.4 %collective-permute-start.7 = (bf16[2,128,768]{2,1,0:T(8,128)(2,1)S(1)}, bf16[2,128,768]{2,1,0:T(8,128)(2,1)S(1)}, u32[]{:S(2)}, u32[]{:S(2)}) collective-permute-start(bf16[2,128,768]{2,1,0:T(8,128)(2,1)S(1)} %bitcast.152), channel_id=1, source_target_pairs={{0,4},{1,5},{2,6},{3,7},{4,0},{5,1},{6,2},{7,3},{8,12},{9,13},{10,... | collective-permute-start | bytes 1179656 | tf_op jit(solution)/shard_map/ppermute | solution.py:391
  40.1 20.8 %collective-permute-start.9 = (bf16[2,128,768]{2,1,0:T(8,128)(2,1)S(1)}, bf16[2,128,768]{2,1,0:T(8,128)(2,1)S(1)}, u32[]{:S(2)}, u32[]{:S(2)}) collective-permute-start(bf16[2,128,768]{2,1,0:T(8,128)(2,1)S(1)} %bitcast.153), channel_id=1, source_target_pairs={{2,4},{3,5},{4,2},{5,3},{10,12},{11,13},{12,10},{13,11},{18,20},{1... | collective-permute-start | bytes 1179656 | tf_op jit(solution)/shard_map/ppermute | solution.py:391
  44.1 51.4 %collective-permute-start.14 = (bf16[192,768]{1,0:T(8,128)(2,1)S(1)}, bf16[192,768]{1,0:T(8,128)(2,1)S(1)}, u32[]{:S(2)}, u32[]{:S(2)}) collective-permute-start(bf16[192,768]{1,0:T(8,128)(2,1)S(1)} %pad_maximum_fusion.2.refs_12_), channel_id=1, source_target_pairs={{0,8},{1,9},{2,10},{3,11},{4,12},{5,13},{6,14},{7,15},{8,0},{9,1},... | collective-permute-start | bytes 884744 | tf_op jit(solution)/shard_map/ppermute | solution.py:391
  47.7 47.8 %collective-permute-start.11 = (bf16[192,768]{1,0:T(8,128)(2,1)S(1)}, bf16[192,768]{1,0:T(8,128)(2,1)S(1)}, u32[]{:S(2)}, u32[]{:S(2)}) collective-permute-start(bf16[192,768]{1,0:T(8,128)(2,1)S(1)} %pad_maximum_fusion.1.refs_8_), channel_id=1, source_target_pairs={{0,8},{1,9},{2,10},{3,11},{4,12},{5,13},{6,14},{7,15},{8,0},{9,1},... | collective-permute-start | bytes 884744 | tf_op jit(solution)/shard_map/ppermute | solution.py:391
  52.9 43.3 %collective-permute-start.12 = (bf16[192,768]{1,0:T(8,128)(2,1)S(1)}, bf16[192,768]{1,0:T(8,128)(2,1)}, u32[]{:S(2)}, u32[]{:S(2)}) collective-permute-start(bf16[192,768]{1,0:T(8,128)(2,1)S(1)} %pad_maximum_fusion.1.refs_8_), channel_id=1, source_target_pairs={{0,16},{1,17},{2,18},{3,19},{4,20},{5,21},{6,22},{7,23},{8,24},{9,... | collective-permute-start | bytes 884744 | tf_op jit(solution)/shard_map/ppermute | solution.py:391
  60.4 41.9 %collective-permute-start.16 = (bf16[192,768]{1,0:T(8,128)(2,1)}, bf16[192,768]{1,0:T(8,128)(2,1)S(1)}, u32[]{:S(2)}, u32[]{:S(2)}) collective-permute-start(bf16[192,768]{1,0:T(8,128)(2,1)} %collective-permute-done.15.refs_14_), channel_id=1, source_target_pairs={{0,8},{1,9},{2,10},{3,11},{4,12},{5,13},{6,14},{7,15},{8,0},{9,1},... | collective-permute-start | bytes 884744 | tf_op jit(solution)/shard_map/ppermute | solution.py:391
  96.1 19.5 %collective-permute-start.6 = (bf16[2,128,768]{2,1,0:T(8,128)(2,1)S(1)}, bf16[2,128,768]{2,1,0:T(8,128)(2,1)S(1)}, u32[]{:S(2)}, u32[]{:S(2)}) collective-permute-start(bf16[2,128,768]{2,1,0:T(8,128)(2,1)S(1)} %collective-permute-done.5.refs_2_), channel_id=1, source_target_pairs={{0,1},{1,0},{2,3},{3,2},{4,5},{5,4},{6,7},{7,6},{8,9},{9,8},{10,11... | collective-permute-start | bytes 1179656 | tf_op jit(solution)/shard_map/ppermute | solution.py:391
  113.6 29.0 %collective-permute-start.32 = (bf16[192,768]{1,0:T(8,128)(2,1)S(1)}, bf16[192,768]{1,0:T(8,128)(2,1)}, u32[]{:S(2)}, u32[]{:S(2)}) collective-permute-start(bf16[192,768]{1,0:T(8,128)(2,1)S(1)} %pad_maximum_fusion.4.refs_9_), channel_id=1, source_target_pairs={{0,16},{1,17},{2,18},{3,19},{4,20},{5,21},{6,22},{7,23},{8,24},{9,... | collective-permute-start | bytes 884744 | tf_op jit(solution)/shard_map/ppermute | solution.py:391
  115.1 28.1 %collective-permute-start.28 = (bf16[192,768]{1,0:T(8,128)(2,1)S(1)}, bf16[192,768]{1,0:T(8,128)(2,1)}, u32[]{:S(2)}, u32[]{:S(2)}) collective-permute-start(bf16[192,768]{1,0:T(8,128)(2,1)S(1)} %pad_maximum_fusion.3.refs_5_), channel_id=1, source_target_pairs={{0,8},{1,9},{2,10},{3,11},{4,12},{5,13},{6,14},{7,15},{8,0},{9,1},... | collective-permute-start | bytes 884744 | tf_op jit(solution)/shard_map/ppermute | solution.py:391
  131.2 22.0 %collective-permute-start.29 = (bf16[192,768]{1,0:T(8,128)(2,1)S(1)}, bf16[192,768]{1,0:T(8,128)(2,1)}, u32[]{:S(2)}, u32[]{:S(2)}) collective-permute-start(bf16[192,768]{1,0:T(8,128)(2,1)S(1)} %pad_maximum_fusion.3.refs_5_), channel_id=1, source_target_pairs={{0,16},{1,17},{2,18},{3,19},{4,20},{5,21},{6,22},{7,23},{8,24},{9,... | collective-permute-start | bytes 884744 | tf_op jit(solution)/shard_map/ppermute | solution.py:391
  146.9 26.8 %collective-permute-start.23 = (bf16[512,768]{1,0:T(8,128)(2,1)S(1)}, bf16[512,768]{1,0:T(8,128)(2,1)S(1)}, u32[]{:S(2)}, u32[]{:S(2)}) collective-permute-start(bf16[512,768]{1,0:T(8,128)(2,1)S(1)} %bitcast.118), channel_id=1, source_target_pairs={{0,1},{1,0},{2,3},{3,2},{4,5},{5,4},{6,7},{7,6},{8,9},{9,8},{10,11... | collective-permute-start | bytes 2359304 | tf_op jit(solution)/shard_map/ppermute | solution.py:391
  169.7 19.9 %collective-permute-start.44 = (bf16[2,128,768]{2,1,0:T(8,128)(2,1)}, bf16[2,128,768]{2,1,0:T(8,128)(2,1)}, u32[]{:S(2)}, u32[]{:S(2)}) collective-permute-start(bf16[2,128,768]{2,1,0:T(8,128)(2,1)} %bitcast.129), channel_id=1, source_target_pairs={{0,1},{1,0},{2,3},{3,2},{4,5},{5,4},{6,7},{7,6},{8,9},{9,8},{10,11... | collective-permute-start | bytes 1179656 | tf_op jit(solution)/shard_map/ppermute | solution.py:391
  208.2 24.4 %collective-permute-start.82 = (bf16[384,384]{1,0:T(8,128)(2,1)}, bf16[384,384]{1,0:T(8,128)(2,1)S(1)}, u32[]{:S(2)}, u32[]{:S(2)}) collective-permute-start(bf16[384,384]{1,0:T(8,128)(2,1)} %get-tuple-element.138), channel_id=1, source_target_pairs={{0,16},{1,17},{2,18},{3,19},{4,20},{5,21},{6,22},{7,23},{8,24},{9,... | collective-permute-start | bytes 884744 | tf_op jit(solution)/shard_map/ppermute | solution.py:391
  210.3 37.1 %collective-permute-start.88 = (bf16[384,384]{1,0:T(8,128)(2,1)}, bf16[384,384]{1,0:T(8,128)(2,1)S(1)}, u32[]{:S(2)}, u32[]{:S(2)}) collective-permute-start(bf16[384,384]{1,0:T(8,128)(2,1)} %get-tuple-element.142), channel_id=1, source_target_pairs={{0,8},{1,9},{2,10},{3,11},{4,12},{5,13},{6,14},{7,15},{8,0},{9,1},... | collective-permute-start | bytes 884744 | tf_op jit(solution)/shard_map/ppermute | solution.py:391
  219.1 21.4 %collective-permute-start.69 = (bf16[192,768]{1,0:T(8,128)(2,1)}, bf16[192,768]{1,0:T(8,128)(2,1)S(1)}, u32[]{:S(2)}, u32[]{:S(2)}) collective-permute-start(bf16[192,768]{1,0:T(8,128)(2,1)} %get-tuple-element.128), channel_id=1, source_target_pairs={{0,16},{1,17},{2,18},{3,19},{4,20},{5,21},{6,22},{7,23},{8,24},{9,... | collective-permute-start | bytes 884744 | tf_op jit(solution)/shard_map/ppermute | solution.py:391
  240.3 37.6 %collective-permute-start.45 = (bf16[512,768]{1,0:T(8,128)(2,1)S(1)}, bf16[512,768]{1,0:T(8,128)(2,1)S(1)}, u32[]{:S(2)}, u32[]{:S(2)}) collective-permute-start(bf16[512,768]{1,0:T(8,128)(2,1)S(1)} %copy-done.10), channel_id=1, source_target_pairs={{0,1},{1,0},{2,3},{3,2},{4,5},{5,4},{6,7},{7,6},{8,9},{9,8},{10,11... | collective-permute-start | bytes 2359304 | tf_op jit(solution)/shard_map/ppermute | solution.py:391
  247.4 64.0 %collective-permute-start.85 = (bf16[96,384]{1,0:T(8,128)(2,1)S(1)}, bf16[96,384]{1,0:T(8,128)(2,1)S(1)}, u32[]{:S(2)}, u32[]{:S(2)}) collective-permute-start(bf16[96,384]{1,0:T(8,128)(2,1)S(1)} %get-tuple-element.190), channel_id=1, source_target_pairs={{0,2},{1,3},{2,0},{3,1},{4,6},{5,7},{6,4},{7,5},{8,10},{9,11},{10,... | collective-permute-start | bytes 221192 | tf_op jit(solution)/shard_map/ppermute | solution.py:391
  272.5 38.9 %collective-permute-start.86 = (bf16[96,384]{1,0:T(8,128)(2,1)S(1)}, bf16[96,384]{1,0:T(8,128)(2,1)S(1)}, u32[]{:S(2)}, u32[]{:S(2)}) collective-permute-start(bf16[96,384]{1,0:T(8,128)(2,1)S(1)} %get-tuple-element.192), channel_id=1, source_target_pairs={{0,4},{1,5},{2,6},{3,7},{4,0},{5,1},{6,2},{7,3},{8,12},{9,13},{10,... | collective-permute-start | bytes 221192 | tf_op jit(solution)/shard_map/ppermute | solution.py:391
  277.2 34.2 %collective-permute-start.87 = (bf16[96,384]{1,0:T(8,128)(2,1)S(1)}, bf16[96,384]{1,0:T(8,128)(2,1)S(1)}, u32[]{:S(2)}, u32[]{:S(2)}) collective-permute-start(bf16[96,384]{1,0:T(8,128)(2,1)S(1)} %get-tuple-element.191), channel_id=1, source_target_pairs={{0,6},{1,7},{2,4},{3,5},{4,2},{5,3},{6,0},{7,1},{8,14},{9,15},{10,... | collective-permute-start | bytes 221192 | tf_op jit(solution)/shard_map/ppermute | solution.py:391
  336.9 20.1 %collective-permute-start.57 = (bf16[192,768]{1,0:T(8,128)(2,1)S(1)}, bf16[192,768]{1,0:T(8,128)(2,1)S(1)}, u32[]{:S(2)}, u32[]{:S(2)}) collective-permute-start(bf16[192,768]{1,0:T(8,128)(2,1)S(1)} %copy-done.51), channel_id=1, source_target_pairs={{0,8},{1,9},{2,10},{3,11},{4,12},{5,13},{6,14},{7,15},{8,0},{9,1},... | collective-permute-start | bytes 884744 | tf_op jit(solution)/shard_map/ppermute | solution.py:391
  337.2 30.9 %collective-permute-start.46 = (bf16[4,2,128,768]{3,2,1,0:T(8,128)(2,1)}, bf16[4,2,128,768]{3,2,1,0:T(8,128)(2,1)S(1)}, u32[]{:S(2)}, u32[]{:S(2)}) collective-permute-start(bf16[4,2,128,768]{3,2,1,0:T(8,128)(2,1)} %get-tuple-element.110), channel_id=1, source_target_pairs={{0,1},{1,0},{2,3},{3,2},{4,5},{5,4},{6,7},{7,6},{8,9},{9,8},{10,11... | collective-permute-start | bytes 4718600 | tf_op jit(solution)/shard_map/ppermute | solution.py:391
  368.4 19.7 %collective-permute-start.47 = (bf16[2,128,768]{2,1,0:T(8,128)(2,1)S(1)}, bf16[2,128,768]{2,1,0:T(8,128)(2,1)S(1)}, u32[]{:S(2)}, u32[]{:S(2)}) collective-permute-start(bf16[2,128,768]{2,1,0:T(8,128)(2,1)S(1)} %get-tuple-element.179), channel_id=1, source_target_pairs={{0,2},{1,3},{2,0},{3,1},{4,6},{5,7},{6,4},{7,5},{8,10},{9,11},{10,... | collective-permute-start | bytes 1179656 | tf_op jit(solution)/shard_map/ppermute | solution.py:391
  368.5 21.7 %collective-permute-start.48 = (bf16[2,128,768]{2,1,0:T(8,128)(2,1)S(1)}, bf16[2,128,768]{2,1,0:T(8,128)(2,1)S(1)}, u32[]{:S(2)}, u32[]{:S(2)}) collective-permute-start(bf16[2,128,768]{2,1,0:T(8,128)(2,1)S(1)} %get-tuple-element.181), channel_id=1, source_target_pairs={{0,4},{1,5},{2,6},{3,7},{4,0},{5,1},{6,2},{7,3},{8,12},{9,13},{10,... | collective-permute-start | bytes 1179656 | tf_op jit(solution)/shard_map/ppermute | solution.py:391
  (139 other events, 1623.9 us)

commit v2 on v1

--- a/solution.py
+++ b/solution.py
@@ -383,8 +383,9 @@
 
 
 CORE, Z1, Z2, Z3 = pairs(0, 1), pairs(0, 2), pairs(0, 4), pairs(0, 6)
-Z3_INNER = pairs(0, 6, lambda dp, seq: seq // 2 in (1, 2))
 X, Y = pairs(1, 0), pairs(2, 0)
+MIDDLE = pairs(0, 6, lambda dp, seq: seq // 2 in (1, 2))
+OUTWARD = pairs(0, 2, lambda dp, seq: seq // 2 in (1, 2))
 
 
 def send(value, route):
@@ -393,6 +394,10 @@
 
 def after(value, *events):
     return lax.optimization_barrier((value, *events))[0]
+
+
+def after_both(values, events):
+    return lax.optimization_barrier((tuple(values), tuple(events)))[0]
 
 
 def my_chip():
@@ -430,47 +435,138 @@
     )
 
 
-def gather_z(block):
-    parts = [block, send(block, Z1), send(block, Z2), send(block, Z3)]
-    half = block.shape[1] // 2
+def line(block):
+    return [block, send(block, Z1), send(block, Z2), send(block, Z3)]
+
+
+def across(parts, rows):
+    return tuple(
+        jnp.concatenate(
+            [p[:48, c : c + 768] for p in parts] + [p[48:, c : c + 768] for p in parts if rows > 48], axis=0
+        )
+        for c in (0, 768)
+    )
+
+
+def near_hop(first, second):
     return (
-        jnp.concatenate([p[:, :half] for p in parts], axis=0),
-        jnp.concatenate([p[:, half:] for p in parts], axis=0),
-    )
-
-
-def gather_xy(first, second):
-    first_x, second_y = send(first, X), send(second, Y)
-    first_y, second_x = send(first, Y), send(second, X)
-    return (
-        (first, first_x, first_y, send(first_x, Y)),
-        (second, second_x, second_y, send(second_y, X)),
-    )
-
-
-def placed(groups, rows, target, cols, sems, base):
+        jnp.concatenate([first, send(first, X)], axis=0),
+        jnp.concatenate([second, send(second, Y)], axis=0),
+    )
+
+
+def far_hop(first, second):
+    return (first, send(first, Y), second, send(second, X))
+
+
+def placed(groups, target, sems, base):
     me = my_chip()
-    half = groups[0].shape[1]
+    pitch = groups[0].shape[0] // 2
     copies = []
-    for g in range(4):
+    for half in range(2):
+        for far in range(2):
+            for near in range(2):
+                for z in range(4):
+                    across_bits = far * 8 + near * 4 if half == 0 else near * 8 + far * 4
+                    at = pl.multiple_of(((across_bits + z) ^ me) * 48, 16)
+                    copies.append(
+                        pltpu.make_async_copy(
+                            groups[half * 2 + far].at[pl.ds(near * pitch + z * 48, 48), :],
+                            target.at[pl.ds(at, 48), pl.ds(half * 768, 768)],
+                            sems.at[base + len(copies)],
+                        )
+                    )
+    return copies
+
+
+def placed_hidden(both, w1, w2, sems):
+    me = my_chip() % 4
+    first, second = [], []
+    for line_index in range(4):
         for z in range(4):
-            at = pl.multiple_of(((g * 4 + z) ^ me) * rows, 16)
-            copies.append(
-                pltpu.make_async_copy(
-                    groups[g].at[pl.ds(z * rows, rows), :],
-                    target.at[pl.ds(at, rows), pl.ds(cols, half)],
-                    sems.at[base + g * 4 + z],
+            b, i = line_index * 4 + (z ^ me), line_index * 4 + z
+            rows = both.at[pl.ds(i * 48, 48)]
+            at1, at2 = pl.multiple_of(b * 48, 16), pl.multiple_of(b * 96, 16)
+            first.append(
+                pltpu.make_async_copy(rows.at[:, pl.ds(0, 1536)], w1.at[pl.ds(at1, 48)], sems.at[i])
+            )
+            for part in range(2):
+                second.append(
+                    pltpu.make_async_copy(
+                        rows.at[:, pl.ds(1536 + 768 * part, 768)],
+                        w2.at[pl.ds(at2 + 48 * part, 48)],
+                        sems.at[16 + 2 * i + part],
+                    )
                 )
-            )
-    return copies
+    return (first, second)
+
+
+def prepare_kernel(*refs):
+    weights, vecs, outer_ref = refs[0:4], refs[4:13], refs[13]
+    mine_ref, theirs_ref, rows_ref = refs[14:]
+    even = my_core() == 0
+    theirs_ref[24:32] = jnp.zeros((8, 1536), BF16)
+    for i, ref in enumerate(weights):
+        w, cols = ref[...].astype(BF16), slice(384 * i, 384 * i + 384)
+        mine_ref[0:24, cols] = jnp.where(even, w[:, :384], w[:, 384:])
+        theirs_ref[0:24, cols] = jnp.where(even, w[:, 384:], w[:, :384])
+    pieces = []
+    for ref in vecs:
+        pieces += [ref[...], jnp.zeros((1, 128 - ref.shape[1]), F32)]
+    row = jnp.concatenate(pieces + [jnp.zeros((1, 384), F32)], axis=1)
+    row = jnp.where(lax.broadcasted_iota(jnp.int32, (8, 1536), 0) == 0, row, 0.0).astype(BF16)
+    mine_ref[24:32] = row
+    theirs_ref[24:32] = row
+    rows_ref[:, 0:768] = outer_ref[0:48].astype(BF16)
+    rows_ref[:, 768:1536] = outer_ref[48:96].astype(BF16)
+
+
+def chip_rows_kernel(mine_ref, got_ref, out_ref):
+    even = my_core() == 0
+    mine, got = mine_ref[...].astype(F32), got_ref[...].astype(F32)
+    out_ref[0:24] = jnp.where(even, mine[:24], got[:24]).astype(BF16)
+    out_ref[24:48] = jnp.where(even, got[:24], mine[:24]).astype(BF16)
+    first = jnp.where(even, mine[24:32], got[24:32])
+    second = jnp.where(even, got[24:32], mine[24:32])
+    row = lax.broadcasted_iota(jnp.int32, (8, 1536), 0)
+    out_ref[48:56] = jnp.where(row == 1, second[0:1], jnp.where(row == 0, first[0:1], 0.0)).astype(BF16)
+
+
+def owner_kernel(first_ref, second_ref, *refs):
+    parts, (keep_ref, other_ref) = refs[:3], refs[3:]
+    even = my_core() == 0
+    for c, ref in ((0, first_ref), (768, second_ref)):
+        cols = slice(c, c + 768)
+        a, b, d = (p[:, cols].astype(F32) for p in parts)
+        rows = ref[0:48].astype(F32) + a[:48] + b[:48] + d[:48]
+        keep_ref[0:24, cols] = jnp.where(even, rows[:24], rows[24:])
+        other_ref[0:24, cols] = jnp.where(even, rows[24:], rows[:24]).astype(BF16)
+        vec = ref[192:200].astype(F32) + a[48:56] + b[48:56] + d[48:56]
+        zero = jnp.zeros((7, 768), F32)
+        keep_ref[24:32, cols] = jnp.concatenate([jnp.where(even, vec[0:1], vec[1:2]), zero], axis=0)
+        other_ref[24:32, cols] = jnp.concatenate([jnp.where(even, vec[1:2], vec[0:1]), zero], axis=0).astype(BF16)
+
+
+def result_kernel(keep_ref, got_ref, *refs):
+    outs, vecs = refs[:4], refs[4:]
+    even = my_core() == 0
+    for i, ref in enumerate(outs):
+        cols = slice(384 * i, 384 * i + 384)
+        keep, got = keep_ref[0:24, cols], got_ref[0:24, cols].astype(F32)
+        ref[:, 0:384] = jnp.where(even, keep, got)
+        ref[:, 384:768] = jnp.where(even, got, keep)
+    vec = keep_ref[24:25] + got_ref[24:32].astype(F32)[0:1]
+    for i, ref in enumerate(vecs):
+        ref[...] = vec[:, 128 * i : 128 * i + ref.shape[1]]
 
 
 def project_kernel(*refs):
-    xs, first, second = refs[0:8], refs[8:12], refs[12:16]
-    bq_ref, bv_ref = refs[16:18]
-    q_ref, k_ref, v_ref, w_ref, x_ref, sems = refs[18:]
-    loads = [pltpu.make_async_copy(xs[s], x_ref.at[s], sems.at[32 + s]) for s in range(8)]
-    loads += placed(first, 48, w_ref, 0, sems, 0) + placed(second, 48, w_ref, 768, sems, 16)
+    xs, theirs, groups = refs[0:5], refs[5], refs[6:10]
+    bq_ref, bv_ref = refs[10:12]
+    q_ref, k_ref, v_ref, w_ref, x_ref, sems = refs[12:]
+    slots = [*zip((0, 1, 2, 4, 6), xs), *((2 * z + 3, theirs.at[z]) for z in range(3))]
+    loads = [pltpu.make_async_copy(ref, x_ref.at[s], sems.at[32 + s]) for s, ref in slots]
+    loads += placed(groups, w_ref, sems, 0)
     for c in loads:
         c.start()
     for c in loads:
@@ -496,19 +592,26 @@
 
 def attend_kernel(q_ref, k_ref, v_ref, kseg_ref, qseg_ref, mix_ref, low_ref, lse_ref):
     mask = jnp.where(kseg_ref[0] == qseg_ref[0], 0.0, -1e30)
-    q = q_ref[:, 0].reshape(2 * BAND, 384)
-    for h in range(6):
-        cols = slice(64 * h, 64 * h + 64)
-        k = k_ref[:, 0, :, cols].reshape(8 * BAND, 64)
-        v = v_ref[:, 0, :, cols].reshape(8 * BAND, 64)
-        s = dot_nt(k, q[:, cols]) + mask
-        top = jnp.max(s, axis=0, keepdims=True)
-        e = jnp.exp(s - top)
-        total = jnp.sum(e, axis=0, keepdims=True)
-        mixed = dot_tn(v, e.astype(BF16)) * (1.0 / total)
-        mix_ref[0, cols] = mixed
-        low_ref[0, cols] = mixed.astype(BF16)
-        lse_ref[0, h : h + 1] = top + jnp.log(total)
+
+    def pair(j, _):
+        both = pl.ds(pl.multiple_of(128 * j, 128), 128)
+        q2 = q_ref[:, 0, :, both].reshape(2 * BAND, 128)
+        k2 = k_ref[:, 0, :, both].reshape(8 * BAND, 128)
+        v2 = v_ref[:, 0, :, both].reshape(8 * BAND, 128)
+        for h in range(2):
+            cols = slice(64 * h, 64 * h + 64)
+            s = dot_nt(k2[:, cols], q2[:, cols]) + mask
+            top = jnp.max(s, axis=0, keepdims=True)
+            e = jnp.exp(s - top)
+            total = jnp.sum(e, axis=0, keepdims=True)
+            mixed = dot_tn(v2[:, cols], e.astype(BF16)) * (1.0 / total)
+            rows = pl.ds(pl.multiple_of(128 * j + 64 * h, 64), 64)
+            mix_ref[0, rows] = mixed
+            low_ref[0, rows] = mixed.astype(BF16)
+            lse_ref[0, pl.ds(2 * j + h, 1)] = top + jnp.log(total)
+        return 0
+
+    lax.fori_loop(0, 3, pair, 0)
 
 
 def norm(z):
@@ -529,11 +632,10 @@
 
 def forward_kernel(*refs):
     x_ref, own_ref, other_ref, vec_ref, b1_ref = refs[0:5]
-    wa, wb, va, vb = refs[5:9], refs[9:13], refs[13:17], refs[17:21]
-    n1_ref, r1_ref, low_ref, act_ref, slope_ref, f_ref, w1_ref, w2_ref, tok_ref, sems = refs[21:]
-    loads1 = placed(wa, 48, w1_ref, 0, sems, 0) + placed(wb, 48, w1_ref, 768, sems, 16)
-    loads2 = placed(va, 96, w2_ref, 0, sems, 32) + placed(vb, 96, w2_ref, 384, sems, 48)
-    tokens = pltpu.make_async_copy(x_ref.at[pl.ds(0, 2)], tok_ref, sems.at[64])
+    both = refs[5]
+    n1_ref, r1_ref, low_ref, act_ref, slope_ref, f_ref, w1_ref, w2_ref, tok_ref, sems = refs[6:]
+    loads1, loads2 = placed_hidden(both, w1_ref, w2_ref, sems)
+    tokens = pltpu.make_async_copy(x_ref.at[pl.ds(0, 2)], tok_ref, sems.at[48])
     for c in [tokens] + loads1 + loads2:
         c.start()
     tokens.wait()
@@ -575,8 +677,7 @@
 
 
 def middle_kernel(
-    n1_ref, own_ref, other_ref, cot_ref, pcot_ref, vec_ref, slope_ref, w1_ref, w2_ref,
-    out_ref, df_ref, dz_ref, du_ref, dh_ref, sums_ref, db1_ref,
+    n1_ref, own_ref, other_ref, cot_ref, pcot_ref, vec_ref, out_ref, df_ref, dz_ref, sums_ref,
 ):
     g1, s1, b2, g2, s2 = (vec_ref[i : i + 1] for i in (3, 4, 5, 6, 7))
 
@@ -608,6 +709,8 @@
     lax.fori_loop(0, 2, own_rows, 0)
     lax.fori_loop(0, 2, other_rows, 0)
 
+
+def hidden_kernel(df_ref, slope_ref, w1_ref, w2_ref, du_ref, dh_ref, db1_ref):
     def hidden(j, _):
         cols = pl.ds(pl.multiple_of(j * 256, 256), 256)
         du = (dot_nt(df_ref[...], w2_ref[cols, :]) * slope_ref[:, cols].astype(F32)).astype(BF16)
@@ -662,109 +765,142 @@
 
 def attend_back_kernel(q_ref, k_ref, v_ref, mix_ref, da_ref, lse_ref, kseg_ref, qseg_ref, dq_ref, dk_ref, dv_ref):
     mask = jnp.where(kseg_ref[0] == qseg_ref[0], 0.0, -1e30)
-    q = q_ref[:, 0].reshape(2 * BAND, 384)
-    for pair in range(3):
+
+    def pair(j, _):
+        both = pl.ds(pl.multiple_of(128 * j, 128), 128)
+        q2 = q_ref[:, 0, :, both].reshape(2 * BAND, 128)
+        k2 = k_ref[:, 0, :, both].reshape(8 * BAND, 128)
+        v2 = v_ref[:, 0, :, both].reshape(8 * BAND, 128)
         dks, dvs, dqs = [], [], []
-        for h in (2 * pair, 2 * pair + 1):
+        for h in range(2):
             cols = slice(64 * h, 64 * h + 64)
-            k = k_ref[:, 0, :, cols].reshape(8 * BAND, 64)
-            v = v_ref[:, 0, :, cols].reshape(8 * BAND, 64)
-            qh, da = q[:, cols], da_ref[0, cols]
-            p = jnp.exp(dot_nt(k, qh) + mask - lse_ref[0, h : h + 1])
-            delta = jnp.sum(da.astype(F32) * mix_ref[0, cols], axis=0, keepdims=True)
+            rows = pl.ds(pl.multiple_of(128 * j + 64 * h, 64), 64)
+            k, v, qh, da = k2[:, cols], v2[:, cols], q2[:, cols], da_ref[0, rows]
+            p = jnp.exp(dot_nt(k, qh) + mask - lse_ref[0, pl.ds(2 * j + h, 1)])
+            delta = jnp.sum(da.astype(F32) * mix_ref[0, rows], axis=0, keepdims=True)
             ds = (p * (dot_nn(v, da) - delta)).astype(BF16)
             dvs.append(dot_nt(p.astype(BF16), da))
             dks.append(dot_nn(ds, qh))
             dqs.append(dot_tn(k, ds))
-        both = slice(128 * pair, 128 * pair + 128)
-        dk_ref[:, 0, :, both] = jnp.concatenate(dks, axis=1).astype(BF16).reshape(8, BAND, 128)
-        dv_ref[:, 0, :, both] = jnp.concatenate(dvs, axis=1).astype(BF16).reshape(8, BAND, 128)
+        dk_ref[:, :, both] = jnp.concatenate(dks, axis=1).astype(BF16).reshape(8, BAND, 128)
+        dv_ref[:, :, both] = jnp.concatenate(dvs, axis=1).astype(BF16).reshape(8, BAND, 128)
         dq = jnp.transpose(jnp.concatenate(dqs, axis=0) * 0.125)
-        dq_ref[:, 0, :, both] = dq.astype(BF16).reshape(2, BAND, 128)
+        dq_ref[:, :, both] = dq.astype(BF16).reshape(2, BAND, 128)
+        return 0
+
+    lax.fori_loop(0, 3, pair, 0)
 
 
 def token_grad_kernel(dq_ref, dk_ref, dv_ref, w_ref, own_ref, send_ref):
-    z = pl.program_id(0)
-    for c, ref in enumerate((own_ref, send_ref)):
-        dk = dk_ref[c].reshape(2 * BAND, 384)
-        dv = dv_ref[c].reshape(2 * BAND, 384)
-        ref[0] = (dot_nt(dk, w_ref[:, 384:768]) + dot_nt(dv, w_ref[:, 768:1152])).astype(BF16).reshape(2, BAND, 768)
-
-        @pl.when(z == 0)
-        def _():
-            dq = dq_ref[c].reshape(2 * BAND, 384)
-            dx = dot_nt(dk, w_ref[:, 384:768]) + dot_nt(dv, w_ref[:, 768:1152]) + dot_nt(dq, w_ref[:, 0:384])
-            ref[0] = dx.astype(BF16).reshape(2, BAND, 768)
-
-
-def place_rows(scratch, value, first_block, rows, cols):
-    me = my_chip()
-    for i in range(value.shape[0] // rows):
-        at = pl.multiple_of(((first_block + i) ^ me) * rows, 16)
-        scratch[pl.ds(at, rows), cols] = value[i * rows : (i + 1) * rows].astype(BF16)
-
-
-def flush(scratch, outs, sems):
-    rows, half = outs[0].shape
-    copies = []
-    for i, out in enumerate(outs):
-        src = scratch.at[pl.ds((i % 4) * rows, rows), pl.ds((i // 4) * half, half)]
-        copies.append(pltpu.make_async_copy(src, out, sems.at[i]))
+    def step(z, _):
+        dk = dk_ref[pl.ds(2 * z, 2)].reshape(2 * BAND, 384)
+        dv = dv_ref[pl.ds(2 * z, 2)].reshape(2 * BAND, 384)
+        dx = dot_nt(dk, w_ref[:, 384:768]) + dot_nt(dv, w_ref[:, 768:1152])
+        own_ref[z] = dx[:BAND].astype(BF16)
+        send_ref[z] = dx[BAND:].astype(BF16)
+        return 0
+
+    lax.fori_loop(1, 4, step, 0)
+    dx = dot_nt(dk_ref[0:2].reshape(2 * BAND, 384), w_ref[:, 384:768])
+    dx += dot_nt(dv_ref[0:2].reshape(2 * BAND, 384), w_ref[:, 768:1152])
+    dx += dot_nt(dq_ref[...].reshape(2 * BAND, 384), w_ref[:, 0:384])
+    own_ref[0] = dx[:BAND].astype(BF16)
+    send_ref[0] = dx[BAND:].astype(BF16)
+
+
+def stored_at(block):
+    p = block ^ my_chip()
+    y, x, z = p // 8, (p // 4) % 2, p % 4
+    return ((y, x * 4 + z), (x, y * 4 + z))
+
+
+def place_rows(halves, block, first, second):
+    for ref, (away, row), value in zip(halves, stored_at(block), (first, second)):
+        ref[away, pl.ds(pl.multiple_of(row * 48, 16), 48)] = value
+
+
+def flush(halves, outs, sems):
+    copies = [
+        pltpu.make_async_copy(halves[i // 2].at[i % 2], out.at[pl.ds(0, 384)], sems.at[i])
+        for i, out in enumerate(outs)
+    ]
+    return copies
+
+
+def finish(copies):
     for c in copies:
         c.start()
     for c in copies:
         c.wait()
 
 
-def outer_grad_kernel(act_ref, df_ref, *refs):
-    outs, scratch, sems = refs[:8], refs[8], refs[9]
+def outer_grad_kernel(act_ref, df_ref, out_ref):
+    me = my_chip() % 4
 
     def step(j, _):
         cols = pl.ds(pl.multiple_of(j * 384, 384), 384)
-        place_rows(scratch, dot_tn(act_ref[:, cols], df_ref[...]), j * 4, 96, slice(0, 768))
+        value = dot_tn(act_ref[:, cols], df_ref[...]).astype(BF16)
+        for i in range(4):
+            rows = pl.ds(pl.multiple_of((j * 4 + (i ^ me)) * 48, 16), 48)
+            out_ref[rows, 0:768] = value[96 * i : 96 * i + 48]
+            out_ref[rows, 768:1536] = value[96 * i + 48 : 96 * i + 96]
         return 0
 
     lax.fori_loop(0, 4, step, 0)
-    flush(scratch, outs, sems)
-
-
-def inner_grad_kernel(low_ref, du_ref, *refs):
-    outs, scratch, sems = refs[:8], refs[8], refs[9]
+
+
+def inner_grad_kernel(low_ref, du_ref, out_ref):
+    me = my_chip() % 4
 
     def step(j, _):
         cols = pl.ds(pl.multiple_of(j * 384, 384), 384)
-        place_rows(scratch, dot_tn(low_ref[:, cols], du_ref[...]), j * 8, 48, slice(0, 1536))
+        value = dot_tn(low_ref[:, cols], du_ref[...]).astype(BF16)
+        for i in range(8):
+            rows = pl.ds(pl.multiple_of((j * 8 + (i ^ me)) * 48, 16), 48)
+            out_ref[rows, :] = value[48 * i : 48 * i + 48]
         return 0
 
     lax.fori_loop(0, 2, step, 0)
-    flush(scratch, outs, sems)
-
-
-def projection_grad_kernel(x_ref, dq_ref, dk_ref, dv_ref, mix0_ref, mix1_ref, half_ref, *refs):
-    outs, sums_ref, scratch, sems = refs[:8], refs[8], refs[9], refs[10]
-    dq = dq_ref[...].reshape(4 * BAND, 384)
-    sums_ref[0:1] = jnp.sum(dq.astype(F32), axis=0, keepdims=True)
-
-    def count(s, acc):
-        return acc + jnp.sum(dv_ref[s].reshape(2 * BAND, 384).astype(F32), axis=0, keepdims=True)
-
-    sums_ref[1:2] = lax.fori_loop(0, 8, count, jnp.zeros((1, 384), F32))
+
+
+def projection_grad_kernel(x_ref, *refs):
+    dqs, dks, dvs, (mix0, mix1, other_ref, half_ref, vec_ref) = refs[0:2], refs[2:4], refs[4:6], refs[6:11]
+    refs = refs[11:]
+    outs, halves, dwo_ref, sems = refs[:4], refs[4:6], refs[6], refs[7]
+    core = my_core()
     half = half_ref[...].reshape(2, 2, BAND, 384)
+    own = [half[:, m].reshape(2 * BAND, 384) for m in range(2)]
+    dwo = dot_nn(mix0[...], own[0]) + dot_nn(mix1[...], own[1])
+    dwo_ref[pl.ds(pl.multiple_of(core * 384, 384), 384)] = dwo.astype(BF16)
+    other = [jnp.concatenate([half[1, m], half[0, m]], axis=0) for m in range(2)]
+    dwo = dot_nn(other_ref[0], other[0]) + dot_nn(other_ref[1], other[1])
+    dwo_ref[pl.ds(pl.multiple_of((1 - core) * 384, 384), 384)] = dwo.astype(BF16)
 
     def step(j, _):
         cols = pl.ds(pl.multiple_of(j * 384, 384), 384)
-        x = x_ref[:, :, :, cols].reshape(16 * BAND, 384)
-        place_rows(scratch, dot_tn(x[: 4 * BAND], dq), j * 8, 48, slice(0, 384))
-        place_rows(scratch, dot_tn(x, dk_ref[...].reshape(16 * BAND, 384)), j * 8, 48, slice(384, 768))
-        place_rows(scratch, dot_tn(x, dv_ref[...].reshape(16 * BAND, 384)), j * 8, 48, slice(768, 1152))
-        rows = pl.ds(pl.multiple_of(j * 384, 384), 384)
-        dwo = dot_nn(mix0_ref[rows], half[:, 0].reshape(2 * BAND, 384))
-        dwo += dot_nn(mix1_ref[rows], half[:, 1].reshape(2 * BAND, 384))
-        place_rows(scratch, dwo, j * 8, 48, slice(1152, 1536))
+        x = [x_ref[:, m, :, cols].reshape(8 * BAND, 384) for m in range(2)]
+
+        def total(refs, count):
+            terms = [dot_tn(x[m][: count * BAND], refs[m][...].reshape(count * BAND, 384)) for m in range(2)]
+            return (terms[0] + terms[1]).astype(BF16)
+
+        dwq, dwk, dwv = total(dqs, 2), total(dks, 8), total(dvs, 8)
+        for i in range(8):
+            rows = slice(48 * i, 48 * i + 48)
+            dwo = dwo_ref[pl.ds(pl.multiple_of(j * 384 + 48 * i, 16), 48)]
+            place_rows(
+                halves,
+                j * 8 + i,
+                jnp.concatenate([dwq[rows], dwk[rows]], axis=1),
+                jnp.concatenate([dwv[rows], dwo], axis=1),
+            )
         return 0
 
     lax.fori_loop(0, 2, step, 0)
-    flush(scratch, outs, sems)
+    copies = flush(halves, outs, sems)
+    for i, out in enumerate(outs):
+        copies.append(pltpu.make_async_copy(vec_ref.at[i], out.at[pl.ds(384, 64)], sems.at[4 + i]))
+    finish(copies)
 
 
 def add(*terms):
@@ -774,23 +910,55 @@
     return total
 
 
-def scatter_groups(groups, first_route, second_route, near, far, both):
-    from_both = send(groups[both], first_route)
-    from_far = send(groups[far], first_route)
-    passed = add(groups[near], from_both).astype(BF16)
-    return add(groups[0], from_far, send(passed, second_route)).astype(BF16)
-
-
-def scatter_z(block):
-    rows = block.shape[0] // 4
-    part = [block[i * rows : (i + 1) * rows] for i in range(4)]
-    return add(part[0], send(part[1], Z1), send(part[2], Z2), send(part[3], Z3))
-
-
-def scatter_sum(outs):
-    first = scatter_groups(outs[:4], Y, X, 1, 2, 3)
-    second = scatter_groups(outs[4:], X, Y, 2, 1, 3)
-    return (scatter_z(first), scatter_z(second))
+def first_hop(terms):
+    return (terms[0], send(terms[1], Y), terms[2], send(terms[3], X))
+
+
+def halves_of(g, near, rows):
+    return jnp.concatenate(
+        [g[192 * near : 192 * near + 192]] + ([g[384 + 32 * near : 416 + 32 * near]] if rows > 48 else [])
+    )
+
+
+def near_terms(hop, rows):
+    return tuple(
+        add(halves_of(hop[i], 1, rows), halves_of(hop[i + 1], 1, rows)).astype(BF16) for i in (0, 2)
+    )
+
+
+def hop_terms(low):
+    return (send(low[0], X), send(low[1], Y))
+
+
+def far_terms(hop, got, rows):
+    return tuple(
+        add(halves_of(hop[i], 0, rows), halves_of(hop[i + 1], 0, rows), got[i // 2]).astype(BF16) for i in (0, 2)
+    )
+
+
+def along_line(blocks):
+    return (blocks[0], send(blocks[1], Z1), send(blocks[2], Z2), send(blocks[3], Z3))
+
+
+def line_parts(halves, rows):
+    return along_line(
+        [
+            jnp.concatenate(
+                [
+                    jnp.concatenate(
+                        [h[48 * z : 48 * z + 48]] + ([h[192 + 8 * z : 200 + 8 * z]] if rows > 48 else []), axis=0
+                    )
+                    for h in halves
+                ],
+                axis=1,
+            )
+            for z in range(4)
+        ]
+    )
+
+
+def block_parts(block):
+    return along_line([block[48 * z : 48 * z + 48] for z in range(4)])
 
 
 def flip(values, axis, index, bits):
@@ -811,129 +979,127 @@
     me, core = my_chip(), my_core()
     even = core == 0
 
-    four = jnp.stack([w_query, w_key, w_value, w_output], axis=1).astype(BF16).reshape(24, 4, 2, 384)
-    mine, theirs = (
-        jnp.where(even, four[:, :, 0], four[:, :, 1]).reshape(24, 1536),
-        jnp.where(even, four[:, :, 1], four[:, :, 0]).reshape(24, 1536),
-    )
-    got = send(theirs, CORE)
-    square = jnp.where(even, jnp.concatenate([mine, got], 0), jnp.concatenate([got, mine], 0))
+    def in_order(mine, got, axis):
+        return jnp.where(even, jnp.concatenate([mine, got], axis), jnp.concatenate([got, mine], axis))
+
+    lanes = [b_query, b_value, b_output, gain_first, shift_first, b_outer, gain_second, shift_second, b_inner]
+    mine, theirs, outer_rows = call(
+        prepare_kernel, [((32, 1536), BF16), ((32, 1536), BF16), ((48, 1536), BF16)], 14
+    )(w_query, w_key, w_value, w_output, *(v.reshape(1, -1) for v in lanes), w_outer)
+    (square,) = call(chip_rows_kernel, [((56, 1536), BF16)], 2)(mine, send(theirs, CORE))
     wide = w_inner.astype(BF16).reshape(24, CHIPS, 2, 96)
     mine, theirs = (
         jnp.where(even, wide[:, :, 0], wide[:, :, 1]).reshape(24, 1536),
         jnp.where(even, wide[:, :, 1], wide[:, :, 0]).reshape(24, 1536),
     )
-    got = send(theirs, CORE)
-    inner_rows = jnp.where(even, jnp.concatenate([mine, got], 0), jnp.concatenate([got, mine], 0))
-    outer_rows = w_outer.astype(BF16)
-
-    own_vec = jnp.concatenate(
-        [b_query, b_value, b_output, gain_first, shift_first, b_outer, gain_second, shift_second, b_inner]
-    ).astype(BF16)
-    spot = (jnp.arange(CHIPS)[:, None, None] == me) & (jnp.arange(2)[None, :, None] == core)
-    vecs = jnp.where(spot, own_vec[None, None, :], jnp.zeros((), BF16))
-    for route in (CORE, Z1, Z2, X, Y):
-        vecs = vecs + send(vecs, route)
-    vecs = vecs.astype(F32)
-    vec8 = vecs[:, :, :192].reshape(CHIPS, 2, 8, 24).transpose(2, 0, 1, 3).reshape(8, 768)
-    b1 = jnp.where(even, vecs[:, 0, 192:], vecs[:, 1, 192:]).reshape(1, 1536)
-    bq = jnp.where(even, vec8[0:1, :384], vec8[0:1, 384:])
-    bv = jnp.where(even, vec8[1:2, :384], vec8[1:2, 384:])
-
+    inner_rows = in_order(mine, send(theirs, CORE), 0)
     tokens, cot = inputs[:, 0], cotangent[:, 0]
-    square_a, square_d = gather_z(square)
-    tokens_z = after(tokens, square_a)
-    near = [tokens, send(tokens_z, Z1), send(tokens_z, Z2), send(tokens_z, Z3_INNER)]
-    slots = []
-    for part in near:
-        slots += [part, send(part, CORE)]
-    other_cot = send(cot, CORE)
-    square_a, square_d = gather_xy(square_a, square_d)
-    inner_a, inner_d = gather_z(after(inner_rows, near[1], near[2], near[3]))
-    inner_a, inner_d = gather_xy(after(inner_a, *square_a), after(inner_d, *square_d))
-    outer_a, outer_d = gather_z(after(outer_rows, near[1], near[2], near[3]))
-    outer_a, outer_d = gather_xy(after(outer_a, *inner_a), after(outer_d, *inner_d))
-
     segs = segments[:, 0]
     segs = flip(segs.reshape(2, 8, BAND), 1, seq, 3)
     kseg = segs.reshape(2, 8 * BAND, 1)
     qseg = segs[:, :2].reshape(2, 1, 2 * BAND)
 
+    other_tokens = send(tokens, CORE)
+    hidden_rows = jnp.concatenate([inner_rows, outer_rows], axis=1)
+    square, hidden_rows, other_tokens = after_both((square, hidden_rows, other_tokens), ())
+    square = across(line(square), 56)
+    hidden_rows, square = after_both((hidden_rows, square), ())
+    hidden = line(hidden_rows)
+    got = (send(square[0], X), send(square[1], Y))
+    got, square = after_both((got, square), hidden[1:2])
+    square = far_hop(*(jnp.concatenate(pair, axis=0) for pair in zip(square, got)))
+    hidden, tokens = after_both((hidden, tokens), square)
+    hidden = lax.all_gather(jnp.concatenate(hidden, axis=0), "dp", axis=0, tiled=True)
+    beside, opposite = send(tokens, Z1), send(tokens, MIDDLE)
+    square, beside, opposite = after_both((square, beside, opposite), ())
+    outside = (seq // 2 == 0) | (seq // 2 == 3)
+    second = jnp.where(outside, send(opposite, OUTWARD), send(beside, MIDDLE))
+    theirs = send(jnp.stack([beside, second, opposite]), CORE)
+    slots = [tokens, other_tokens, beside, second, opposite, theirs]
+
+    places = jnp.arange(CHIPS)
+    order = ((places[:, None] ^ me) == places[None, :]).astype(BF16)
+    vecs = []
+    for half, turn in ((square[:2], (0, 1, 2, 3)), (square[2:], (0, 2, 1, 3))):
+        rows = [g[224 * near + 192 : 224 * near + 224].reshape(4, 8, 768)[:, :2] for g in half for near in (0, 1)]
+        vecs.append(jnp.concatenate([rows[i] for i in turn], axis=0))
+    vecs = jnp.concatenate(vecs, axis=2).reshape(CHIPS, 2 * 1536)
+    vecs = dot_nn(order, vecs).reshape(CHIPS, 2, 12, 128)
+    vec8 = vecs[:, :, :8, :24].transpose(2, 0, 1, 3).reshape(8, 768)
+    b1 = jnp.where(even, vecs[:, 0, 8, :96], vecs[:, 1, 8, :96]).reshape(1, 1536)
+    bq = jnp.where(even, vec8[0:1, :384], vec8[0:1, 384:])
+    bv = jnp.where(even, vec8[1:2, :384], vec8[1:2, 384:])
+
     slot_shape, head_shape = (2, BAND, 768), (2, BAND, 384)
     q, k, v, w_abs, x_all = call(
         project_kernel,
         [((2, *head_shape), BF16), ((8, *head_shape), BF16), ((8, *head_shape), BF16), ((768, 1536), BF16), ((8, *slot_shape), BF16)],
-        18,
-        in_specs=[IN_PLACE] * 16 + [IN_VMEM] * 2,
+        12,
+        in_specs=[IN_PLACE] * 10 + [IN_VMEM] * 2,
         scratch=[pltpu.SemaphoreType.DMA((40,))],
         cost=(2_800_000_000, 16_000_000),
-    )(*slots, *square_a, *square_d, bq, bv)
-
+    )(*slots, *square, bq, bv)
     wo_half = w_abs[:, 1152:]
     wo_mine = jnp.where(even, wo_half[:384], wo_half[384:])
     wo_got = send(jnp.where(even, wo_half[384:], wo_half[:384]), CORE)
-    wo = jnp.where(even, jnp.concatenate([wo_mine, wo_got], 1), jnp.concatenate([wo_got, wo_mine], 1))
-
-    q_spec = pl.BlockSpec((2, 1, BAND, 384), lambda m: (0, m, 0, 0))
-    k_spec = pl.BlockSpec((8, 1, BAND, 384), lambda m: (0, m, 0, 0))
-    seg_specs = [
-        pl.BlockSpec((1, 8 * BAND, 1), lambda m: (m, 0, 0)),
-        pl.BlockSpec((1, 1, 2 * BAND), lambda m: (m, 0, 0)),
-    ]
-    t_spec = pl.BlockSpec((1, 384, 2 * BAND), lambda m: (m, 0, 0))
-    lse_spec = pl.BlockSpec((1, 8, 2 * BAND), lambda m: (m, 0, 0))
+    wo = in_order(wo_mine, wo_got, 1)
+
+    def attention_specs(m=None):
+        micro = (lambda i: i) if m is None else (lambda i: m)
+        q_spec = pl.BlockSpec((2, 1, BAND, 384), lambda i: (0, micro(i), 0, 0))
+        k_spec = pl.BlockSpec((8, 1, BAND, 384), lambda i: (0, micro(i), 0, 0))
+        t_spec = pl.BlockSpec((1, 384, 2 * BAND), lambda i: (micro(i), 0, 0))
+        lse_spec = pl.BlockSpec((1, 8, 2 * BAND), lambda i: (micro(i), 0, 0))
+        segs = [
+            pl.BlockSpec((1, 8 * BAND, 1), lambda i: (micro(i), 0, 0)),
+            pl.BlockSpec((1, 1, 2 * BAND), lambda i: (micro(i), 0, 0)),
+        ]
+        return ([q_spec, k_spec, k_spec], [t_spec, t_spec, lse_spec], segs)
+
+    qkv_specs, mix_specs, seg_specs = attention_specs()
+    other_cot = send(after(cot, q), CORE)
+
     mix, mix_low, lse = call(
         attend_kernel,
         [((2, 384, 256), F32), ((2, 384, 256), BF16), ((2, 8, 256), F32)],
         5,
         grid=(2,),
-        in_specs=[q_spec, k_spec, k_spec, *seg_specs],
-        out_specs=[t_spec, t_spec, lse_spec],
+        in_specs=qkv_specs + seg_specs,
+        out_specs=mix_specs,
         cost=(1_600_000_000, 8_000_000),
     )(q, k, v, kseg, qseg)
-    mix_other = send(mix_low, CORE)
-
     branch = [dot_tn(mix_low[m], wo).astype(BF16).reshape(2, 1, BAND, 768) for m in range(2)]
-    branch = jnp.concatenate(branch, axis=1).reshape(2, 2 * BAND, 768)
-    branch = branch.reshape(4 * BAND, 768)
+    branch = jnp.concatenate(branch, axis=1).reshape(4 * BAND, 768)
     branch_other = send(branch, CORE)
     n1, r1, hid_low, act, slope, f_own, w1, w2 = call(
         forward_kernel,
         [((512, 768), F32), ((512, 1), F32), ((512, 768), BF16), ((512, 1536), BF16), ((512, 1536), BF16), ((512, 768), BF16), ((768, 1536), BF16), ((1536, 768), BF16)],
-        21,
-        in_specs=[IN_PLACE] + [IN_VMEM] * 4 + [IN_PLACE] * 16,
-        scratch=[pltpu.VMEM((2, *slot_shape), BF16), pltpu.SemaphoreType.DMA((65,))],
+        6,
+        in_specs=[IN_PLACE] + [IN_VMEM] * 4 + [IN_PLACE],
+        scratch=[pltpu.VMEM((2, *slot_shape), BF16), pltpu.SemaphoreType.DMA((49,))],
         cost=(2_500_000_000, 16_000_000),
-    )(x_all, branch, branch_other, vec8, b1, *inner_a, *inner_d, *outer_a, *outer_d)
-
-    result, df, dz2, du, dh_own, sums2, db1 = call(
+    )(x_all, branch, branch_other, vec8, b1, hidden)
+    mix_other = send(after(mix_low, n1), CORE)
+    result, df, dz2, sums2 = call(
         middle_kernel,
-        [((256, 768), BF16), ((512, 768), BF16), ((512, 768), F32), ((512, 1536), BF16), ((512, 768), BF16), ((8, 768), F32), ((1, 1536), F32)],
-        9,
-        cost=(2_500_000_000, 16_000_000),
-    )(n1, f_own, send(f_own, CORE), cot.reshape(256, 768), other_cot.reshape(256, 768), vec8, slope, w1, w2)
+        [((256, 768), BF16), ((512, 768), BF16), ((512, 768), F32), ((8, 768), F32)],
+        6,
+        cost=(50_000_000, 8_000_000),
+    )(n1, f_own, send(f_own, CORE), cot.reshape(256, 768), other_cot.reshape(256, 768), vec8)
+
+    piece = [pltpu.VMEM((2, 384, 768), BF16)] * 2
+    (outer_terms,) = call(outer_grad_kernel, [((768, 1536), BF16)], 2, cost=(1_200_000_000, 6_000_000))(act, df)
+    outer_block = lax.psum_scatter(outer_terms, "dp", scatter_dimension=0, tiled=True)
+    du, dh_own, db1 = call(
+        hidden_kernel,
+        [((512, 1536), BF16), ((512, 768), BF16), ((1, 1536), F32)],
+        4,
+        cost=(2_400_000_000, 9_000_000),
+    )(after(df, outer_terms), slope, w1, w2)
     dh_other = send(dh_own, CORE)
-
-    piece = [pltpu.SemaphoreType.DMA((8,))]
-    outer_terms = call(
-        outer_grad_kernel,
-        [((384, 384), BF16)] * 8,
-        2,
-        out_specs=[IN_PLACE] * 8,
-        scratch=[pltpu.VMEM((1536, 768), BF16)] + piece,
-        cost=(1_200_000_000, 6_000_000),
-    )(act, df)
-    outer_sum_a, outer_sum_d = scatter_sum(outer_terms)
-    inner_terms = call(
-        inner_grad_kernel,
-        [((192, 768), BF16)] * 8,
-        2,
-        out_specs=[IN_PLACE] * 8,
-        scratch=[pltpu.VMEM((768, 1536), BF16)] + piece,
-        cost=(1_200_000_000, 6_000_000),
-    )(hid_low, du)
-    inner_sum_a, inner_sum_d = scatter_sum(inner_terms)
-
+    (inner_terms,) = call(inner_grad_kernel, [((768, 1536), BF16)], 2, cost=(1_200_000_000, 6_000_000))(hid_low, du)
+    inner_block = lax.psum_scatter(inner_terms, "dp", scatter_dimension=0, tiled=True)
+    dh_own = after(dh_own, inner_terms)
     dz1, do, do_half, da, sums1 = call(
         first_kernel,
         [((256, 768), F32), ((512, 768), BF16), ((512, 384), BF16), ((2, 384, 256), BF16), ((8, 768), F32)],
@@ -941,80 +1107,94 @@
         cost=(300_000_000, 10_000_000),
     )(dz2, dh_own, dh_other, n1, r1, vec8, wo)
 
-    dq, dk, dv = call(
-        attend_back_kernel,
-        [((2, *head_shape), BF16), ((8, *head_shape), BF16), ((8, *head_shape), BF16)],
-        8,
-        grid=(2,),
-        in_specs=[q_spec, k_spec, k_spec, t_spec, t_spec, lse_spec, *seg_specs],
-        out_specs=[q_spec, k_spec, k_spec],
-        cost=(4_000_000_000, 12_000_000),
-    )(q, k, v, mix, da, lse, kseg, qseg)
-
-    by_z = pl.BlockSpec((1, *slot_shape), lambda z: (z, 0, 0, 0))
-    heads_by_z = pl.BlockSpec((2, *head_shape), lambda z: (z, 0, 0, 0))
-    dx_own, dx_send = call(
-        token_grad_kernel,
-        [((4, *slot_shape), BF16)] * 2,
-        4,
-        grid=(4,),
-        in_specs=[pl.BlockSpec((2, *head_shape), lambda z: (0, 0, 0, 0)), heads_by_z, heads_by_z, pl.BlockSpec((768, 1536), lambda z: (0, 0))],
-        out_specs=[by_z, by_z],
-        cost=(2_700_000_000, 10_000_000),
-    )(dq, dk, dv, w_abs)
-    dx_got = send(dx_send, CORE)
-    dx = [add(dx_own[z], dx_got[z]) for z in range(4)]
-    low_dx = [d.astype(BF16) for d in dx]
-    grad_tokens = add(
-        dx[0], dz1.reshape(slot_shape), send(low_dx[1], Z1), send(low_dx[2], Z2), send(low_dx[3], Z3_INNER)
-    ).astype(BF16)
-
-    mix_full = [
-        jnp.where(even, jnp.concatenate([mix_low[m], jnp.roll(mix_other[m], BAND, 1)], 0), jnp.concatenate([jnp.roll(mix_other[m], BAND, 1), mix_low[m]], 0))
-        for m in range(2)
-    ]
-    *square_terms, sums0 = call(
+    def back(m, events):
+        specs = attention_specs(m)
+        return call(
+            attend_back_kernel,
+            [((2, BAND, 384), BF16), ((8, BAND, 384), BF16), ((8, BAND, 384), BF16)],
+            8,
+            grid=(1,),
+            in_specs=specs[0] + specs[1] + specs[2],
+            out_specs=[pl.BlockSpec((n, BAND, 384), lambda i: (0, 0, 0)) for n in (2, 8, 8)],
+            cost=(2_000_000_000, 6_000_000),
+        )(q, k, v, mix, after(da, *events), lse, kseg, qseg)
+
+    def token_grads(grads, events):
+        own, away = call(
+            token_grad_kernel, [((4, BAND, 768), BF16)] * 2, 4, cost=(1_350_000_000, 5_000_000)
+        )(*after_both(grads, events), w_abs)
+        return (own, away, send(away, CORE))
+
+    def core_sums(own, got):
+        return [add(own[z], got[z]) if z == 0 else add(own[z], got[z]).astype(BF16) for z in range(4)]
+
+    def line_sums(sums):
+        return (sums[0], send(sums[1], Z1), send(sums[2], Z2), send(sums[3], MIDDLE))
+
+    grads0 = back(0, ())
+    dx0, _, got0 = token_grads(grads0, ())
+    grads1 = back(1, (dx0, outer_block))
+    outer_parts = after_both(block_parts(outer_block), grads1[:1])
+    low0 = core_sums(dx0, after(got0, grads1[0]))
+    grads1, _ = lax.optimization_barrier((grads1, (outer_parts, low0)))
+    sent0 = line_sums(low0)
+
+    def widen(value):
+        zero = jnp.zeros_like(value)
+        return in_order(value, zero, 1)
+
+    def column(index):
+        return sum(jnp.sum(g[index].astype(F32), axis=(0, 1)) for g in (grads0, grads1))[None]
+
+    eight = jnp.concatenate(
+        [widen(column(0)), widen(column(2)), sums1[2:3], sums1[0:1], sums1[1:2], sums2[2:3], sums2[0:1], sums2[1:2]], 0
+    )
+    eight = jnp.pad(eight.reshape(8, CHIPS, 2, 24), ((0, 0), (0, 0), (0, 0), (0, 104))).transpose(1, 2, 0, 3)
+    db1 = jnp.where(jnp.arange(2)[None, :, None] == core, db1.reshape(CHIPS, 1, 96), 0.0)
+    db1 = jnp.pad(db1, ((0, 0), (0, 0), (0, 416)))
+    vec_grads = jnp.concatenate([eight.reshape(CHIPS, 2, 1024), db1], axis=2).reshape(CHIPS, 3072)
+    vec_grads = dot_nn(order, vec_grads.astype(BF16)).astype(BF16).reshape(2, 2, 4, 2, 1536)
+    vec_grads = jnp.pad(vec_grads, ((0, 0), (0, 0), (0, 0), (0, 6), (0, 0)))
+    vec_first = vec_grads[..., :768].reshape(2, 64, 768)
+    vec_second = vec_grads[..., 768:].transpose(1, 0, 2, 3, 4).reshape(2, 64, 768)
+    square_terms = call(
         projection_grad_kernel,
-        [((192, 768), BF16)] * 8 + [((8, 384), F32)],
-        7,
-        out_specs=[IN_PLACE] * 8 + [IN_VMEM],
-        scratch=[pltpu.VMEM((768, 1536), BF16)] + piece,
+        [((448, 768), BF16)] * 4,
+        12,
+        out_specs=[IN_PLACE] * 4,
+        scratch=piece + [pltpu.VMEM((768, 384), BF16), pltpu.SemaphoreType.DMA((8,))],
         cost=(3_300_000_000, 12_000_000),
-    )(x_all, dq, dk, dv, mix_full[0], mix_full[1], do_half)
-    square_sum_a, square_sum_d = scatter_sum(square_terms)
-
-    zero = jnp.zeros((1, 384), F32)
-    bq_g, bv_g = (
-        jnp.where(even, jnp.concatenate([sums0[i : i + 1], zero], 1), jnp.concatenate([zero, sums0[i : i + 1]], 1))
-        for i in (0, 1)
-    )
-    eight = jnp.concatenate(
-        [bq_g, bv_g, sums1[2:3], sums1[0:1], sums1[1:2], sums2[2:3], sums2[0:1], sums2[1:2]], 0
-    )
-    eight = eight.reshape(8, CHIPS, 2, 24).transpose(1, 2, 0, 3).reshape(CHIPS, 2, 192)
-    db1 = db1.reshape(CHIPS, 1, 96)
-    db1 = jnp.where(jnp.arange(2)[None, :, None] == core, db1, 0.0)
-    vec_grads = jnp.concatenate([eight, db1], axis=2)
-    for route in (CORE, Z1, Z2, X, Y):
-        vec_grads = vec_grads + send(vec_grads, route)
-    own = jnp.sum(jnp.where(spot, vec_grads, 0.0), axis=(0, 1))
-
-    def to_owner(first, second):
-        value = jnp.concatenate([first, second], axis=1)
-        keep = jnp.where(even, value[:24], value[24:])
-        other = jnp.where(even, value[24:], value[:24]).astype(BF16)
-        return (keep, send(other, CORE).astype(F32))
-
-    keep, got = (v.reshape(24, 4, 384) for v in to_owner(square_sum_a, square_sum_d))
-    squares = jnp.where(even, jnp.concatenate([keep, got], 2), jnp.concatenate([got, keep], 2))
-    keep, got = (v.reshape(24, CHIPS, 1, 96) for v in to_owner(inner_sum_a, inner_sum_d))
-    grad_inner = jnp.where(even, jnp.concatenate([keep, got], 2), jnp.concatenate([got, keep], 2)).reshape(24, 3072)
-    grad_outer = jnp.concatenate([outer_sum_a, outer_sum_d], axis=1)
-    small = [own[24 * i : 24 * i + 24] for i in range(8)]
+    )(x_all, grads0[0], grads1[0], grads0[1], grads1[1], grads0[2], grads1[2], mix_low[0], mix_low[1], mix_other, do_half, jnp.concatenate([vec_first, vec_second]))
+    square_hop = first_hop(square_terms)
+    dx1, _, got1 = token_grads(grads1, square_terms[:1])
+    inner_block, sent0 = after_both((inner_block, sent0), (dx1,))
+    inner_parts = block_parts(inner_block)
+    square_hop, inner_parts, got1 = after_both((square_hop, inner_parts, got1), (dx1,))
+    square_sent = hop_terms(near_terms(square_hop, 56))
+    sent1 = line_sums(core_sums(dx1, got1))
+    square_sent, sent1, square_hop = after_both((square_sent, sent1, square_hop), ())
+    square_half = far_terms(square_hop, square_sent, 56)
+    square_parts = line_parts(square_half, 56)
+
+    outer_total = add(*outer_parts)
+    inner_total = add(*inner_parts)
+    grad_outer = jnp.concatenate([outer_total[:, :768], outer_total[:, 768:]], axis=0)
+    keep = jnp.where(even, inner_total[:24], inner_total[24:])
+    got = send(jnp.where(even, inner_total[24:], inner_total[:24]).astype(BF16), CORE).astype(F32)
+    grad_inner = in_order(keep.reshape(24, CHIPS, 1, 96), got.reshape(24, CHIPS, 1, 96), 2).reshape(24, 3072)
+    keep, other = call(owner_kernel, [((32, 1536), F32), ((32, 1536), BF16)], 5)(*square_half, *square_parts[1:])
+    grads = call(
+        result_kernel,
+        [((24, 768), F32)] * 4 + [((1, 24), F32)] * 8 + [((1, 96), F32)],
+        2,
+    )(keep, send(other, CORE))
+    squares, small = grads[:4], [g.reshape(-1) for g in grads[4:]]
+    dz1 = dz1.reshape(slot_shape)
+    grad_tokens = jnp.stack([add(dz1[m], *sent).astype(BF16) for m, sent in enumerate((sent0, sent1))])
     return (
         result.reshape(2, 1, BAND, 768), grad_tokens[:, None],
-        squares[:, 0], small[0], squares[:, 1], squares[:, 2], small[1], squares[:, 3], small[2],
-        small[3], small[4], grad_inner, own[192:], grad_outer, small[5], small[6], small[7],
+        squares[0], small[0], squares[1], squares[2], small[1], squares[3], small[2],
+        small[3], small[4], grad_inner, small[8], grad_outer, small[5], small[6], small[7],
     )
 
 

time: 398 us -> 319 us (0.80); the launches traced: 391 us -> 317 us
  waiting for transfers between devices: 153 us -> 84.4 us
  starting transfers between devices: 104 us -> 57.9 us
  Pallas kernels: 93.5 us -> 110 us
  between operations: 2.39 us -> 15.1 us
  local copies, waits for them, and re-layouts: 18.9 us -> 25.1 us
  other arithmetic: 17.1 us -> 22.5 us
    ppermute x94 -> x47, waiting for transfers between devices: 153 us -> 82.7 us  [send(): return lax.ppermute(value, BOTH, route)]
    ppermute x94 -> x47, starting transfers between devices: 104 us -> 57.6 us  [send(): return lax.ppermute(value, BOTH, route)]
    pallas_call x5 -> x12, Pallas kernels: 41.2 us -> 62.8 us  [the longest x2 15.6 us: back(): call(attend_back_kernel, [((2, BAND, 384), BF16), ((8, BAND, 384), BF16),...]
    pallas_call x1, Pallas kernels: 11.7 us -> 5.13 us  [per_device_paired(): call(middle_kernel, [((256, 768), BF16), ((512, 768), BF16), ((512, 768),...]
    unnamed x140 -> x126, local copies, waits for them, and re-layouts: 5.58 us -> 11.5 us
    convert_element_type x17 -> x7, other arithmetic: 1.48 us -> 7.21 us  [the longest x2 4.3 us: core_sums(): add(own[z], got[z]).astype(BF16)]
    select_n x14 -> x6, other arithmetic: 4.41 us -> 0.26 us  [the longest x3 0.2 us: in_order(): jnp.where(even, jnp.concatenate([mine, got], axis), jnp.concatenate([got,...]
  transfers between devices with their start and end apart: 94 -> 50, of which waited for: 41 -> 18; matrix products, arithmetic and copies ran while one was open for 7% -> 11% of each run, Pallas kernels for 20% -> 26%
where the time goes in v2:
time: 319 us; the launch traced here: 317 us
  Pallas kernels  110 us (34%)
  waiting for transfers between devices  84.4 us (26%)
  starting transfers between devices  57.9 us (18%)
  local copies, waits for them, and re-layouts  25.1 us (8%)
  other arithmetic  22.5 us (7%)
  between operations  15.1 us (5%)
    ppermute x47, waiting for transfers between devices, send(): return lax.ppermute(value, BOTH, route)  82.7 us
    ppermute x47, starting transfers between devices, send(): return lax.ppermute(value, BOTH, route)  57.6 us
    pallas_call x2, Pallas kernels, back(): call(attend_back_kernel, [((2, BAND, 384), BF16), ((8, BAND, 384), BF16),...  15.6 us
    pallas_call x1, Pallas kernels, per_device_paired(): call(forward_kernel, [((512, 768), F32), ((512, 1), F32), ((512, 768), BF...  12.5 us
    pallas_call x1, Pallas kernels, per_device_paired(): call(project_kernel, [((2, *head_shape), BF16), ((8, *head_shape), BF16),...  12.1 us
    pallas_call x1, Pallas kernels, per_device_paired(): call(attend_kernel, [((2, 384, 256), F32), ((2, 384, 256), BF16), ((2, 8,...  12 us
    pallas_call x2, Pallas kernels, token_grads(): call(token_grad_kernel, [((4, BAND, 768), BF16)] * 2, 4, cost=(1350000000...  11.9 us
    unnamed x126, local copies, waits for them, and re-layouts  11.5 us
  transfers between devices with their start and end apart: 50, of which 18 were waited for; matrix products, arithmetic and copies ran while one was open for 11% of the time, Pallas kernels for 26%

profile of v2, /device:TPU:0, one launch (start us, length us, event | category | flops | bytes accessed | tf_op | source)
XLA Modules:
  0.0 317.4 jit_solution(1753204001185750515)
XLA Ops:
  21.6 4.9 %collective-permute-done.3 = bf16[56,1536]{1,0:T(8,128)(2,1)S(1)} collective-permute-done((bf16[56,1536]{1,0:T(8,128)(2,1)}, bf16[56,1536]{1,0:T(8,128)(2,1)S(1)}, u32[]{:S(2)}, u32[]{:S(2)}) %collective-permute-start.3) | collective-permute-done | bytes 172064 | tf_op jit(solution)/shard_map/ppermute | solution.py:392
  26.5 7.3 %collective-permute-done.4 = bf16[56,1536]{1,0:T(8,128)(2,1)S(1)} collective-permute-done((bf16[56,1536]{1,0:T(8,128)(2,1)}, bf16[56,1536]{1,0:T(8,128)(2,1)S(1)}, u32[]{:S(2)}, u32[]{:S(2)}) %collective-permute-start.4) | collective-permute-done | bytes 172064 | tf_op jit(solution)/shard_map/ppermute | solution.py:392
  41.1 6.0 %collective-permute-done.6 = bf16[48,3072]{1,0:T(8,128)(2,1)S(1)} collective-permute-done((bf16[48,3072]{1,0:T(8,128)(2,1)S(1)}, bf16[48,3072]{1,0:T(8,128)(2,1)S(1)}, u32[]{:S(2)}, u32[]{:S(2)}) %collective-permute-start.6) | collective-permute-done | bytes 294944 | tf_op jit(solution)/shard_map/ppermute | solution.py:392
  48.4 3.5 %collective-permute-start.7 = (bf16[48,3072]{1,0:T(8,128)(2,1)S(1)}, bf16[48,3072]{1,0:T(8,128)(2,1)S(1)}, u32[]{:S(2)}, u32[]{:S(2)}) collective-permute-start(bf16[48,3072]{1,0:T(8,128)(2,1)S(1)} %pad_maximum_fusion.4), channel_id=1, source_target_pairs={{0,4},{1,5},{2,6},{3,7},{4,0},{5,1},{6,2},{7,3},{8,12},{9,13},{10,... | collective-permute-start | bytes 884744 | tf_op jit(solution)/shard_map/ppermute | solution.py:392
  53.3 17.3 %collective-permute-done.7 = bf16[48,3072]{1,0:T(8,128)(2,1)S(1)} collective-permute-done((bf16[48,3072]{1,0:T(8,128)(2,1)S(1)}, bf16[48,3072]{1,0:T(8,128)(2,1)S(1)}, u32[]{:S(2)}, u32[]{:S(2)}) %collective-permute-start.7) | collective-permute-done | bytes 294944 | tf_op jit(solution)/shard_map/ppermute | solution.py:392
  74.8 5.6 %collective-permute-start.13 = (bf16[2,128,768]{2,1,0:T(8,128)(2,1)}, bf16[2,128,768]{2,1,0:T(8,128)(2,1)S(1)}, u32[]{:S(2)}, u32[]{:S(2)}) collective-permute-start(bf16[2,128,768]{2,1,0:T(8,128)(2,1)} %bitcast.187), channel_id=1, source_target_pairs={{0,2},{1,3},{2,0},{3,1},{4,6},{5,7},{6,4},{7,5},{8,10},{9,11},{10,... | collective-permute-start | bytes 1179656 | tf_op jit(solution)/shard_map/ppermute | solution.py:392
  83.7 5.1 %collective-permute-done.13.refs_2_ = bf16[2,128,768]{2,1,0:T(8,128)(2,1)S(1)} collective-permute-done((bf16[2,128,768]{2,1,0:T(8,128)(2,1)}, bf16[2,128,768]{2,1,0:T(8,128)(2,1)S(1)}, u32[]{:S(2)}, u32[]{:S(2)}) %collective-permute-start.13) | collective-permute-done | bytes 393248 | tf_op jit(solution)/shard_map/ppermute | solution.py:392
  92.6 8.4 %collective-permute-done.15 = bf16[2,128,768]{2,1,0:T(8,128)(2,1)S(1)} collective-permute-done((bf16[2,128,768]{2,1,0:T(8,128)(2,1)S(1)}, bf16[2,128,768]{2,1,0:T(8,128)(2,1)S(1)}, u32[]{:S(2)}, u32[]{:S(2)}) %collective-permute-start.15) | collective-permute-done | bytes 393248 | tf_op jit(solution)/shard_map/ppermute | solution.py:392
  104.4 12.1 %shard_map.307 = (bf16[2,2,128,384]{3,2,1,0:T(8,128)(2,1)}, bf16[8,2,128,384]{3,2,1,0:T(8,128)(2,1)}, bf16[8,2,128,384]{3,2,1,0:T(8,128)(2,1)}, bf16[768,1536]{1,0:T(8,128)(2,1)}, bf16[8,2,128,768]{3,2,1,0:T(8,128)(2,1)}) custom-call(bf16[2,128,768]{2,1,0:T(8,128)(2,1)} %bitcast.189, bf16[2,128,768]{2,1,0:T(8,128)(2,1)} %copy-done.57, ...), custom_call_target="tpu_custom_call" | custom-call | flops 2800000000 | bytes 16000000 | tf_op jit(solution)/shard_map/pallas_call | solution.py:1034
  119.4 12.0 %shard_map.308 = (f32[2,384,256]{2,1,0:T(8,128)}, bf16[2,384,256]{2,1,0:T(8,128)(2,1)}, f32[2,8,256]{2,1,0:T(8,128)}) custom-call(bf16[2,2,128,384]{3,2,1,0:T(8,128)(2,1)} %get-tuple-element.161.q_ref, bf16[8,2,128,384]{3,2,1,0:T(8,128)(2,1)} %get-tuple-element.162.k_ref, bf16[8,2,128,384]{3,2,1,0:T(8,128)(2,1)} %get-tuple-element.163.v_ref, ...), custom_call_target="tpu_custom_call" | custom-call | flops 1600000000 | bytes 8000000 | tf_op jit(solution)/shard_map/pallas_call | solution.py:1062
  136.9 12.5 %shard_map.309 = (f32[512,768]{1,0:T(8,128)}, f32[512,1]{1,0:T(8,128)}, bf16[512,768]{1,0:T(8,128)(2,1)}, bf16[512,1536]{1,0:T(8,128)(2,1)}, bf16[512,1536]{1,0:...) custom-call(bf16[8,2,128,768]{3,2,1,0:T(8,128)(2,1)} %get-tuple-element.160.refs_0_.x_, ...), custom_call_target="tpu_custom_call" | custom-call | flops 2500000000 | bytes 16000000 | tf_op jit(solution)/shard_map/pallas_call | solution.py:1074
  153.3 5.1 %shard_map.310 = (bf16[256,768]{1,0:T(8,128)(2,1)}, bf16[512,768]{1,0:T(8,128)(2,1)}, f32[512,768]{1,0:T(8,128)}, f32[8,768]{1,0:T(8,128)}) custom-call(f32[512,768]{1,0:T(8,128)} %get-tuple-element.170.n1_ref, bf16[512,768]{1,0:T(8,128)(2,1)} %get-tuple-element.171.own_ref, bf16[512,768]{1,0:T(8,128)(2,1)} %copy-done.16, bf16[256,768]{1,0:T(8,128)(2,1)} %bitcast.159, ...), custom_call_target="tpu_custom_call" | custom-call | flops 50000000 | bytes 8000000 | tf_op jit(solution)/shard_map/pallas_call | solution.py:1083
  158.4 5.1 %shard_map.311 = bf16[768,1536]{1,0:T(8,128)(2,1)} custom-call(bf16[512,1536]{1,0:T(8,128)(2,1)} %get-tuple-element.176.act_ref, bf16[512,768]{1,0:T(8,128)(2,1)} %get-tuple-element.177.df_ref), custom_call_target="tpu_custom_call" | custom-call | flops 1200000000 | bytes 6000000 | tf_op jit(solution)/shard_map/pallas_call | solution.py:1091
  163.9 8.4 %shard_map.312 = (bf16[512,1536]{1,0:T(8,128)(2,1)}, bf16[512,768]{1,0:T(8,128)(2,1)}, f32[1,1536]{1,0:T(1,128)}) custom-call(bf16[512,768]{1,0:T(8,128)(2,1)} %get-tuple-element.177.df_ref, bf16[512,1536]{1,0:T(8,128)(2,1)} %get-tuple-element.178.slope_ref, bf16[768,1536]{1,0:T(8,128)(2,1)} %get-tuple-element.179.w1_ref, ...), custom_call_target="tpu_custom_call" | custom-call | flops 2400000000 | bytes 9000000 | tf_op jit(solution)/shard_map/pallas_call | solution.py:1093
  172.3 4.7 %shard_map.313 = bf16[768,1536]{1,0:T(8,128)(2,1)} custom-call(bf16[512,768]{1,0:T(8,128)(2,1)} %get-tuple-element.182.low_ref, bf16[512,1536]{1,0:T(8,128)(2,1)} %get-tuple-element.183.du_ref), custom_call_target="tpu_custom_call" | custom-call | flops 1200000000 | bytes 6000000 | tf_op jit(solution)/shard_map/pallas_call | solution.py:1100
  181.3 5.5 %shard_map.314 = (f32[256,768]{1,0:T(8,128)}, bf16[512,768]{1,0:T(8,128)(2,1)}, bf16[512,384]{1,0:T(8,128)(2,1)}, bf16[2,384,256]{2,1,0:T(8,128)(2,1)}, f32[8,768]{1,0:T(8,128)}) custom-call(f32[512,768]{1,0:T(8,128)} %get-tuple-element.174.dz_ref, bf16[512,768]{1,0:T(8,128)(2,1)} %get-tuple-element.184.own_ref, bf16[512,768]{1,0:T(8,128)(2,1)} %copy-done.15, ...), custom_call_target="tpu_custom_call" | custom-call | flops 300000000 | bytes 10000000 | tf_op jit(solution)/shard_map/pallas_call | solution.py:1103
  186.8 7.8 %shard_map.315 = (bf16[2,128,384]{2,1,0:T(8,128)(2,1)}, bf16[8,128,384]{2,1,0:T(8,128)(2,1)}, bf16[8,128,384]{2,1,0:T(8,128)(2,1)}) custom-call(bf16[2,2,128,384]{3,2,1,0:T(8,128)(2,1)} %get-tuple-element.161.q_ref, bf16[8,2,128,384]{3,2,1,0:T(8,128)(2,1)} %get-tuple-element.162.k_ref, bf16[8,2,128,384]{3,2,1,0:T(8,128)(2,1)} %get-tuple-element.163.v_ref, ...), custom_call_target="tpu_custom_call" | custom-call | flops 2000000000 | bytes 6000000 | tf_op jit(solution)/shard_map/pallas_call | solution.py:1112
  194.6 5.9 %shard_map.316 = (bf16[4,128,768]{2,1,0:T(8,128)(2,1)}, bf16[4,128,768]{2,1,0:T(8,128)(2,1)}) custom-call(bf16[2,128,384]{2,1,0:T(8,128)(2,1)} %get-tuple-element.207.refs_0_, bf16[8,128,384]{2,1,0:T(8,128)(2,1)} %get-tuple-element.208.refs_2_, bf16[8,128,384]{2,1,0:T(8,128)(2,1)} %get-tuple-element.192.dv_ref, bf16[768,1536]{1,0:T(8,128)(2,1)} %get-tuple-element.165.w_ref), custom_call_target="tpu_custom_call" | custom-call | flops 1350000000 | bytes 5000000 | tf_op jit(solution)/shard_map/pallas_call | solution.py:1123
  209.0 7.8 %shard_map.317 = (bf16[2,128,384]{2,1,0:T(8,128)(2,1)}, bf16[8,128,384]{2,1,0:T(8,128)(2,1)}, bf16[8,128,384]{2,1,0:T(8,128)(2,1)}) custom-call(bf16[2,2,128,384]{3,2,1,0:T(8,128)(2,1)} %get-tuple-element.161.q_ref, bf16[8,2,128,384]{3,2,1,0:T(8,128)(2,1)} %get-tuple-element.162.k_ref, bf16[8,2,128,384]{3,2,1,0:T(8,128)(2,1)} %get-tuple-element.163.v_ref, ...), custom_call_target="tpu_custom_call" | custom-call | flops 2000000000 | bytes 6000000 | tf_op jit(solution)/shard_map/pallas_call | solution.py:1112
  226.4 9.6 %shard_map.318 = (bf16[448,768]{1,0:T(8,128)(2,1)}, bf16[448,768]{1,0:T(8,128)(2,1)}, bf16[448,768]{1,0:T(8,128)(2,1)}, bf16[448,768]{1,0:T(8,128)(2,1)}) custom-call(bf16[8,2,128,768]{3,2,1,0:T(8,128)(2,1)} %get-tuple-element.160.refs_0_.x_ref, bf16[2,128,384]{2,1,0:T(8,128)(2,1)} %get-tuple-element.207.refs_0_, ...), custom_call_target="tpu_custom_call" | custom-call | flops 3300000000 | bytes 12000000 | tf_op jit(solution)/shard_map/pallas_call | solution.py:1160
  236.1 6.0 %shard_map.319 = (bf16[4,128,768]{2,1,0:T(8,128)(2,1)}, bf16[4,128,768]{2,1,0:T(8,128)(2,1)}) custom-call(bf16[2,128,384]{2,1,0:T(8,128)(2,1)} %get-tuple-element.216.refs_1_.dq_ref, bf16[8,128,384]{2,1,0:T(8,128)(2,1)} %get-tuple-element.217.refs_3_.dk_ref, bf16[8,128,384]{2,1,0:T(8,128)(2,1)} %get-tuple-element.218.refs_5_.dv_ref, ...), custom_call_target="tpu_custom_call" | custom-call | flops 1350000000 | bytes 5000000 | tf_op jit(solution)/shard_map/pallas_call | solution.py:1123
  255.1 7.4 %collective-permute-done.34 = bf16[48,1536]{1,0:T(8,128)(2,1)S(1)} collective-permute-done((bf16[48,1536]{1,0:T(8,128)(2,1)S(1)}, bf16[48,1536]{1,0:T(8,128)(2,1)S(1)}, u32[]{:S(2)}, u32[]{:S(2)}) %collective-permute-start.34) | collective-permute-done | bytes 147488 | tf_op jit(solution)/shard_map/ppermute | solution.py:392
  277.9 4.3 %collective-permute-done.40 = bf16[128,768]{1,0:T(8,128)(2,1)} collective-permute-done((bf16[128,768]{1,0:T(8,128)(2,1)}, bf16[128,768]{1,0:T(8,128)(2,1)}, u32[]{:S(2)}, u32[]{:S(2)}) %collective-permute-start.40) | collective-permute-done | bytes 196640 | tf_op jit(solution)/shard_map/ppermute | solution.py:392
  294.7 8.8 %collective-permute-done.43.refs_1_ = bf16[56,1536]{1,0:T(8,128)(2,1)S(1)} collective-permute-done((bf16[56,1536]{1,0:T(8,128)(2,1)S(1)}, bf16[56,1536]{1,0:T(8,128)(2,1)S(1)}, u32[]{:S(2)}, u32[]{:S(2)}) %collective-permute-start.43) | collective-permute-done | bytes 172064 | tf_op jit(solution)/shard_map/ppermute | solution.py:392
  (360 shorter events, 121.2 us)
Async XLA Ops:
  7.2 128.8 %all-gather.2.cloned.1.call-start = ((), (), s32[]{:S(2)}) async-start(), calls=%async_computation.2 | async-start | bytes 5898240 | tf_op jit(solution)/shard_map/all_gather | solution.py:1012
  18.0 15.7 %collective-permute-start.4 = (bf16[56,1536]{1,0:T(8,128)(2,1)}, bf16[56,1536]{1,0:T(8,128)(2,1)S(1)}, u32[]{:S(2)}, u32[]{:S(2)}) collective-permute-start(bf16[56,1536]{1,0:T(8,128)(2,1)} %shard_map.306), channel_id=1, source_target_pairs={{0,4},{1,5},{2,6},{3,7},{4,0},{5,1},{6,2},{7,3},{8,12},{9,13},{10,... | collective-permute-start | bytes 516104 | tf_op jit(solution)/shard_map/ppermute | solution.py:392
  47.2 23.5 %collective-permute-start.12 = (bf16[448,768]{1,0:T(8,128)(2,1)S(1)}, bf16[448,768]{1,0:T(8,128)(2,1)S(1)}, u32[]{:S(2)}, u32[]{:S(2)}) collective-permute-start(bf16[448,768]{1,0:T(8,128)(2,1)S(1)} %constant_dynamic-update-slice_fusion.10.refs_8_), channel_id=1, source_target_pairs={{0,8},{1,9},{2,10},{3,11},{4,12},{5,13},{6,14},{7,15},{8,0},{9,1},... | collective-permute-start | bytes 2064392 | tf_op jit(solution)/shard_map/ppermute | solution.py:392
  47.9 22.8 %collective-permute-start.11 = (bf16[448,768]{1,0:T(8,128)(2,1)S(1)}, bf16[448,768]{1,0:T(8,128)(2,1)S(1)}, u32[]{:S(2)}, u32[]{:S(2)}) collective-permute-start(bf16[448,768]{1,0:T(8,128)(2,1)S(1)} %constant_dynamic-update-slice_fusion.8.refs_6_), channel_id=1, source_target_pairs={{0,16},{1,17},{2,18},{3,19},{4,20},{5,21},{6,22},{7,23},{8,24},{9,... | collective-permute-start | bytes 2064392 | tf_op jit(solution)/shard_map/ppermute | solution.py:392
  48.4 22.2 %collective-permute-start.7 = (bf16[48,3072]{1,0:T(8,128)(2,1)S(1)}, bf16[48,3072]{1,0:T(8,128)(2,1)S(1)}, u32[]{:S(2)}, u32[]{:S(2)}) collective-permute-start(bf16[48,3072]{1,0:T(8,128)(2,1)S(1)} %pad_maximum_fusion.4), channel_id=1, source_target_pairs={{0,4},{1,5},{2,6},{3,7},{4,0},{5,1},{6,2},{7,3},{8,12},{9,13},{10,... | collective-permute-start | bytes 884744 | tf_op jit(solution)/shard_map/ppermute | solution.py:392
  51.9 18.7 %collective-permute-start.8 = (bf16[48,3072]{1,0:T(8,128)(2,1)S(1)}, bf16[48,3072]{1,0:T(8,128)(2,1)S(1)}, u32[]{:S(2)}, u32[]{:S(2)}) collective-permute-start(bf16[48,3072]{1,0:T(8,128)(2,1)S(1)} %pad_maximum_fusion.4), channel_id=1, source_target_pairs={{0,6},{1,7},{2,4},{3,5},{4,2},{5,3},{6,0},{7,1},{8,14},{9,15},{10,... | collective-permute-start | bytes 884744 | tf_op jit(solution)/shard_map/ppermute | solution.py:392
  72.1 130.5 %reduce-scatter.5.cloned.1.call-start = ((), (), s32[]{:S(2)}) async-start(), calls=%async_computation.4 | async-start | bytes 2949120 | tf_op jit(solution)/shard_map/reduce_scatter | solution.py:1092
  74.8 14.0 %collective-permute-start.13 = (bf16[2,128,768]{2,1,0:T(8,128)(2,1)}, bf16[2,128,768]{2,1,0:T(8,128)(2,1)S(1)}, u32[]{:S(2)}, u32[]{:S(2)}) collective-permute-start(bf16[2,128,768]{2,1,0:T(8,128)(2,1)} %bitcast.187), channel_id=1, source_target_pairs={{0,2},{1,3},{2,0},{3,1},{4,6},{5,7},{6,4},{7,5},{8,10},{9,11},{10,... | collective-permute-start | bytes 1179656 | tf_op jit(solution)/shard_map/ppermute | solution.py:392
  117.6 13.8 %collective-permute-start.18 = (bf16[384,384]{1,0:T(8,128)(2,1)S(1)}, bf16[384,384]{1,0:T(8,128)(2,1)S(1)}, u32[]{:S(2)}, u32[]{:S(2)}) collective-permute-start(bf16[384,384]{1,0:T(8,128)(2,1)S(1)} %get-tuple-element.315), channel_id=1, source_target_pairs={{0,1},{1,0},{2,3},{3,2},{4,5},{5,4},{6,7},{7,6},{8,9},{9,8},{10,11... | collective-permute-start | bytes 884744 | tf_op jit(solution)/shard_map/ppermute | solution.py:392
  163.6 80.4 %reduce-scatter.3.cloned.1.call-start = ((), (), s32[]{:S(2)}) async-start(), calls=%async_computation.3 | async-start | bytes 2949120 | tf_op jit(solution)/shard_map/reduce_scatter | solution.py:1101
  179.1 47.4 %collective-permute-start.30 = (bf16[2,384,256]{2,1,0:T(8,128)(2,1)S(1)}, bf16[2,384,256]{2,1,0:T(8,128)(2,1)}, u32[]{:S(2)}, u32[]{:S(2)}) collective-permute-start(bf16[2,384,256]{2,1,0:T(8,128)(2,1)S(1)} %copy-done.4), channel_id=1, source_target_pairs={{0,1},{1,0},{2,3},{3,2},{4,5},{5,4},{6,7},{7,6},{8,9},{9,8},{10,11... | collective-permute-start | bytes 1179656 | tf_op jit(solution)/shard_map/ppermute | solution.py:392
  200.5 16.2 %collective-permute-start.23 = (bf16[4,128,768]{2,1,0:T(8,128)(2,1)}, bf16[4,128,768]{2,1,0:T(8,128)(2,1)S(1)}, u32[]{:S(2)}, u32[]{:S(2)}) collective-permute-start(bf16[4,128,768]{2,1,0:T(8,128)(2,1)} %get-tuple-element.194), channel_id=1, source_target_pairs={{0,1},{1,0},{2,3},{3,2},{4,5},{5,4},{6,7},{7,6},{8,9},{9,8},{10,11... | collective-permute-start | bytes 2359304 | tf_op jit(solution)/shard_map/ppermute | solution.py:392
  204.6 16.3 %collective-permute-start.27 = (bf16[48,1536]{1,0:T(8,128)(2,1)}, bf16[48,1536]{1,0:T(8,128)(2,1)}, u32[]{:S(2)}, u32[]{:S(2)}) collective-permute-start(bf16[48,1536]{1,0:T(8,128)(2,1)} %get-tuple-element.340), channel_id=1, source_target_pairs={{0,2},{1,3},{2,0},{3,1},{4,6},{5,7},{6,4},{7,5},{8,10},{9,11},{10,... | collective-permute-start | bytes 442376 | tf_op jit(solution)/shard_map/ppermute | solution.py:392
  206.5 17.2 %collective-permute-start.28 = (bf16[48,1536]{1,0:T(8,128)(2,1)}, bf16[48,1536]{1,0:T(8,128)(2,1)}, u32[]{:S(2)}, u32[]{:S(2)}) collective-permute-start(bf16[48,1536]{1,0:T(8,128)(2,1)} %get-tuple-element.339), channel_id=1, source_target_pairs={{0,4},{1,5},{2,6},{3,7},{4,0},{5,1},{6,2},{7,3},{8,12},{9,13},{10,... | collective-permute-start | bytes 442376 | tf_op jit(solution)/shard_map/ppermute | solution.py:392
  208.5 16.2 %collective-permute-start.29 = (bf16[48,1536]{1,0:T(8,128)(2,1)}, bf16[48,1536]{1,0:T(8,128)(2,1)}, u32[]{:S(2)}, u32[]{:S(2)}) collective-permute-start(bf16[48,1536]{1,0:T(8,128)(2,1)} %get-tuple-element.338), channel_id=1, source_target_pairs={{0,6},{1,7},{2,4},{3,5},{4,2},{5,3},{6,0},{7,1},{8,14},{9,15},{10,... | collective-permute-start | bytes 442376 | tf_op jit(solution)/shard_map/ppermute | solution.py:392
  219.8 23.7 %collective-permute-start.24 = (bf16[128,768]{1,0:T(8,128)(2,1)}, bf16[128,768]{1,0:T(8,128)(2,1)S(1)}, u32[]{:S(2)}, u32[]{:S(2)}) collective-permute-start(bf16[128,768]{1,0:T(8,128)(2,1)} %get-tuple-element.322), channel_id=1, source_target_pairs={{0,2},{1,3},{2,0},{3,1},{4,6},{5,7},{6,4},{7,5},{8,10},{9,11},{10,... | collective-permute-start | bytes 589832 | tf_op jit(solution)/shard_map/ppermute | solution.py:392
  220.9 23.2 %collective-permute-start.25 = (bf16[128,768]{1,0:T(8,128)(2,1)}, bf16[128,768]{1,0:T(8,128)(2,1)S(1)}, u32[]{:S(2)}, u32[]{:S(2)}) collective-permute-start(bf16[128,768]{1,0:T(8,128)(2,1)} %get-tuple-element.321), channel_id=1, source_target_pairs={{0,4},{1,5},{2,6},{3,7},{4,0},{5,1},{6,2},{7,3},{8,12},{9,13},{10,... | collective-permute-start | bytes 589832 | tf_op jit(solution)/shard_map/ppermute | solution.py:392
  223.7 20.4 %collective-permute-start.26 = (bf16[128,768]{1,0:T(8,128)(2,1)S(1)}, bf16[128,768]{1,0:T(8,128)(2,1)S(1)}, u32[]{:S(2)}, u32[]{:S(2)}) collective-permute-start(bf16[128,768]{1,0:T(8,128)(2,1)S(1)} %get-tuple-element.320), channel_id=1, source_target_pairs={{2,4},{3,5},{4,2},{5,3},{10,12},{11,13},{12,10},{13,11},{18,20},{1... | collective-permute-start | bytes 589832 | tf_op jit(solution)/shard_map/ppermute | solution.py:392
  242.0 20.5 %collective-permute-start.36 = (bf16[4,128,768]{2,1,0:T(8,128)(2,1)}, bf16[4,128,768]{2,1,0:T(8,128)(2,1)}, u32[]{:S(2)}, u32[]{:S(2)}) collective-permute-start(bf16[4,128,768]{2,1,0:T(8,128)(2,1)} %get-tuple-element.228), channel_id=1, source_target_pairs={{0,1},{1,0},{2,3},{3,2},{4,5},{5,4},{6,7},{7,6},{8,9},{9,8},{10,11... | collective-permute-start | bytes 2359304 | tf_op jit(solution)/shard_map/ppermute | solution.py:392
  242.0 20.5 %collective-permute-start.31 = (bf16[448,768]{1,0:T(8,128)(2,1)}, bf16[448,768]{1,0:T(8,128)(2,1)S(1)}, u32[]{:S(2)}, u32[]{:S(2)}) collective-permute-start(bf16[448,768]{1,0:T(8,128)(2,1)} %get-tuple-element.224), channel_id=1, source_target_pairs={{0,16},{1,17},{2,18},{3,19},{4,20},{5,21},{6,22},{7,23},{8,24},{9,... | collective-permute-start | bytes 2064392 | tf_op jit(solution)/shard_map/ppermute | solution.py:392
  243.5 19.1 %collective-permute-start.32 = (bf16[448,768]{1,0:T(8,128)(2,1)}, bf16[448,768]{1,0:T(8,128)(2,1)S(1)}, u32[]{:S(2)}, u32[]{:S(2)}) collective-permute-start(bf16[448,768]{1,0:T(8,128)(2,1)} %get-tuple-element.226), channel_id=1, source_target_pairs={{0,8},{1,9},{2,10},{3,11},{4,12},{5,13},{6,14},{7,15},{8,0},{9,1},... | collective-permute-start | bytes 2064392 | tf_op jit(solution)/shard_map/ppermute | solution.py:392
  248.7 13.8 %collective-permute-start.34 = (bf16[48,1536]{1,0:T(8,128)(2,1)S(1)}, bf16[48,1536]{1,0:T(8,128)(2,1)S(1)}, u32[]{:S(2)}, u32[]{:S(2)}) collective-permute-start(bf16[48,1536]{1,0:T(8,128)(2,1)S(1)} %get-tuple-element.335), channel_id=1, source_target_pairs={{0,4},{1,5},{2,6},{3,7},{4,0},{5,1},{6,2},{7,3},{8,12},{9,13},{10,... | collective-permute-start | bytes 442376 | tf_op jit(solution)/shard_map/ppermute | solution.py:392
  287.2 16.3 %collective-permute-start.43 = (bf16[56,1536]{1,0:T(8,128)(2,1)S(1)}, bf16[56,1536]{1,0:T(8,128)(2,1)S(1)}, u32[]{:S(2)}, u32[]{:S(2)}) collective-permute-start(bf16[56,1536]{1,0:T(8,128)(2,1)S(1)} %maximum_maximum_fusion.1), channel_id=1, source_target_pairs={{0,4},{1,5},{2,6},{3,7},{4,0},{5,1},{6,2},{7,3},{8,12},{9,13},{10,... | collective-permute-start | bytes 516104 | tf_op jit(solution)/shard_map/ppermute | solution.py:392
  289.9 13.6 %collective-permute-start.42 = (bf16[56,1536]{1,0:T(8,128)(2,1)S(1)}, bf16[56,1536]{1,0:T(8,128)(2,1)S(1)}, u32[]{:S(2)}, u32[]{:S(2)}) collective-permute-start(bf16[56,1536]{1,0:T(8,128)(2,1)S(1)} %maximum_maximum_fusion), channel_id=1, source_target_pairs={{0,2},{1,3},{2,0},{3,1},{4,6},{5,7},{6,4},{7,5},{8,10},{9,11},{10,... | collective-permute-start | bytes 516104 | tf_op jit(solution)/shard_map/ppermute | solution.py:392
  (94 other events, 672.8 us)
Sparse Core Ops, SparseCore 0:
  72.1 60.3 all-gather.1
  163.7 38.8 reduce-scatter.4
  205.7 37.3 reduce-scatter.2

commit v3 on v2

--- a/solution.py
+++ b/solution.py
@@ -385,7 +385,6 @@
 CORE, Z1, Z2, Z3 = pairs(0, 1), pairs(0, 2), pairs(0, 4), pairs(0, 6)
 X, Y = pairs(1, 0), pairs(2, 0)
 MIDDLE = pairs(0, 6, lambda dp, seq: seq // 2 in (1, 2))
-OUTWARD = pairs(0, 2, lambda dp, seq: seq // 2 in (1, 2))
 
 
 def send(value, route):
@@ -439,66 +438,45 @@
     return [block, send(block, Z1), send(block, Z2), send(block, Z3)]
 
 
-def across(parts, rows):
-    return tuple(
-        jnp.concatenate(
-            [p[:48, c : c + 768] for p in parts] + [p[48:, c : c + 768] for p in parts if rows > 48], axis=0
+def lines(block):
+    return lax.all_gather(block, "dp", axis=0, tiled=True)
+
+
+def placed(rows, target, sems, base):
+    me = my_chip() % 4
+    copies = []
+    for i in range(CHIPS):
+        at = pl.multiple_of(((i // 4) * 4 + ((i % 4) ^ me)) * 48, 16)
+        copies.append(
+            pltpu.make_async_copy(
+                rows.at[pl.ds((i // 4) * 224 + (i % 4) * 48, 48)], target.at[pl.ds(at, 48)], sems.at[base + i]
+            )
         )
-        for c in (0, 768)
-    )
-
-
-def near_hop(first, second):
-    return (
-        jnp.concatenate([first, send(first, X)], axis=0),
-        jnp.concatenate([second, send(second, Y)], axis=0),
-    )
-
-
-def far_hop(first, second):
-    return (first, send(first, Y), second, send(second, X))
-
-
-def placed(groups, target, sems, base):
+    return copies
+
+
+def x_then_y(first, second):
+    return (send(first, X), send(second, Y))
+
+
+def y_then_x(first, second):
+    return (send(first, Y), send(second, X))
+
+
+def placed_hidden(groups, targets, sems):
     me = my_chip()
-    pitch = groups[0].shape[0] // 2
-    copies = []
-    for half in range(2):
-        for far in range(2):
-            for near in range(2):
-                for z in range(4):
-                    across_bits = far * 8 + near * 4 if half == 0 else near * 8 + far * 4
-                    at = pl.multiple_of(((across_bits + z) ^ me) * 48, 16)
-                    copies.append(
-                        pltpu.make_async_copy(
-                            groups[half * 2 + far].at[pl.ds(near * pitch + z * 48, 48), :],
-                            target.at[pl.ds(at, 48), pl.ds(half * 768, 768)],
-                            sems.at[base + len(copies)],
-                        )
-                    )
+    copies = ([], [])
+    for i, group in enumerate(groups):
+        which, far, near = i // 4, (i // 2) % 2, i % 2
+        for z in range(4):
+            b = (far * (8, 4)[which] + near * (4, 8)[which] + z) ^ me
+            for part in range(1 + which):
+                cols = pl.ds(768 * part, 768) if which else pl.ds(0, 1536)
+                at = pl.multiple_of(b * (48, 96)[which] + 48 * part, 16)
+                sem = sems.at[16 * which + len(copies[which])]
+                rows = group.at[pl.ds(z * 48, 48), cols]
+                copies[which].append(pltpu.make_async_copy(rows, targets[which].at[pl.ds(at, 48)], sem))
     return copies
-
-
-def placed_hidden(both, w1, w2, sems):
-    me = my_chip() % 4
-    first, second = [], []
-    for line_index in range(4):
-        for z in range(4):
-            b, i = line_index * 4 + (z ^ me), line_index * 4 + z
-            rows = both.at[pl.ds(i * 48, 48)]
-            at1, at2 = pl.multiple_of(b * 48, 16), pl.multiple_of(b * 96, 16)
-            first.append(
-                pltpu.make_async_copy(rows.at[:, pl.ds(0, 1536)], w1.at[pl.ds(at1, 48)], sems.at[i])
-            )
-            for part in range(2):
-                second.append(
-                    pltpu.make_async_copy(
-                        rows.at[:, pl.ds(1536 + 768 * part, 768)],
-                        w2.at[pl.ds(at2 + 48 * part, 48)],
-                        sems.at[16 + 2 * i + part],
-                    )
-                )
-    return (first, second)
 
 
 def prepare_kernel(*refs):
@@ -561,12 +539,12 @@
 
 
 def project_kernel(*refs):
-    xs, theirs, groups = refs[0:5], refs[5], refs[6:10]
-    bq_ref, bv_ref = refs[10:12]
-    q_ref, k_ref, v_ref, w_ref, x_ref, sems = refs[12:]
+    xs, theirs, rows = refs[0:5], refs[5], refs[6]
+    bq_ref, bv_ref = refs[7:9]
+    q_ref, k_ref, v_ref, w_ref, x_ref, sems = refs[9:]
     slots = [*zip((0, 1, 2, 4, 6), xs), *((2 * z + 3, theirs.at[z]) for z in range(3))]
     loads = [pltpu.make_async_copy(ref, x_ref.at[s], sems.at[32 + s]) for s, ref in slots]
-    loads += placed(groups, w_ref, sems, 0)
+    loads += placed(rows, w_ref, sems, 0)
     for c in loads:
         c.start()
     for c in loads:
@@ -590,28 +568,78 @@
     lax.fori_loop(0, 8, slot, 0)
 
 
-def attend_kernel(q_ref, k_ref, v_ref, kseg_ref, qseg_ref, mix_ref, low_ref, lse_ref):
-    mask = jnp.where(kseg_ref[0] == qseg_ref[0], 0.0, -1e30)
+def fill_mask(mask_ref, kseg_ref, qseg_ref):
+    for c in range(4):
+        rows = slice(256 * c, 256 * c + 256)
+        mask_ref[rows] = jnp.where(kseg_ref[0, rows] == qseg_ref[0], 0.0, -1e30)
+
+
+def attend_kernel(
+    q_ref, k_ref, v_ref, kseg_ref, qseg_ref, rows_ref, got_ref,
+    mix_ref, low_ref, lse_ref, out_ref, wo_ref, mask_ref, score_ref, weight_ref, sems,
+):
+    core, me = my_core(), my_chip() % 4
+    first = pl.program_id(0) == 0
+    loads = []
+    for i in range(8):
+        at = pl.ds(pl.multiple_of((i // 4) * 192 + ((i % 4) ^ me) * 48, 16), 48)
+        row = (i // 4) * 224 + (i % 4) * 48
+        mine = rows_ref.at[pl.ds(pl.multiple_of(core * 448 + row, 16), 48), pl.ds(1152, 384)]
+        for j, src in enumerate((mine, got_ref.at[pl.ds(row, 48)])):
+            cols = pl.ds(pl.multiple_of((core if j == 0 else 1 - core) * 384, 128), 384)
+            loads.append(pltpu.make_async_copy(src, wo_ref.at[at, cols], sems.at[2 * i + j]))
+
+    @pl.when(first)
+    def _():
+        for c in loads:
+            c.start()
+
+    fill_mask(mask_ref, kseg_ref, qseg_ref)
 
     def pair(j, _):
         both = pl.ds(pl.multiple_of(128 * j, 128), 128)
         q2 = q_ref[:, 0, :, both].reshape(2 * BAND, 128)
-        k2 = k_ref[:, 0, :, both].reshape(8 * BAND, 128)
+
+        def score(c, tops):
+            rows = pl.ds(pl.multiple_of(256 * c, 256), 256)
+            k2 = k_ref[pl.ds(2 * c, 2), 0, :, both].reshape(256, 128)
+            new = []
+            for h in range(2):
+                cols = slice(64 * h, 64 * h + 64)
+                s = dot_nt(k2[:, cols], q2[:, cols]) + mask_ref[rows]
+                score_ref[h, rows] = s
+                new.append(jnp.maximum(tops[h], jnp.max(s, axis=0, keepdims=True)))
+            return tuple(new)
+
+        tops = lax.fori_loop(0, 4, score, (jnp.full((1, 256), -1e30, F32),) * 2, unroll=True)
+
+        def weigh(c, totals):
+            rows = pl.ds(pl.multiple_of(256 * c, 256), 256)
+            new = []
+            for h in range(2):
+                e = jnp.exp(score_ref[h, rows] - tops[h])
+                weight_ref[h, rows] = e.astype(BF16)
+                new.append(totals[h] + jnp.sum(e, axis=0, keepdims=True))
+            return tuple(new)
+
+        totals = lax.fori_loop(0, 4, weigh, (jnp.zeros((1, 256), F32),) * 2, unroll=True)
         v2 = v_ref[:, 0, :, both].reshape(8 * BAND, 128)
         for h in range(2):
-            cols = slice(64 * h, 64 * h + 64)
-            s = dot_nt(k2[:, cols], q2[:, cols]) + mask
-            top = jnp.max(s, axis=0, keepdims=True)
-            e = jnp.exp(s - top)
-            total = jnp.sum(e, axis=0, keepdims=True)
-            mixed = dot_tn(v2[:, cols], e.astype(BF16)) * (1.0 / total)
+            mixed = dot_tn(v2[:, 64 * h : 64 * h + 64], weight_ref[h]) * (1.0 / totals[h])
             rows = pl.ds(pl.multiple_of(128 * j + 64 * h, 64), 64)
             mix_ref[0, rows] = mixed
             low_ref[0, rows] = mixed.astype(BF16)
-            lse_ref[0, pl.ds(2 * j + h, 1)] = top + jnp.log(total)
+            lse_ref[0, pl.ds(2 * j + h, 1)] = tops[h] + jnp.log(totals[h])
         return 0
 
     lax.fori_loop(0, 3, pair, 0)
+
+    @pl.when(first)
+    def _():
+        for c in loads:
+            c.wait()
+
+    out_ref[:, 0] = dot_tn(low_ref[0], wo_ref[...]).astype(BF16).reshape(2, BAND, 768)
 
 
 def norm(z):
@@ -632,19 +660,24 @@
 
 def forward_kernel(*refs):
     x_ref, own_ref, other_ref, vec_ref, b1_ref = refs[0:5]
-    both = refs[5]
-    n1_ref, r1_ref, low_ref, act_ref, slope_ref, f_ref, w1_ref, w2_ref, tok_ref, sems = refs[6:]
-    loads1, loads2 = placed_hidden(both, w1_ref, w2_ref, sems)
-    tokens = pltpu.make_async_copy(x_ref.at[pl.ds(0, 2)], tok_ref, sems.at[48])
-    for c in [tokens] + loads1 + loads2:
+    n1_ref, r1_ref, low_ref, act_ref, slope_ref, f_ref, w1_ref, w2_ref, tok_buf, own_buf, other_buf, sems = refs[13:]
+    loads1, loads2 = placed_hidden(refs[5:13], (w1_ref, w2_ref), sems)
+    early = [
+        pltpu.make_async_copy(src, dst, sems.at[48 + i])
+        for i, (src, dst) in enumerate(
+            ((x_ref.at[pl.ds(0, 2)], tok_buf), (own_ref, own_buf), (other_ref, other_buf))
+        )
+    ]
+    for c in early + loads1 + loads2:
         c.start()
-    tokens.wait()
+    for c in early:
+        c.wait()
     bo, g1, s1 = vec_ref[2:3], vec_ref[3:4], vec_ref[4:5]
 
     def rows(i, _):
         r = pl.ds(i * 128, 128)
-        o = pl.ds((i ^ 2) * 128, 128)
-        z = tok_ref[i // 2, i % 2].astype(F32) + (own_ref[r].astype(F32) + other_ref[o].astype(F32)) + bo
+        c, m = i // 2, i % 2
+        z = tok_buf[c, m].astype(F32) + (own_buf[c, m].astype(F32) + other_buf[1 - c, m].astype(F32)) + bo
         n, rstd = norm(z)
         n1_ref[r] = n
         r1_ref[r] = rstd
@@ -677,8 +710,10 @@
 
 
 def middle_kernel(
-    n1_ref, own_ref, other_ref, cot_ref, pcot_ref, vec_ref, out_ref, df_ref, dz_ref, sums_ref,
+    n1_ref, own_ref, other_ref, cot_ref, theirs_ref, vec_ref, out_ref, df_ref, dz_ref, sums_ref, pcot_ref, sem,
 ):
+    load = pltpu.make_async_copy(theirs_ref.at[3], pcot_ref, sem)
+    load.start()
     g1, s1, b2, g2, s2 = (vec_ref[i : i + 1] for i in (3, 4, 5, 6, 7))
 
     def rows(i, which):
@@ -686,7 +721,7 @@
         r, o = pl.ds(base + i * 128, 128), pl.ds(256 - base + i * 128, 128)
         z = n1_ref[r] * g1 + s1 + (own_ref[r].astype(F32) + other_ref[o].astype(F32)) + b2
         n, rstd = norm(z)
-        grad = ref[pl.ds(i * 128, 128)].astype(F32)
+        grad = ref[i].astype(F32)
         dz = norm_grad(grad, n, rstd, g2)
         dz_ref[r] = dz
         df_ref[r] = dz.astype(BF16)
@@ -707,6 +742,7 @@
         return 0
 
     lax.fori_loop(0, 2, own_rows, 0)
+    load.wait()
     lax.fori_loop(0, 2, other_rows, 0)
 
 
@@ -728,7 +764,9 @@
     lax.fori_loop(0, 3, back, 0)
 
 
-def first_kernel(dz_ref, own_ref, other_ref, n1_ref, r1_ref, vec_ref, wo_ref, dz1_ref, do_ref, half_ref, da_ref, sums_ref):
+def first_kernel(
+    dz_ref, own_ref, other_ref, n1_ref, r1_ref, vec_ref, wo_ref, dz1_ref, do_ref, half_ref, da_ref, sums_ref,
+):
     g1 = vec_ref[3:4]
     core = my_core()
     sums_ref[...] = jnp.zeros_like(sums_ref)
@@ -763,22 +801,29 @@
             da_ref[m, :, c * BAND : (c + 1) * BAND] = dot_nt(wo_ref[...], part).astype(BF16)
 
 
-def attend_back_kernel(q_ref, k_ref, v_ref, mix_ref, da_ref, lse_ref, kseg_ref, qseg_ref, dq_ref, dk_ref, dv_ref):
-    mask = jnp.where(kseg_ref[0] == qseg_ref[0], 0.0, -1e30)
+def attend_back_kernel(
+    q_ref, k_ref, v_ref, mix_ref, da_ref, lse_ref, kseg_ref, qseg_ref, w_ref, dq_ref, dk_ref, dv_ref, own_ref, send_ref, sums_ref,
+    mask_ref,
+):
+    fill_mask(mask_ref, kseg_ref, qseg_ref)
 
     def pair(j, _):
         both = pl.ds(pl.multiple_of(128 * j, 128), 128)
         q2 = q_ref[:, 0, :, both].reshape(2 * BAND, 128)
+        das, deltas, lses = [], [], []
+        for h in range(2):
+            rows = pl.ds(pl.multiple_of(128 * j + 64 * h, 64), 64)
+            das.append(da_ref[0, rows])
+            deltas.append(jnp.sum(das[h].astype(F32) * mix_ref[0, rows], axis=0, keepdims=True))
+            lses.append(lse_ref[0, pl.ds(2 * j + h, 1)])
         k2 = k_ref[:, 0, :, both].reshape(8 * BAND, 128)
         v2 = v_ref[:, 0, :, both].reshape(8 * BAND, 128)
         dks, dvs, dqs = [], [], []
         for h in range(2):
             cols = slice(64 * h, 64 * h + 64)
-            rows = pl.ds(pl.multiple_of(128 * j + 64 * h, 64), 64)
-            k, v, qh, da = k2[:, cols], v2[:, cols], q2[:, cols], da_ref[0, rows]
-            p = jnp.exp(dot_nt(k, qh) + mask - lse_ref[0, pl.ds(2 * j + h, 1)])
-            delta = jnp.sum(da.astype(F32) * mix_ref[0, rows], axis=0, keepdims=True)
-            ds = (p * (dot_nn(v, da) - delta)).astype(BF16)
+            k, v, qh, da = k2[:, cols], v2[:, cols], q2[:, cols], das[h]
+            p = jnp.exp(dot_nt(k, qh) + mask_ref[...] - lses[h])
+            ds = (p * (dot_nn(v, da) - deltas[h])).astype(BF16)
             dvs.append(dot_nt(p.astype(BF16), da))
             dks.append(dot_nn(ds, qh))
             dqs.append(dot_tn(k, ds))
@@ -790,8 +835,9 @@
 
     lax.fori_loop(0, 3, pair, 0)
 
-
-def token_grad_kernel(dq_ref, dk_ref, dv_ref, w_ref, own_ref, send_ref):
+    sums_ref[0:1] = jnp.sum(dq_ref[...].reshape(2 * BAND, 384).astype(F32), axis=0, keepdims=True)
+    sums_ref[1:2] = jnp.sum(dv_ref[...].reshape(8 * BAND, 384).astype(F32), axis=0, keepdims=True)
+
     def step(z, _):
         dk = dk_ref[pl.ds(2 * z, 2)].reshape(2 * BAND, 384)
         dv = dv_ref[pl.ds(2 * z, 2)].reshape(2 * BAND, 384)
@@ -808,6 +854,20 @@
     send_ref[0] = dx[BAND:].astype(BF16)
 
 
+def inner_grad_kernel(low_ref, du_ref, out_ref):
+    me = my_chip() % 4
+
+    def step(j, _):
+        cols = pl.ds(pl.multiple_of(j * 384, 384), 384)
+        value = dot_tn(low_ref[:, cols], du_ref[...]).astype(BF16)
+        for i in range(8):
+            rows = pl.ds(pl.multiple_of((j * 8 + (i ^ me)) * 48, 16), 48)
+            out_ref[rows, :] = value[48 * i : 48 * i + 48]
+        return 0
+
+    lax.fori_loop(0, 2, step, 0)
+
+
 def stored_at(block):
     p = block ^ my_chip()
     y, x, z = p // 8, (p // 4) % 2, p % 4
@@ -834,33 +894,18 @@
         c.wait()
 
 
-def outer_grad_kernel(act_ref, df_ref, out_ref):
-    me = my_chip() % 4
+def outer_grad_kernel(act_ref, df_ref, *refs):
+    outs, halves, sems = refs[:4], refs[4:6], refs[6]
 
     def step(j, _):
         cols = pl.ds(pl.multiple_of(j * 384, 384), 384)
         value = dot_tn(act_ref[:, cols], df_ref[...]).astype(BF16)
         for i in range(4):
-            rows = pl.ds(pl.multiple_of((j * 4 + (i ^ me)) * 48, 16), 48)
-            out_ref[rows, 0:768] = value[96 * i : 96 * i + 48]
-            out_ref[rows, 768:1536] = value[96 * i + 48 : 96 * i + 96]
+            place_rows(halves, j * 4 + i, value[96 * i : 96 * i + 48], value[96 * i + 48 : 96 * i + 96])
         return 0
 
     lax.fori_loop(0, 4, step, 0)
-
-
-def inner_grad_kernel(low_ref, du_ref, out_ref):
-    me = my_chip() % 4
-
-    def step(j, _):
-        cols = pl.ds(pl.multiple_of(j * 384, 384), 384)
-        value = dot_tn(low_ref[:, cols], du_ref[...]).astype(BF16)
-        for i in range(8):
-            rows = pl.ds(pl.multiple_of((j * 8 + (i ^ me)) * 48, 16), 48)
-            out_ref[rows, :] = value[48 * i : 48 * i + 48]
-        return 0
-
-    lax.fori_loop(0, 2, step, 0)
+    finish(flush(halves, outs, sems))
 
 
 def projection_grad_kernel(x_ref, *refs):
@@ -987,7 +1032,7 @@
         prepare_kernel, [((32, 1536), BF16), ((32, 1536), BF16), ((48, 1536), BF16)], 14
     )(w_query, w_key, w_value, w_output, *(v.reshape(1, -1) for v in lanes), w_outer)
     (square,) = call(chip_rows_kernel, [((56, 1536), BF16)], 2)(mine, send(theirs, CORE))
-    wide = w_inner.astype(BF16).reshape(24, CHIPS, 2, 96)
+    wide = after(w_inner, mine).astype(BF16).reshape(24, CHIPS, 2, 96)
     mine, theirs = (
         jnp.where(even, wide[:, :, 0], wide[:, :, 1]).reshape(24, 1536),
         jnp.where(even, wide[:, :, 1], wide[:, :, 0]).reshape(24, 1536),
@@ -1002,48 +1047,41 @@
     other_tokens = send(tokens, CORE)
     hidden_rows = jnp.concatenate([inner_rows, outer_rows], axis=1)
     square, hidden_rows, other_tokens = after_both((square, hidden_rows, other_tokens), ())
-    square = across(line(square), 56)
-    hidden_rows, square = after_both((hidden_rows, square), ())
+    square = line(square)
+    square = jnp.concatenate([p[:48] for p in square] + [p[48:] for p in square], axis=0)
+    square, hidden_rows = after_both((square, hidden_rows), ())
+    square = lines(square)
     hidden = line(hidden_rows)
-    got = (send(square[0], X), send(square[1], Y))
-    got, square = after_both((got, square), hidden[1:2])
-    square = far_hop(*(jnp.concatenate(pair, axis=0) for pair in zip(square, got)))
-    hidden, tokens = after_both((hidden, tokens), square)
-    hidden = lax.all_gather(jnp.concatenate(hidden, axis=0), "dp", axis=0, tiled=True)
-    beside, opposite = send(tokens, Z1), send(tokens, MIDDLE)
-    square, beside, opposite = after_both((square, beside, opposite), ())
-    outside = (seq // 2 == 0) | (seq // 2 == 3)
-    second = jnp.where(outside, send(opposite, OUTWARD), send(beside, MIDDLE))
-    theirs = send(jnp.stack([beside, second, opposite]), CORE)
-    slots = [tokens, other_tokens, beside, second, opposite, theirs]
-
+    hidden, tokens = after_both((hidden, tokens), (kseg, qseg))
+    hidden = [jnp.concatenate([h[:, c : c + 1536] for h in hidden], axis=0) for c in (0, 1536)]
     places = jnp.arange(CHIPS)
     order = ((places[:, None] ^ me) == places[None, :]).astype(BF16)
-    vecs = []
-    for half, turn in ((square[:2], (0, 1, 2, 3)), (square[2:], (0, 2, 1, 3))):
-        rows = [g[224 * near + 192 : 224 * near + 224].reshape(4, 8, 768)[:, :2] for g in half for near in (0, 1)]
-        vecs.append(jnp.concatenate([rows[i] for i in turn], axis=0))
-    vecs = jnp.concatenate(vecs, axis=2).reshape(CHIPS, 2 * 1536)
-    vecs = dot_nn(order, vecs).reshape(CHIPS, 2, 12, 128)
+    line_order = ((places[:, None] ^ (me % 4)) == places[None, :]).astype(BF16)
+    vecs = square.reshape(4, 224, 1536)[:, 192:].reshape(CHIPS, 8, 1536)[:, :2].reshape(CHIPS, 2 * 1536)
+    vecs = dot_nn(line_order, vecs).reshape(CHIPS, 2, 12, 128)
     vec8 = vecs[:, :, :8, :24].transpose(2, 0, 1, 3).reshape(8, 768)
     b1 = jnp.where(even, vecs[:, 0, 8, :96], vecs[:, 1, 8, :96]).reshape(1, 1536)
     bq = jnp.where(even, vec8[0:1, :384], vec8[0:1, 384:])
     bv = jnp.where(even, vec8[1:2, :384], vec8[1:2, 384:])
 
+    wo_rows = square[:, 1152:]
+    wo_got = send(jnp.where(even, wo_rows[448:], wo_rows[:448]), CORE)
+
+    near = x_then_y(*hidden)
+    beside, second, opposite = send(tokens, Z1), send(tokens, Z2), send(tokens, MIDDLE)
+    theirs = send(jnp.stack(after_both((beside, second, opposite, cot), (near, vec8, b1, bq, bv, wo_got))), CORE)
+    slots = [tokens, other_tokens, beside, second, opposite, theirs]
+    far = y_then_x(*hidden)
+
     slot_shape, head_shape = (2, BAND, 768), (2, BAND, 384)
     q, k, v, w_abs, x_all = call(
         project_kernel,
         [((2, *head_shape), BF16), ((8, *head_shape), BF16), ((8, *head_shape), BF16), ((768, 1536), BF16), ((8, *slot_shape), BF16)],
-        12,
-        in_specs=[IN_PLACE] * 10 + [IN_VMEM] * 2,
+        9,
+        in_specs=[IN_PLACE] * 7 + [IN_VMEM] * 2,
         scratch=[pltpu.SemaphoreType.DMA((40,))],
         cost=(2_800_000_000, 16_000_000),
-    )(*slots, *square, bq, bv)
-    wo_half = w_abs[:, 1152:]
-    wo_mine = jnp.where(even, wo_half[:384], wo_half[384:])
-    wo_got = send(jnp.where(even, wo_half[384:], wo_half[:384]), CORE)
-    wo = in_order(wo_mine, wo_got, 1)
-
+    )(*slots, square, bq, bv)
     def attention_specs(m=None):
         micro = (lambda i: i) if m is None else (lambda i: m)
         q_spec = pl.BlockSpec((2, 1, BAND, 384), lambda i: (0, micro(i), 0, 0))
@@ -1057,49 +1095,71 @@
         return ([q_spec, k_spec, k_spec], [t_spec, t_spec, lse_spec], segs)
 
     qkv_specs, mix_specs, seg_specs = attention_specs()
-    other_cot = send(after(cot, q), CORE)
-
-    mix, mix_low, lse = call(
+    near, (q, k, v) = after_both((near, (q, k, v)), far)
+    both = y_then_x(*near)
+    mix, mix_low, lse, branch, wo = call(
         attend_kernel,
-        [((2, 384, 256), F32), ((2, 384, 256), BF16), ((2, 8, 256), F32)],
-        5,
+        [((2, 384, 256), F32), ((2, 384, 256), BF16), ((2, 8, 256), F32), ((2, *slot_shape), BF16), ((384, 768), BF16)],
+        7,
         grid=(2,),
-        in_specs=qkv_specs + seg_specs,
-        out_specs=mix_specs,
-        cost=(1_600_000_000, 8_000_000),
-    )(q, k, v, kseg, qseg)
-    branch = [dot_tn(mix_low[m], wo).astype(BF16).reshape(2, 1, BAND, 768) for m in range(2)]
-    branch = jnp.concatenate(branch, axis=1).reshape(4 * BAND, 768)
+        in_specs=qkv_specs + seg_specs + [IN_PLACE] * 2,
+        out_specs=[
+            *mix_specs,
+            pl.BlockSpec((2, 1, BAND, 768), lambda i: (0, i, 0, 0)),
+            pl.BlockSpec((384, 768), lambda i: (0, 0)),
+        ],
+        scratch=[
+            pltpu.VMEM((1024, 256), F32),
+            pltpu.VMEM((2, 1024, 256), F32),
+            pltpu.VMEM((2, 1024, 256), BF16),
+            pltpu.SemaphoreType.DMA((16,)),
+        ],
+        cost=(1_900_000_000, 10_000_000),
+    )(q, k, v, kseg, qseg, square, wo_got)
+    branch, both = after_both((branch, both), ())
+    hidden = [g[i] for i in range(2) for g in (hidden, near, far, both)]
     branch_other = send(branch, CORE)
     n1, r1, hid_low, act, slope, f_own, w1, w2 = call(
         forward_kernel,
         [((512, 768), F32), ((512, 1), F32), ((512, 768), BF16), ((512, 1536), BF16), ((512, 1536), BF16), ((512, 768), BF16), ((768, 1536), BF16), ((1536, 768), BF16)],
-        6,
-        in_specs=[IN_PLACE] + [IN_VMEM] * 4 + [IN_PLACE],
-        scratch=[pltpu.VMEM((2, *slot_shape), BF16), pltpu.SemaphoreType.DMA((49,))],
+        13,
+        in_specs=[IN_PLACE] * 3 + [IN_VMEM] * 2 + [IN_PLACE] * 8,
+        scratch=[pltpu.VMEM((2, *slot_shape), BF16)] * 3 + [pltpu.SemaphoreType.DMA((51,))],
         cost=(2_500_000_000, 16_000_000),
-    )(x_all, branch, branch_other, vec8, b1, hidden)
+    )(x_all, branch, branch_other, vec8, b1, *hidden)
     mix_other = send(after(mix_low, n1), CORE)
     result, df, dz2, sums2 = call(
         middle_kernel,
         [((256, 768), BF16), ((512, 768), BF16), ((512, 768), F32), ((8, 768), F32)],
         6,
+        in_specs=[IN_VMEM] * 4 + [IN_PLACE, IN_VMEM],
+        scratch=[pltpu.VMEM(slot_shape, BF16), pltpu.SemaphoreType.DMA],
         cost=(50_000_000, 8_000_000),
-    )(n1, f_own, send(f_own, CORE), cot.reshape(256, 768), other_cot.reshape(256, 768), vec8)
+    )(n1, f_own, send(f_own, CORE), cot, theirs, vec8)
 
     piece = [pltpu.VMEM((2, 384, 768), BF16)] * 2
-    (outer_terms,) = call(outer_grad_kernel, [((768, 1536), BF16)], 2, cost=(1_200_000_000, 6_000_000))(act, df)
-    outer_block = lax.psum_scatter(outer_terms, "dp", scatter_dimension=0, tiled=True)
+    outer_terms = call(
+        outer_grad_kernel,
+        [((384, 768), BF16)] * 4,
+        2,
+        out_specs=[IN_PLACE] * 4,
+        scratch=piece + [pltpu.SemaphoreType.DMA((4,))],
+        cost=(1_200_000_000, 6_000_000),
+    )(act, df)
+    outer_hop = first_hop(outer_terms)
     du, dh_own, db1 = call(
         hidden_kernel,
         [((512, 1536), BF16), ((512, 768), BF16), ((1, 1536), F32)],
         4,
         cost=(2_400_000_000, 9_000_000),
-    )(after(df, outer_terms), slope, w1, w2)
+    )(after(df, *outer_terms), slope, w1, w2)
     dh_other = send(dh_own, CORE)
     (inner_terms,) = call(inner_grad_kernel, [((768, 1536), BF16)], 2, cost=(1_200_000_000, 6_000_000))(hid_low, du)
     inner_block = lax.psum_scatter(inner_terms, "dp", scatter_dimension=0, tiled=True)
-    dh_own = after(dh_own, inner_terms)
+    outer_hop = after_both(outer_hop, (inner_terms,))
+    outer_low = near_terms(outer_hop, 48)
+    dh_own = after(dh_own, inner_terms, *outer_low)
+    outer_sent = hop_terms(outer_low)
     dz1, do, do_half, da, sums1 = call(
         first_kernel,
         [((256, 768), F32), ((512, 768), BF16), ((512, 384), BF16), ((2, 384, 256), BF16), ((8, 768), F32)],
@@ -1109,21 +1169,17 @@
 
     def back(m, events):
         specs = attention_specs(m)
+        shapes = [(2, BAND, 384), (8, BAND, 384), (8, BAND, 384), (4, BAND, 768), (4, BAND, 768)]
         return call(
             attend_back_kernel,
-            [((2, BAND, 384), BF16), ((8, BAND, 384), BF16), ((8, BAND, 384), BF16)],
-            8,
+            [(shape, BF16) for shape in shapes] + [((8, 384), F32)],
+            9,
             grid=(1,),
-            in_specs=specs[0] + specs[1] + specs[2],
-            out_specs=[pl.BlockSpec((n, BAND, 384), lambda i: (0, 0, 0)) for n in (2, 8, 8)],
-            cost=(2_000_000_000, 6_000_000),
-        )(q, k, v, mix, after(da, *events), lse, kseg, qseg)
-
-    def token_grads(grads, events):
-        own, away = call(
-            token_grad_kernel, [((4, BAND, 768), BF16)] * 2, 4, cost=(1_350_000_000, 5_000_000)
-        )(*after_both(grads, events), w_abs)
-        return (own, away, send(away, CORE))
+            in_specs=specs[0] + specs[1] + specs[2] + [pl.BlockSpec((768, 1536), lambda i: (0, 0))],
+            out_specs=[pl.BlockSpec(shape, lambda i: (0, 0, 0)) for shape in shapes] + [pl.BlockSpec((8, 384), lambda i: (0, 0))],
+            scratch=[pltpu.VMEM((1024, 256), F32)],
+            cost=(3_400_000_000, 10_000_000),
+        )(q, k, v, mix, after(da, *events), lse, kseg, qseg, w_abs)
 
     def core_sums(own, got):
         return [add(own[z], got[z]) if z == 0 else add(own[z], got[z]).astype(BF16) for z in range(4)]
@@ -1131,23 +1187,26 @@
     def line_sums(sums):
         return (sums[0], send(sums[1], Z1), send(sums[2], Z2), send(sums[3], MIDDLE))
 
-    grads0 = back(0, ())
-    dx0, _, got0 = token_grads(grads0, ())
-    grads1 = back(1, (dx0, outer_block))
-    outer_parts = after_both(block_parts(outer_block), grads1[:1])
-    low0 = core_sums(dx0, after(got0, grads1[0]))
-    grads1, _ = lax.optimization_barrier((grads1, (outer_parts, low0)))
+    outer_hop, outer_sent = after_both((outer_hop, outer_sent), (da,))
+    outer_half = far_terms(outer_hop, outer_sent, 48)
+    *grads0, dx0, dx_send, sums_q0 = back(0, outer_half)
+    outer_parts = line_parts(outer_half, 48)
+    got0 = send(dx_send, CORE)
+    *grads1, dx1, dx_send, sums_q1 = back(1, (dx0,))
+    outer_parts, got0, dx0 = after_both((outer_parts, got0, dx0), grads1[:1])
+    got1 = send(dx_send, CORE)
+    low0 = core_sums(dx0, got0)
+    grads1, _ = lax.optimization_barrier((grads1, (outer_parts, low0, inner_block)))
+    inner_parts = block_parts(inner_block)
     sent0 = line_sums(low0)
 
     def widen(value):
         zero = jnp.zeros_like(value)
         return in_order(value, zero, 1)
 
-    def column(index):
-        return sum(jnp.sum(g[index].astype(F32), axis=(0, 1)) for g in (grads0, grads1))[None]
-
+    sums_q = sums_q0 + sums_q1
     eight = jnp.concatenate(
-        [widen(column(0)), widen(column(2)), sums1[2:3], sums1[0:1], sums1[1:2], sums2[2:3], sums2[0:1], sums2[1:2]], 0
+        [widen(sums_q[0:1]), widen(sums_q[1:2]), sums1[2:3], sums1[0:1], sums1[1:2], sums2[2:3], sums2[0:1], sums2[1:2]], 0
     )
     eight = jnp.pad(eight.reshape(8, CHIPS, 2, 24), ((0, 0), (0, 0), (0, 0), (0, 104))).transpose(1, 2, 0, 3)
     db1 = jnp.where(jnp.arange(2)[None, :, None] == core, db1.reshape(CHIPS, 1, 96), 0.0)
@@ -1166,13 +1225,10 @@
         cost=(3_300_000_000, 12_000_000),
     )(x_all, grads0[0], grads1[0], grads0[1], grads1[1], grads0[2], grads1[2], mix_low[0], mix_low[1], mix_other, do_half, jnp.concatenate([vec_first, vec_second]))
     square_hop = first_hop(square_terms)
-    dx1, _, got1 = token_grads(grads1, square_terms[:1])
-    inner_block, sent0 = after_both((inner_block, sent0), (dx1,))
-    inner_parts = block_parts(inner_block)
-    square_hop, inner_parts, got1 = after_both((square_hop, inner_parts, got1), (dx1,))
+    inner_parts, got1 = after_both((inner_parts, got1), square_terms)
+    sent1 = line_sums(core_sums(dx1, got1))
+    square_hop, sent0 = after_both((square_hop, sent0), ())
     square_sent = hop_terms(near_terms(square_hop, 56))
-    sent1 = line_sums(core_sums(dx1, got1))
-    square_sent, sent1, square_hop = after_both((square_sent, sent1, square_hop), ())
     square_half = far_terms(square_hop, square_sent, 56)
     square_parts = line_parts(square_half, 56)
 

time: 319 us -> 301 us (0.944)
  waiting for transfers between devices: 84.4 us -> 73.2 us
  starting transfers between devices: 57.9 us -> 67 us
  Pallas kernels: 110 us -> 104 us
  other arithmetic: 22.5 us -> 18.6 us
    ppermute x47 -> x51, waiting for transfers between devices: 82.7 us -> 68.2 us  [send(): return lax.ppermute(value, BOTH, route)]
    ppermute x47 -> x51, starting transfers between devices: 57.6 us -> 66.9 us  [send(): return lax.ppermute(value, BOTH, route)]
    all_gather x1, waiting for transfers between devices: 0.01 us -> 4.97 us  [lines(): return lax.all_gather(block, 'dp', axis=0, tiled=True)]
    pallas_call x5 -> x3, Pallas kernels: 32.6 us -> 28.4 us  [the longest x2 23.2 us: back(): call(attend_back_kernel, [(shape, BF16) for shape in shapes] + [((8, 384)...]
    unnamed x126 -> x78, local copies, waits for them, and re-layouts: 11.5 us -> 7.88 us
    reshape x5 -> x1, local copies, waits for them, and re-layouts: 3.51 us -> 0.19 us  [per_device_paired(): wide = after(w_inner, mine).astype(BF16).reshape(24, CHIPS, 2, 96)]
  transfers between devices with their start and end apart: 50 -> 53, of which waited for: 18 -> 26; matrix products, arithmetic and copies ran while one was open for 11% -> 10% of each run, Pallas kernels for 26% -> 25%
where the time goes in v3:
time: 301 us; the launch traced here: 300 us
  Pallas kernels  104 us (35%)
  waiting for transfers between devices  73.2 us (24%)
  starting transfers between devices  67 us (22%)
  local copies, waits for them, and re-layouts  22 us (7%)
  other arithmetic  18.6 us (6%)
  between operations  15.2 us (5%)
    ppermute x51, waiting for transfers between devices, send(): return lax.ppermute(value, BOTH, route)  68.2 us
    ppermute x51, starting transfers between devices, send(): return lax.ppermute(value, BOTH, route)  66.9 us
    pallas_call x2, Pallas kernels, back(): call(attend_back_kernel, [(shape, BF16) for shape in shapes] + [((8, 384)...  23.2 us
    pallas_call x1, Pallas kernels, per_device_paired(): call(forward_kernel, [((512, 768), F32), ((512, 1), F32), ((512, 768), BF...  12.3 us
    pallas_call x1, Pallas kernels, per_device_paired(): call(project_kernel, [((2, *head_shape), BF16), ((8, *head_shape), BF16),...  11.9 us
    pallas_call x1, Pallas kernels, per_device_paired(): call(attend_kernel, [((2, 384, 256), F32), ((2, 384, 256), BF16), ((2, 8,...  10.5 us
    pallas_call x1, Pallas kernels, per_device_paired(): call(projection_grad_kernel, [((448, 768), BF16)] * 4, 12, out_specs=[IN_...  9.56 us
    pallas_call x1, Pallas kernels, per_device_paired(): call(hidden_kernel, [((512, 1536), BF16), ((512, 768), BF16), ((1, 1536),...  8.33 us
  transfers between devices with their start and end apart: 53, of which 26 were waited for; matrix products, arithmetic and copies ran while one was open for 10% of the time, Pallas kernels for 25%

profile of v3, /device:TPU:0, one launch (start us, length us, event | category | flops | bytes accessed | tf_op | source)
XLA Modules:
  0.0 300.2 jit_solution(7140941160069872305)
XLA Ops:
  21.4 3.6 %collective-permute-done.3 = bf16[56,1536]{1,0:T(8,128)(2,1)S(1)} collective-permute-done((bf16[56,1536]{1,0:T(8,128)(2,1)}, bf16[56,1536]{1,0:T(8,128)(2,1)S(1)}, u32[]{:S(2)}, u32[]{:S(2)}) %collective-permute-start.3) | collective-permute-done | bytes 172064 | tf_op jit(solution)/shard_map/ppermute | solution.py:391
  25.0 9.5 %collective-permute-done.4 = bf16[56,1536]{1,0:T(8,128)(2,1)S(1)} collective-permute-done((bf16[56,1536]{1,0:T(8,128)(2,1)}, bf16[56,1536]{1,0:T(8,128)(2,1)S(1)}, u32[]{:S(2)}, u32[]{:S(2)}) %collective-permute-start.4) | collective-permute-done | bytes 172064 | tf_op jit(solution)/shard_map/ppermute | solution.py:391
  38.8 3.3 %collective-permute-start.6 = (bf16[48,3072]{1,0:T(8,128)(2,1)S(1)}, bf16[48,3072]{1,0:T(8,128)(2,1)S(1)}, u32[]{:S(2)}, u32[]{:S(2)}) collective-permute-start(bf16[48,3072]{1,0:T(8,128)(2,1)S(1)} %pad_maximum_fusion.4), channel_id=1, source_target_pairs={{0,2},{1,3},{2,0},{3,1},{4,6},{5,7},{6,4},{7,5},{8,10},{9,11},{10,... | collective-permute-start | bytes 884744 | tf_op jit(solution)/shard_map/ppermute | solution.py:391
  45.9 7.8 %collective-permute-done.6 = bf16[48,3072]{1,0:T(8,128)(2,1)S(1)} collective-permute-done((bf16[48,3072]{1,0:T(8,128)(2,1)S(1)}, bf16[48,3072]{1,0:T(8,128)(2,1)S(1)}, u32[]{:S(2)}, u32[]{:S(2)}) %collective-permute-start.6) | collective-permute-done | bytes 294944 | tf_op jit(solution)/shard_map/ppermute | solution.py:391
  53.7 11.9 %collective-permute-done.7 = bf16[48,3072]{1,0:T(8,128)(2,1)S(1)} collective-permute-done((bf16[48,3072]{1,0:T(8,128)(2,1)S(1)}, bf16[48,3072]{1,0:T(8,128)(2,1)S(1)}, u32[]{:S(2)}, u32[]{:S(2)}) %collective-permute-start.7) | collective-permute-done | bytes 294944 | tf_op jit(solution)/shard_map/ppermute | solution.py:391
  65.6 6.1 %collective-permute-start.10 = (bf16[2,128,768]{2,1,0:T(8,128)(2,1)}, bf16[2,128,768]{2,1,0:T(8,128)(2,1)S(1)}, u32[]{:S(2)}, u32[]{:S(2)}) collective-permute-start(bf16[2,128,768]{2,1,0:T(8,128)(2,1)} %bitcast.9.refs_0_), channel_id=1, source_target_pairs={{0,4},{1,5},{2,6},{3,7},{4,0},{5,1},{6,2},{7,3},{8,12},{9,13},{10,... | collective-permute-start | bytes 1179656 | tf_op jit(solution)/shard_map/ppermute | solution.py:391
  77.6 5.0 %all-gather.2.cloned.1.call-done.refs_6_.rows_ref = bf16[896,1536]{1,0:T(8,128)(2,1)} async-done(((bf16[224,1536]{1,0:T(8,128)(2,1)}), bf16[896,1536]{1,0:T(8,128)(2,1)}) %all-gather.2.cloned.1.call-update) | async-done | bytes 2752528 | tf_op jit(solution)/shard_map/all_gather | solution.py:442
  97.6 11.9 %shard_map.307 = (bf16[2,2,128,384]{3,2,1,0:T(8,128)(2,1)}, bf16[8,2,128,384]{3,2,1,0:T(8,128)(2,1)}, bf16[8,2,128,384]{3,2,1,0:T(8,128)(2,1)}, bf16[768,1536]{1,0:T(8,128)(2,1)}, bf16[8,2,128,768]{3,2,1,0:T(8,128)(2,1)}) custom-call(bf16[2,128,768]{2,1,0:T(8,128)(2,1)} %bitcast.9.refs_0_, bf16[2,128,768]{2,1,0:T(8,128)(2,1)} %collective-permute-done.2.refs_1_, ...), custom_call_target="tpu_custom_call" | custom-call | flops 2800000000 | bytes 16000000 | tf_op jit(solution)/shard_map/pallas_call | solution.py:1077
  112.1 10.5 %shard_map.308 = (f32[2,384,256]{2,1,0:T(8,128)}, bf16[2,384,256]{2,1,0:T(8,128)(2,1)}, f32[2,8,256]{2,1,0:T(8,128)}, bf16[2,2,128,768]{3,2,1,0:T(8,128)(2,1)}, bf16[384,768]{1,0:T(8,128)(2,1)}) custom-call(bf16[2,2,128,384]{3,2,1,0:T(8,128)(2,1)} %get-tuple-element.166.q_ref, bf16[8,2,128,384]{3,2,1,0:T(8,128)(2,1)} %get-tuple-element.167.k_ref, ...), custom_call_target="tpu_custom_call" | custom-call | flops 1900000000 | bytes 10000000 | tf_op jit(solution)/shard_map/pallas_call | solution.py:1100
  129.5 12.3 %shard_map.309 = (f32[512,768]{1,0:T(8,128)}, f32[512,1]{1,0:T(8,128)}, bf16[512,768]{1,0:T(8,128)(2,1)}, bf16[512,1536]{1,0:T(8,128)(2,1)}, bf16[512,1536]{1,0:...) custom-call(bf16[8,2,128,768]{3,2,1,0:T(8,128)(2,1)} %get-tuple-element.162.refs_0_.x_, ...), custom_call_target="tpu_custom_call" | custom-call | flops 2500000000 | bytes 16000000 | tf_op jit(solution)/shard_map/pallas_call | solution.py:1122
  145.3 5.1 %shard_map.310 = (bf16[256,768]{1,0:T(8,128)(2,1)}, bf16[512,768]{1,0:T(8,128)(2,1)}, f32[512,768]{1,0:T(8,128)}, f32[8,768]{1,0:T(8,128)}) custom-call(f32[512,768]{1,0:T(8,128)} %get-tuple-element.175.n1_ref, bf16[512,768]{1,0:T(8,128)(2,1)} %get-tuple-element.176.own_ref, bf16[512,768]{1,0:T(8,128)(2,1)} %copy-done.8, bf16[2,128,768]{2,1,0:T(8,128)(2,1)} %bitcast.132, ...), custom_call_target="tpu_custom_call" | custom-call | flops 50000000 | bytes 8000000 | tf_op jit(solution)/shard_map/pallas_call | solution.py:1131
  150.4 5.2 %shard_map.311 = (bf16[384,768]{1,0:T(8,128)(2,1)}, bf16[384,768]{1,0:T(8,128)(2,1)}, bf16[384,768]{1,0:T(8,128)(2,1)}, bf16[384,768]{1,0:T(8,128)(2,1)}) custom-call(bf16[512,1536]{1,0:T(8,128)(2,1)} %get-tuple-element.180.act_ref, bf16[512,768]{1,0:T(8,128)(2,1)} %get-tuple-element.185.df_ref), custom_call_target="tpu_custom_call" | custom-call | flops 1200000000 | bytes 6000000 | tf_op jit(solution)/shard_map/pallas_call | solution.py:1141
  157.8 8.3 %shard_map.312 = (bf16[512,1536]{1,0:T(8,128)(2,1)}, bf16[512,768]{1,0:T(8,128)(2,1)}, f32[1,1536]{1,0:T(1,128)}) custom-call(bf16[512,768]{1,0:T(8,128)(2,1)} %get-tuple-element.185.df_ref, bf16[512,1536]{1,0:T(8,128)(2,1)} %get-tuple-element.186.slope_ref, bf16[768,1536]{1,0:T(8,128)(2,1)} %get-tuple-element.187.w1_ref, ...), custom_call_target="tpu_custom_call" | custom-call | flops 2400000000 | bytes 9000000 | tf_op jit(solution)/shard_map/pallas_call | solution.py:1150
  166.2 4.8 %shard_map.313 = bf16[768,1536]{1,0:T(8,128)(2,1)} custom-call(bf16[512,768]{1,0:T(8,128)(2,1)} %get-tuple-element.190.low_ref, bf16[512,1536]{1,0:T(8,128)(2,1)} %get-tuple-element.191.du_ref), custom_call_target="tpu_custom_call" | custom-call | flops 1200000000 | bytes 6000000 | tf_op jit(solution)/shard_map/pallas_call | solution.py:1157
  177.7 5.3 %shard_map.314 = (f32[256,768]{1,0:T(8,128)}, bf16[512,768]{1,0:T(8,128)(2,1)}, bf16[512,384]{1,0:T(8,128)(2,1)}, bf16[2,384,256]{2,1,0:T(8,128)(2,1)}, f32[8,768]{1,0:T(8,128)}) custom-call(f32[512,768]{1,0:T(8,128)} %get-tuple-element.178.dz_ref, bf16[512,768]{1,0:T(8,128)(2,1)} %get-tuple-element.196.own_ref, bf16[512,768]{1,0:T(8,128)(2,1)} %copy-done.11, ...), custom_call_target="tpu_custom_call" | custom-call | flops 300000000 | bytes 10000000 | tf_op jit(solution)/shard_map/pallas_call | solution.py:1163
  186.2 3.2 %collective-permute-start.29 = (bf16[48,1536]{1,0:T(8,128)(2,1)S(1)}, bf16[48,1536]{1,0:T(8,128)(2,1)S(1)}, u32[]{:S(2)}, u32[]{:S(2)}) collective-permute-start(bf16[48,1536]{1,0:T(8,128)(2,1)S(1)} %pad_maximum_fusion.9), channel_id=1, source_target_pairs={{0,6},{1,7},{2,4},{3,5},{4,2},{5,3},{6,0},{7,1},{8,14},{9,15},{10,... | collective-permute-start | bytes 442376 | tf_op jit(solution)/shard_map/ppermute | solution.py:391
  189.4 4.4 %collective-permute-start.28 = (bf16[48,1536]{1,0:T(8,128)(2,1)S(1)}, bf16[48,1536]{1,0:T(8,128)(2,1)S(1)}, u32[]{:S(2)}, u32[]{:S(2)}) collective-permute-start(bf16[48,1536]{1,0:T(8,128)(2,1)S(1)} %pad_maximum_fusion.8), channel_id=1, source_target_pairs={{0,4},{1,5},{2,6},{3,7},{4,0},{5,1},{6,2},{7,3},{8,12},{9,13},{10,... | collective-permute-start | bytes 442376 | tf_op jit(solution)/shard_map/ppermute | solution.py:391
  193.9 11.6 %shard_map.315 = (bf16[2,128,384]{2,1,0:T(8,128)(2,1)}, bf16[8,128,384]{2,1,0:T(8,128)(2,1)}, bf16[8,128,384]{2,1,0:T(8,128)(2,1)}, bf16[4,128,768]{2,1,0:T(8,12...) custom-call(bf16[2,2,128,384]{3,2,1,0:T(8,128)(2,1)} %get-tuple-element.166.q_ref, ...), custom_call_target="tpu_custom_call" | custom-call | flops 3400000000 | bytes 10000000 | tf_op jit(solution)/shard_map/pallas_call | solution.py:1173
  205.6 11.7 %shard_map.316 = (bf16[2,128,384]{2,1,0:T(8,128)(2,1)}, bf16[8,128,384]{2,1,0:T(8,128)(2,1)}, bf16[8,128,384]{2,1,0:T(8,128)(2,1)}, bf16[4,128,768]{2,1,0:T(8,12...) custom-call(bf16[2,2,128,384]{3,2,1,0:T(8,128)(2,1)} %get-tuple-element.166.q_ref, ...), custom_call_target="tpu_custom_call" | custom-call | flops 3400000000 | bytes 10000000 | tf_op jit(solution)/shard_map/pallas_call | solution.py:1173
  229.3 9.6 %shard_map.317 = (bf16[448,768]{1,0:T(8,128)(2,1)}, bf16[448,768]{1,0:T(8,128)(2,1)}, bf16[448,768]{1,0:T(8,128)(2,1)}, bf16[448,768]{1,0:T(8,128)(2,1)}) custom-call(bf16[8,2,128,768]{3,2,1,0:T(8,128)(2,1)} %get-tuple-element.162.refs_0_.x_ref, bf16[2,128,384]{2,1,0:T(8,128)(2,1)} %get-tuple-element.211.refs_0_, ...), custom_call_target="tpu_custom_call" | custom-call | flops 3300000000 | bytes 12000000 | tf_op jit(solution)/shard_map/pallas_call | solution.py:1219
  246.3 6.7 %collective-permute-start.41 = (bf16[128,768]{1,0:T(8,128)(2,1)}, bf16[128,768]{1,0:T(8,128)(2,1)S(1)}, u32[]{:S(2)}, u32[]{:S(2)}) collective-permute-start(bf16[128,768]{1,0:T(8,128)(2,1)} %get-tuple-element.322), channel_id=1, source_target_pairs={{0,2},{1,3},{2,0},{3,1},{4,6},{5,7},{6,4},{7,5},{8,10},{9,11},{10,... | collective-permute-start | bytes 589832 | tf_op jit(solution)/shard_map/ppermute | solution.py:391
  262.4 6.6 %collective-permute-done.45 = bf16[224,768]{1,0:T(8,128)(2,1)S(1)} collective-permute-done((bf16[224,768]{1,0:T(8,128)(2,1)S(1)}, bf16[224,768]{1,0:T(8,128)(2,1)S(1)}, u32[]{:S(2)}, u32[]{:S(2)}) %collective-permute-start.45) | collective-permute-done | bytes 344096 | tf_op jit(solution)/shard_map/ppermute | solution.py:391
  271.3 4.4 %collective-permute-start.47 = (bf16[56,1536]{1,0:T(8,128)(2,1)S(1)}, bf16[56,1536]{1,0:T(8,128)(2,1)}, u32[]{:S(2)}, u32[]{:S(2)}) collective-permute-start(bf16[56,1536]{1,0:T(8,128)(2,1)S(1)} %maximum_maximum_fusion.1), channel_id=1, source_target_pairs={{0,4},{1,5},{2,6},{3,7},{4,0},{5,1},{6,2},{7,3},{8,12},{9,13},{10,... | collective-permute-start | bytes 516104 | tf_op jit(solution)/shard_map/ppermute | solution.py:391
  278.4 9.0 %collective-permute-done.47.refs_1_ = bf16[56,1536]{1,0:T(8,128)(2,1)} collective-permute-done((bf16[56,1536]{1,0:T(8,128)(2,1)S(1)}, bf16[56,1536]{1,0:T(8,128)(2,1)}, u32[]{:S(2)}, u32[]{:S(2)}) %collective-permute-start.47) | collective-permute-done | bytes 172064 | tf_op jit(solution)/shard_map/ppermute | solution.py:391
  (289 shorter events, 107.2 us)
Async XLA Ops:
  7.2 75.4 %all-gather.2.cloned.1.call-start = ((), (), s32[]{:S(2)}) async-start(), calls=%async_computation.1 | async-start | bytes 3440640 | tf_op jit(solution)/shard_map/all_gather | solution.py:442
  18.8 15.8 %collective-permute-start.4 = (bf16[56,1536]{1,0:T(8,128)(2,1)}, bf16[56,1536]{1,0:T(8,128)(2,1)S(1)}, u32[]{:S(2)}, u32[]{:S(2)}) collective-permute-start(bf16[56,1536]{1,0:T(8,128)(2,1)} %shard_map.306), channel_id=1, source_target_pairs={{0,4},{1,5},{2,6},{3,7},{4,0},{5,1},{6,2},{7,3},{8,12},{9,13},{10,... | collective-permute-start | bytes 516104 | tf_op jit(solution)/shard_map/ppermute | solution.py:391
  36.3 187.4 %reduce-scatter.2.cloned.1.call-start = ((), (), s32[]{:S(2)}) async-start(), calls=%async_computation.2 | async-start | bytes 2949120 | tf_op jit(solution)/shard_map/reduce_scatter | solution.py:1158
  42.1 23.5 %collective-permute-start.7 = (bf16[48,3072]{1,0:T(8,128)(2,1)S(1)}, bf16[48,3072]{1,0:T(8,128)(2,1)S(1)}, u32[]{:S(2)}, u32[]{:S(2)}) collective-permute-start(bf16[48,3072]{1,0:T(8,128)(2,1)S(1)} %pad_maximum_fusion.4), channel_id=1, source_target_pairs={{0,4},{1,5},{2,6},{3,7},{4,0},{5,1},{6,2},{7,3},{8,12},{9,13},{10,... | collective-permute-start | bytes 884744 | tf_op jit(solution)/shard_map/ppermute | solution.py:391
  43.1 22.5 %collective-permute-start.8 = (bf16[48,3072]{1,0:T(8,128)(2,1)S(1)}, bf16[48,3072]{1,0:T(8,128)(2,1)S(1)}, u32[]{:S(2)}, u32[]{:S(2)}) collective-permute-start(bf16[48,3072]{1,0:T(8,128)(2,1)S(1)} %pad_maximum_fusion.4), channel_id=1, source_target_pairs={{0,6},{1,7},{2,4},{3,5},{4,2},{5,3},{6,0},{7,1},{8,14},{9,15},{10,... | collective-permute-start | bytes 884744 | tf_op jit(solution)/shard_map/ppermute | solution.py:391
  65.6 23.2 %collective-permute-start.10 = (bf16[2,128,768]{2,1,0:T(8,128)(2,1)}, bf16[2,128,768]{2,1,0:T(8,128)(2,1)S(1)}, u32[]{:S(2)}, u32[]{:S(2)}) collective-permute-start(bf16[2,128,768]{2,1,0:T(8,128)(2,1)} %bitcast.9.refs_0_), channel_id=1, source_target_pairs={{0,4},{1,5},{2,6},{3,7},{4,0},{5,1},{6,2},{7,3},{8,12},{9,13},{10,... | collective-permute-start | bytes 1179656 | tf_op jit(solution)/shard_map/ppermute | solution.py:391
  71.7 18.4 %collective-permute-start.11 = (bf16[2,128,768]{2,1,0:T(8,128)(2,1)}, bf16[2,128,768]{2,1,0:T(8,128)(2,1)}, u32[]{:S(2)}, u32[]{:S(2)}) collective-permute-start(bf16[2,128,768]{2,1,0:T(8,128)(2,1)} %bitcast.9.refs_0_), channel_id=1, source_target_pairs={{2,4},{3,5},{4,2},{5,3},{10,12},{11,13},{12,10},{13,11},{18,20},{1... | collective-permute-start | bytes 1179656 | tf_op jit(solution)/shard_map/ppermute | solution.py:391
  73.1 17.0 %collective-permute-start.9 = (bf16[2,128,768]{2,1,0:T(8,128)(2,1)}, bf16[2,128,768]{2,1,0:T(8,128)(2,1)}, u32[]{:S(2)}, u32[]{:S(2)}) collective-permute-start(bf16[2,128,768]{2,1,0:T(8,128)(2,1)} %bitcast.9.refs_0_), channel_id=1, source_target_pairs={{0,2},{1,3},{2,0},{3,1},{4,6},{5,7},{6,4},{7,5},{8,10},{9,11},{10,... | collective-permute-start | bytes 1179656 | tf_op jit(solution)/shard_map/ppermute | solution.py:391
  74.4 17.0 %collective-permute-start.13 = (bf16[192,1536]{1,0:T(8,128)(2,1)S(1)}, bf16[192,1536]{1,0:T(8,128)(2,1)S(1)}, u32[]{:S(2)}, u32[]{:S(2)}) collective-permute-start(bf16[192,1536]{1,0:T(8,128)(2,1)S(1)} %pad_maximum_fusion.2.refs_9_), channel_id=1, source_target_pairs={{0,16},{1,17},{2,18},{3,19},{4,20},{5,21},{6,22},{7,23},{8,24},{9,... | collective-permute-start | bytes 1769480 | tf_op jit(solution)/shard_map/ppermute | solution.py:391
  76.0 15.5 %collective-permute-start.12 = (bf16[192,1536]{1,0:T(8,128)(2,1)S(1)}, bf16[192,1536]{1,0:T(8,128)(2,1)}, u32[]{:S(2)}, u32[]{:S(2)}) collective-permute-start(bf16[192,1536]{1,0:T(8,128)(2,1)S(1)} %pad_maximum_fusion.1.refs_5_), channel_id=1, source_target_pairs={{0,8},{1,9},{2,10},{3,11},{4,12},{5,13},{6,14},{7,15},{8,0},{9,1},... | collective-permute-start | bytes 1769480 | tf_op jit(solution)/shard_map/ppermute | solution.py:391
  93.1 16.4 %collective-permute-start.17 = (bf16[192,1536]{1,0:T(8,128)(2,1)S(1)}, bf16[192,1536]{1,0:T(8,128)(2,1)}, u32[]{:S(2)}, u32[]{:S(2)}) collective-permute-start(bf16[192,1536]{1,0:T(8,128)(2,1)S(1)} %pad_maximum_fusion.2.refs_9_), channel_id=1, source_target_pairs={{0,8},{1,9},{2,10},{3,11},{4,12},{5,13},{6,14},{7,15},{8,0},{9,1},... | collective-permute-start | bytes 1769480 | tf_op jit(solution)/shard_map/ppermute | solution.py:391
  155.6 15.6 %collective-permute-start.22 = (bf16[384,768]{1,0:T(8,128)(2,1)}, bf16[384,768]{1,0:T(8,128)(2,1)S(1)}, u32[]{:S(2)}, u32[]{:S(2)}) collective-permute-start(bf16[384,768]{1,0:T(8,128)(2,1)} %get-tuple-element.182), channel_id=1, source_target_pairs={{0,16},{1,17},{2,18},{3,19},{4,20},{5,21},{6,22},{7,23},{8,24},{9,... | collective-permute-start | bytes 1769480 | tf_op jit(solution)/shard_map/ppermute | solution.py:391
  176.5 50.7 %collective-permute-start.31 = (bf16[2,384,256]{2,1,0:T(8,128)(2,1)}, bf16[2,384,256]{2,1,0:T(8,128)(2,1)}, u32[]{:S(2)}, u32[]{:S(2)}) collective-permute-start(bf16[2,384,256]{2,1,0:T(8,128)(2,1)} %get-tuple-element.230), channel_id=1, source_target_pairs={{0,1},{1,0},{2,3},{3,2},{4,5},{5,4},{6,7},{7,6},{8,9},{9,8},{10,11... | collective-permute-start | bytes 1179656 | tf_op jit(solution)/shard_map/ppermute | solution.py:391
  186.2 33.3 %collective-permute-start.29 = (bf16[48,1536]{1,0:T(8,128)(2,1)S(1)}, bf16[48,1536]{1,0:T(8,128)(2,1)S(1)}, u32[]{:S(2)}, u32[]{:S(2)}) collective-permute-start(bf16[48,1536]{1,0:T(8,128)(2,1)S(1)} %pad_maximum_fusion.9), channel_id=1, source_target_pairs={{0,6},{1,7},{2,4},{3,5},{4,2},{5,3},{6,0},{7,1},{8,14},{9,15},{10,... | collective-permute-start | bytes 442376 | tf_op jit(solution)/shard_map/ppermute | solution.py:391
  189.4 30.6 %collective-permute-start.28 = (bf16[48,1536]{1,0:T(8,128)(2,1)S(1)}, bf16[48,1536]{1,0:T(8,128)(2,1)S(1)}, u32[]{:S(2)}, u32[]{:S(2)}) collective-permute-start(bf16[48,1536]{1,0:T(8,128)(2,1)S(1)} %pad_maximum_fusion.8), channel_id=1, source_target_pairs={{0,4},{1,5},{2,6},{3,7},{4,0},{5,1},{6,2},{7,3},{8,12},{9,13},{10,... | collective-permute-start | bytes 442376 | tf_op jit(solution)/shard_map/ppermute | solution.py:391
  193.8 26.2 %collective-permute-start.27 = (bf16[48,1536]{1,0:T(8,128)(2,1)S(1)}, bf16[48,1536]{1,0:T(8,128)(2,1)S(1)}, u32[]{:S(2)}, u32[]{:S(2)}) collective-permute-start(bf16[48,1536]{1,0:T(8,128)(2,1)S(1)} %pad_maximum_fusion.7), channel_id=1, source_target_pairs={{0,2},{1,3},{2,0},{3,1},{4,6},{5,7},{6,4},{7,5},{8,10},{9,11},{10,... | collective-permute-start | bytes 442376 | tf_op jit(solution)/shard_map/ppermute | solution.py:391
  219.5 19.4 %collective-permute-start.40 = (bf16[4,128,768]{2,1,0:T(8,128)(2,1)}, bf16[4,128,768]{2,1,0:T(8,128)(2,1)S(1)}, u32[]{:S(2)}, u32[]{:S(2)}) collective-permute-start(bf16[4,128,768]{2,1,0:T(8,128)(2,1)} %get-tuple-element.246), channel_id=1, source_target_pairs={{0,1},{1,0},{2,3},{3,2},{4,5},{5,4},{6,7},{7,6},{8,9},{9,8},{10,11... | collective-permute-start | bytes 2359304 | tf_op jit(solution)/shard_map/ppermute | solution.py:391
  220.9 25.4 %collective-permute-start.34 = (bf16[128,768]{1,0:T(8,128)(2,1)}, bf16[128,768]{1,0:T(8,128)(2,1)S(1)}, u32[]{:S(2)}, u32[]{:S(2)}) collective-permute-start(bf16[128,768]{1,0:T(8,128)(2,1)} %get-tuple-element.327), channel_id=1, source_target_pairs={{0,2},{1,3},{2,0},{3,1},{4,6},{5,7},{6,4},{7,5},{8,10},{9,11},{10,... | collective-permute-start | bytes 589832 | tf_op jit(solution)/shard_map/ppermute | solution.py:391
  239.0 16.8 %collective-permute-start.32 = (bf16[448,768]{1,0:T(8,128)(2,1)}, bf16[448,768]{1,0:T(8,128)(2,1)}, u32[]{:S(2)}, u32[]{:S(2)}) collective-permute-start(bf16[448,768]{1,0:T(8,128)(2,1)} %get-tuple-element.238), channel_id=1, source_target_pairs={{0,16},{1,17},{2,18},{3,19},{4,20},{5,21},{6,22},{7,23},{8,24},{9,... | collective-permute-start | bytes 2064392 | tf_op jit(solution)/shard_map/ppermute | solution.py:391
  239.7 16.3 %collective-permute-start.33 = (bf16[448,768]{1,0:T(8,128)(2,1)}, bf16[448,768]{1,0:T(8,128)(2,1)}, u32[]{:S(2)}, u32[]{:S(2)}) collective-permute-start(bf16[448,768]{1,0:T(8,128)(2,1)} %get-tuple-element.240), channel_id=1, source_target_pairs={{0,8},{1,9},{2,10},{3,11},{4,12},{5,13},{6,14},{7,15},{8,0},{9,1},... | collective-permute-start | bytes 2064392 | tf_op jit(solution)/shard_map/ppermute | solution.py:391
  246.3 29.4 %collective-permute-start.41 = (bf16[128,768]{1,0:T(8,128)(2,1)}, bf16[128,768]{1,0:T(8,128)(2,1)S(1)}, u32[]{:S(2)}, u32[]{:S(2)}) collective-permute-start(bf16[128,768]{1,0:T(8,128)(2,1)} %get-tuple-element.322), channel_id=1, source_target_pairs={{0,2},{1,3},{2,0},{3,1},{4,6},{5,7},{6,4},{7,5},{8,10},{9,11},{10,... | collective-permute-start | bytes 589832 | tf_op jit(solution)/shard_map/ppermute | solution.py:391
  253.1 22.8 %collective-permute-start.42 = (bf16[128,768]{1,0:T(8,128)(2,1)}, bf16[128,768]{1,0:T(8,128)(2,1)S(1)}, u32[]{:S(2)}, u32[]{:S(2)}) collective-permute-start(bf16[128,768]{1,0:T(8,128)(2,1)} %get-tuple-element.324), channel_id=1, source_target_pairs={{0,4},{1,5},{2,6},{3,7},{4,0},{5,1},{6,2},{7,3},{8,12},{9,13},{10,... | collective-permute-start | bytes 589832 | tf_op jit(solution)/shard_map/ppermute | solution.py:391
  254.6 21.2 %collective-permute-start.43 = (bf16[128,768]{1,0:T(8,128)(2,1)}, bf16[128,768]{1,0:T(8,128)(2,1)S(1)}, u32[]{:S(2)}, u32[]{:S(2)}) collective-permute-start(bf16[128,768]{1,0:T(8,128)(2,1)} %get-tuple-element.323), channel_id=1, source_target_pairs={{2,4},{3,5},{4,2},{5,3},{10,12},{11,13},{12,10},{13,11},{18,20},{1... | collective-permute-start | bytes 589832 | tf_op jit(solution)/shard_map/ppermute | solution.py:391
  271.3 16.0 %collective-permute-start.47 = (bf16[56,1536]{1,0:T(8,128)(2,1)S(1)}, bf16[56,1536]{1,0:T(8,128)(2,1)}, u32[]{:S(2)}, u32[]{:S(2)}) collective-permute-start(bf16[56,1536]{1,0:T(8,128)(2,1)S(1)} %maximum_maximum_fusion.1), channel_id=1, source_target_pairs={{0,4},{1,5},{2,6},{3,7},{4,0},{5,1},{6,2},{7,3},{8,12},{9,13},{10,... | collective-permute-start | bytes 516104 | tf_op jit(solution)/shard_map/ppermute | solution.py:391
  (66 other events, 514.1 us)
Sparse Core Ops, SparseCore 0:
  36.4 46.1 all-gather.1
  176.7 39.6 reduce-scatter.1

commit v4 on v3

--- a/solution.py
+++ b/solution.py
@@ -541,7 +541,8 @@
 def project_kernel(*refs):
     xs, theirs, rows = refs[0:5], refs[5], refs[6]
     bq_ref, bv_ref = refs[7:9]
-    q_ref, k_ref, v_ref, w_ref, x_ref, sems = refs[9:]
+    q_ref, k_out, v_out, w_out, x_out, k_ref, v_ref, w_ref, x_ref, sems = refs[9:]
+    stores = [pltpu.make_async_copy(w_ref, w_out, sems.at[40]), pltpu.make_async_copy(x_ref, x_out, sems.at[41])]
     slots = [*zip((0, 1, 2, 4, 6), xs), *((2 * z + 3, theirs.at[z]) for z in range(3))]
     loads = [pltpu.make_async_copy(ref, x_ref.at[s], sems.at[32 + s]) for s, ref in slots]
     loads += placed(rows, w_ref, sems, 0)
@@ -549,23 +550,29 @@
         c.start()
     for c in loads:
         c.wait()
+    for c in stores:
+        c.start()
     bq, bv = bq_ref[...], bv_ref[...]
 
-    def queries(s, _):
-        x = x_ref[s].reshape(2 * BAND, 768)
-        q = (dot_nn(x, w_ref[:, 0:384]) + bq).astype(BF16) * jnp.asarray(0.125, BF16)
-        q_ref[s] = q.reshape(2, BAND, 384)
-        return 0
-
-    lax.fori_loop(0, 2, queries, 0)
-
-    def slot(s, _):
-        x = x_ref[s].reshape(2 * BAND, 768)
-        k_ref[s] = dot_nn(x, w_ref[:, 384:768]).astype(BF16).reshape(2, BAND, 384)
-        v_ref[s] = (dot_nn(x, w_ref[:, 768:1152]) + bv).astype(BF16).reshape(2, BAND, 384)
-        return 0
-
-    lax.fori_loop(0, 8, slot, 0)
+    q = (dot_nn(x_ref[0:2].reshape(4 * BAND, 768), w_ref[:, 0:384]) + bq).astype(BF16) * jnp.asarray(0.125, BF16)
+    q_ref[...] = q.reshape(2, 2, BAND, 384)
+
+    def slots4(i, _):
+        four = pl.ds(4 * i, 4)
+        both = dot_nn(x_ref[four].reshape(8 * BAND, 768), w_ref[:, 384:1152])
+        k_ref[four] = both[:, :384].astype(BF16).reshape(4, 2, BAND, 384)
+        v_ref[four] = (both[:, 384:] + bv).astype(BF16).reshape(4, 2, BAND, 384)
+        for n, (src, dst) in enumerate(((k_ref, k_out), (v_ref, v_out))):
+            pltpu.make_async_copy(src.at[four], dst.at[four], sems.at[42 + 2 * i + n]).start()
+        return 0
+
+    lax.fori_loop(0, 2, slots4, 0)
+    for i in range(2):
+        for n, (src, dst) in enumerate(((k_ref, k_out), (v_ref, v_out))):
+            four = pl.ds(4 * i, 4)
+            stores.append(pltpu.make_async_copy(src.at[four], dst.at[four], sems.at[42 + 2 * i + n]))
+    for c in stores:
+        c.wait()
 
 
 def fill_mask(mask_ref, kseg_ref, qseg_ref):
@@ -660,7 +667,10 @@
 
 def forward_kernel(*refs):
     x_ref, own_ref, other_ref, vec_ref, b1_ref = refs[0:5]
-    n1_ref, r1_ref, low_ref, act_ref, slope_ref, f_ref, w1_ref, w2_ref, tok_buf, own_buf, other_buf, sems = refs[13:]
+    n1_out, r1_ref, low_out, act_out, slope_out, f_ref, w1_out, w2_out = refs[13:21]
+    n1_ref, low_ref, act_ref, slope_ref, w1_ref, w2_ref, tok_buf, own_buf, other_buf, sems = refs[21:]
+    results = ((n1_ref, n1_out), (low_ref, low_out), (w1_ref, w1_out), (act_ref, act_out), (slope_ref, slope_out), (w2_ref, w2_out))
+    stores = [pltpu.make_async_copy(src, dst, sems.at[51 + i]) for i, (src, dst) in enumerate(results)]
     loads1, loads2 = placed_hidden(refs[5:13], (w1_ref, w2_ref), sems)
     early = [
         pltpu.make_async_copy(src, dst, sems.at[48 + i])
@@ -687,6 +697,8 @@
     lax.fori_loop(0, 4, rows, 0)
     for c in loads1:
         c.wait()
+    for c in stores[:3]:
+        c.start()
 
     def inner(j, _):
         cols = pl.ds(pl.multiple_of(j * 256, 256), 256)
@@ -700,6 +712,8 @@
     lax.fori_loop(0, 6, inner, 0)
     for c in loads2:
         c.wait()
+    for c in stores[3:]:
+        c.start()
 
     def outer(j, _):
         cols = pl.ds(pl.multiple_of(j * 256, 256), 256)
@@ -707,6 +721,8 @@
         return 0
 
     lax.fori_loop(0, 3, outer, 0)
+    for c in stores:
+        c.wait()
 
 
 def middle_kernel(
@@ -746,7 +762,11 @@
     lax.fori_loop(0, 2, other_rows, 0)
 
 
-def hidden_kernel(df_ref, slope_ref, w1_ref, w2_ref, du_ref, dh_ref, db1_ref):
+def hidden_kernel(df_ref, slope_ref, w1_in, w2_ref, du_out, dh_ref, db1_ref, w1_ref, du_ref, sems):
+    load = pltpu.make_async_copy(w1_in, w1_ref, sems.at[0])
+    store = pltpu.make_async_copy(du_ref, du_out, sems.at[1])
+    load.start()
+
     def hidden(j, _):
         cols = pl.ds(pl.multiple_of(j * 256, 256), 256)
         du = (dot_nt(df_ref[...], w2_ref[cols, :]) * slope_ref[:, cols].astype(F32)).astype(BF16)
@@ -755,6 +775,8 @@
         return 0
 
     lax.fori_loop(0, 6, hidden, 0)
+    store.start()
+    load.wait()
 
     def back(j, _):
         cols = pl.ds(pl.multiple_of(j * 256, 256), 256)
@@ -762,6 +784,7 @@
         return 0
 
     lax.fori_loop(0, 3, back, 0)
+    store.wait()
 
 
 def first_kernel(
@@ -802,9 +825,11 @@
 
 
 def attend_back_kernel(
-    q_ref, k_ref, v_ref, mix_ref, da_ref, lse_ref, kseg_ref, qseg_ref, w_ref, dq_ref, dk_ref, dv_ref, own_ref, send_ref, sums_ref,
-    mask_ref,
+    q_ref, k_ref, v_ref, mix_ref, da_ref, lse_ref, kseg_ref, qseg_ref, w_in, dq_ref, dkv_ref, own_ref, send_ref, sums_ref,
+    mask_ref, w_ref, sem,
 ):
+    load = pltpu.make_async_copy(w_in, w_ref, sem)
+    load.start()
     fill_mask(mask_ref, kseg_ref, qseg_ref)
 
     def pair(j, _):
@@ -827,31 +852,30 @@
             dvs.append(dot_nt(p.astype(BF16), da))
             dks.append(dot_nn(ds, qh))
             dqs.append(dot_tn(k, ds))
-        dk_ref[:, :, both] = jnp.concatenate(dks, axis=1).astype(BF16).reshape(8, BAND, 128)
-        dv_ref[:, :, both] = jnp.concatenate(dvs, axis=1).astype(BF16).reshape(8, BAND, 128)
+        later = pl.ds(pl.multiple_of(384 + 128 * j, 128), 128)
+        dkv_ref[:, :, both] = jnp.concatenate(dks, axis=1).astype(BF16).reshape(8, BAND, 128)
+        dkv_ref[:, :, later] = jnp.concatenate(dvs, axis=1).astype(BF16).reshape(8, BAND, 128)
         dq = jnp.transpose(jnp.concatenate(dqs, axis=0) * 0.125)
         dq_ref[:, :, both] = dq.astype(BF16).reshape(2, BAND, 128)
         return 0
 
     lax.fori_loop(0, 3, pair, 0)
 
+    load.wait()
     sums_ref[0:1] = jnp.sum(dq_ref[...].reshape(2 * BAND, 384).astype(F32), axis=0, keepdims=True)
-    sums_ref[1:2] = jnp.sum(dv_ref[...].reshape(8 * BAND, 384).astype(F32), axis=0, keepdims=True)
-
-    def step(z, _):
-        dk = dk_ref[pl.ds(2 * z, 2)].reshape(2 * BAND, 384)
-        dv = dv_ref[pl.ds(2 * z, 2)].reshape(2 * BAND, 384)
-        dx = dot_nt(dk, w_ref[:, 384:768]) + dot_nt(dv, w_ref[:, 768:1152])
-        own_ref[z] = dx[:BAND].astype(BF16)
-        send_ref[z] = dx[BAND:].astype(BF16)
-        return 0
-
-    lax.fori_loop(1, 4, step, 0)
-    dx = dot_nt(dk_ref[0:2].reshape(2 * BAND, 384), w_ref[:, 384:768])
-    dx += dot_nt(dv_ref[0:2].reshape(2 * BAND, 384), w_ref[:, 768:1152])
-    dx += dot_nt(dq_ref[...].reshape(2 * BAND, 384), w_ref[:, 0:384])
-    own_ref[0] = dx[:BAND].astype(BF16)
-    send_ref[0] = dx[BAND:].astype(BF16)
+    sums_ref[1:2] = jnp.sum(dkv_ref[:, :, 384:].reshape(8 * BAND, 384).astype(F32), axis=0, keepdims=True)
+
+    def step(i, _):
+        dx = dot_nt(dkv_ref[pl.ds(4 * i, 4)].reshape(4 * BAND, 768), w_ref[:, 384:1152])
+        for z in range(2):
+            own_ref[2 * i + z] = dx[2 * z * BAND : (2 * z + 1) * BAND].astype(BF16)
+            send_ref[2 * i + z] = dx[(2 * z + 1) * BAND : (2 * z + 2) * BAND].astype(BF16)
+        return 0
+
+    lax.fori_loop(0, 2, step, 0)
+    dx = dot_nt(dq_ref[...].reshape(2 * BAND, 384), w_ref[:, 0:384])
+    own_ref[0] = (own_ref[0].astype(F32) + dx[:BAND]).astype(BF16)
+    send_ref[0] = (send_ref[0].astype(F32) + dx[BAND:]).astype(BF16)
 
 
 def inner_grad_kernel(low_ref, du_ref, out_ref):
@@ -909,8 +933,8 @@
 
 
 def projection_grad_kernel(x_ref, *refs):
-    dqs, dks, dvs, (mix0, mix1, other_ref, half_ref, vec_ref) = refs[0:2], refs[2:4], refs[4:6], refs[6:11]
-    refs = refs[11:]
+    dqs, dkvs, (mix0, mix1, other_ref, half_ref, vec_ref) = refs[0:2], refs[2:4], refs[4:9]
+    refs = refs[9:]
     outs, halves, dwo_ref, sems = refs[:4], refs[4:6], refs[6], refs[7]
     core = my_core()
     half = half_ref[...].reshape(2, 2, BAND, 384)
@@ -926,18 +950,18 @@
         x = [x_ref[:, m, :, cols].reshape(8 * BAND, 384) for m in range(2)]
 
         def total(refs, count):
-            terms = [dot_tn(x[m][: count * BAND], refs[m][...].reshape(count * BAND, 384)) for m in range(2)]
+            terms = [dot_tn(x[m][: count * BAND], refs[m][...].reshape(count * BAND, -1)) for m in range(2)]
             return (terms[0] + terms[1]).astype(BF16)
 
-        dwq, dwk, dwv = total(dqs, 2), total(dks, 8), total(dvs, 8)
+        dwq, dwkv = total(dqs, 2), total(dkvs, 8)
         for i in range(8):
             rows = slice(48 * i, 48 * i + 48)
             dwo = dwo_ref[pl.ds(pl.multiple_of(j * 384 + 48 * i, 16), 48)]
             place_rows(
                 halves,
                 j * 8 + i,
-                jnp.concatenate([dwq[rows], dwk[rows]], axis=1),
-                jnp.concatenate([dwv[rows], dwo], axis=1),
+                jnp.concatenate([dwq[rows], dwkv[rows, :384]], axis=1),
+                jnp.concatenate([dwkv[rows, 384:], dwo], axis=1),
             )
         return 0
 
@@ -1079,7 +1103,14 @@
         [((2, *head_shape), BF16), ((8, *head_shape), BF16), ((8, *head_shape), BF16), ((768, 1536), BF16), ((8, *slot_shape), BF16)],
         9,
         in_specs=[IN_PLACE] * 7 + [IN_VMEM] * 2,
-        scratch=[pltpu.SemaphoreType.DMA((40,))],
+        out_specs=[IN_VMEM] + [IN_PLACE] * 4,
+        scratch=[
+            pltpu.VMEM((8, *head_shape), BF16),
+            pltpu.VMEM((8, *head_shape), BF16),
+            pltpu.VMEM((768, 1536), BF16),
+            pltpu.VMEM((8, *slot_shape), BF16),
+            pltpu.SemaphoreType.DMA((46,)),
+        ],
         cost=(2_800_000_000, 16_000_000),
     )(*slots, square, bq, bv)
     def attention_specs(m=None):
@@ -1124,7 +1155,17 @@
         [((512, 768), F32), ((512, 1), F32), ((512, 768), BF16), ((512, 1536), BF16), ((512, 1536), BF16), ((512, 768), BF16), ((768, 1536), BF16), ((1536, 768), BF16)],
         13,
         in_specs=[IN_PLACE] * 3 + [IN_VMEM] * 2 + [IN_PLACE] * 8,
-        scratch=[pltpu.VMEM((2, *slot_shape), BF16)] * 3 + [pltpu.SemaphoreType.DMA((51,))],
+        out_specs=[IN_PLACE, IN_VMEM, IN_PLACE, IN_PLACE, IN_PLACE, IN_VMEM, IN_PLACE, IN_PLACE],
+        scratch=[
+            pltpu.VMEM((512, 768), F32),
+            pltpu.VMEM((512, 768), BF16),
+            pltpu.VMEM((512, 1536), BF16),
+            pltpu.VMEM((512, 1536), BF16),
+            pltpu.VMEM((768, 1536), BF16),
+            pltpu.VMEM((1536, 768), BF16),
+            *([pltpu.VMEM((2, *slot_shape), BF16)] * 3),
+            pltpu.SemaphoreType.DMA((57,)),
+        ],
         cost=(2_500_000_000, 16_000_000),
     )(x_all, branch, branch_other, vec8, b1, *hidden)
     mix_other = send(after(mix_low, n1), CORE)
@@ -1151,6 +1192,9 @@
         hidden_kernel,
         [((512, 1536), BF16), ((512, 768), BF16), ((1, 1536), F32)],
         4,
+        in_specs=[IN_VMEM, IN_VMEM, IN_PLACE, IN_VMEM],
+        out_specs=[IN_PLACE, IN_VMEM, IN_VMEM],
+        scratch=[pltpu.VMEM((768, 1536), BF16), pltpu.VMEM((512, 1536), BF16), pltpu.SemaphoreType.DMA((2,))],
         cost=(2_400_000_000, 9_000_000),
     )(after(df, *outer_terms), slope, w1, w2)
     dh_other = send(dh_own, CORE)
@@ -1169,15 +1213,15 @@
 
     def back(m, events):
         specs = attention_specs(m)
-        shapes = [(2, BAND, 384), (8, BAND, 384), (8, BAND, 384), (4, BAND, 768), (4, BAND, 768)]
+        shapes = [(2, BAND, 384), (8, BAND, 768), (4, BAND, 768), (4, BAND, 768)]
         return call(
             attend_back_kernel,
             [(shape, BF16) for shape in shapes] + [((8, 384), F32)],
             9,
             grid=(1,),
-            in_specs=specs[0] + specs[1] + specs[2] + [pl.BlockSpec((768, 1536), lambda i: (0, 0))],
+            in_specs=specs[0] + specs[1] + specs[2] + [IN_PLACE],
             out_specs=[pl.BlockSpec(shape, lambda i: (0, 0, 0)) for shape in shapes] + [pl.BlockSpec((8, 384), lambda i: (0, 0))],
-            scratch=[pltpu.VMEM((1024, 256), F32)],
+            scratch=[pltpu.VMEM((1024, 256), F32), pltpu.VMEM((768, 1536), BF16), pltpu.SemaphoreType.DMA],
             cost=(3_400_000_000, 10_000_000),
         )(q, k, v, mix, after(da, *events), lse, kseg, qseg, w_abs)
 
@@ -1189,10 +1233,11 @@
 
     outer_hop, outer_sent = after_both((outer_hop, outer_sent), (da,))
     outer_half = far_terms(outer_hop, outer_sent, 48)
-    *grads0, dx0, dx_send, sums_q0 = back(0, outer_half)
+    *grads0, dx0, dx_send, sums_q0 = back(0, ())
+    got0 = send(dx_send, CORE)
+    outer_half = after_both(outer_half, grads0[:1])
     outer_parts = line_parts(outer_half, 48)
-    got0 = send(dx_send, CORE)
-    *grads1, dx1, dx_send, sums_q1 = back(1, (dx0,))
+    *grads1, dx1, dx_send, sums_q1 = back(1, (dx0, *outer_half))
     outer_parts, got0, dx0 = after_both((outer_parts, got0, dx0), grads1[:1])
     got1 = send(dx_send, CORE)
     low0 = core_sums(dx0, got0)
@@ -1219,11 +1264,11 @@
     square_terms = call(
         projection_grad_kernel,
         [((448, 768), BF16)] * 4,
-        12,
+        10,
         out_specs=[IN_PLACE] * 4,
         scratch=piece + [pltpu.VMEM((768, 384), BF16), pltpu.SemaphoreType.DMA((8,))],
         cost=(3_300_000_000, 12_000_000),
-    )(x_all, grads0[0], grads1[0], grads0[1], grads1[1], grads0[2], grads1[2], mix_low[0], mix_low[1], mix_other, do_half, jnp.concatenate([vec_first, vec_second]))
+    )(x_all, grads0[0], grads1[0], grads0[1], grads1[1], mix_low[0], mix_low[1], mix_other, do_half, jnp.concatenate([vec_first, vec_second]))
     square_hop = first_hop(square_terms)
     inner_parts, got1 = after_both((inner_parts, got1), square_terms)
     sent1 = line_sums(core_sums(dx1, got1))
@@ -1246,6 +1291,7 @@
     )(keep, send(other, CORE))
     squares, small = grads[:4], [g.reshape(-1) for g in grads[4:]]
     dz1 = dz1.reshape(slot_shape)
+    dz1 = dz1.reshape(2, BAND, 768)
     grad_tokens = jnp.stack([add(dz1[m], *sent).astype(BF16) for m, sent in enumerate((sent0, sent1))])
     return (
         result.reshape(2, 1, BAND, 768), grad_tokens[:, None],

time: 301 us -> 298 us (0.990)
  Pallas kernels: 104 us -> 94.5 us
    pallas_call x2, Pallas kernels: 23.2 us -> 20.1 us  [back(): call(attend_back_kernel, [(shape, BF16) for shape in shapes] + [((8, 384)...]
    unnamed x78 -> x80, local copies, waits for them, and re-layouts: 7.88 us -> 8.84 us
  transfers between devices with their start and end apart: 53 -> 53, of which waited for: 26 -> 23; matrix products, arithmetic and copies ran while one was open for 10% -> 11% of each run, Pallas kernels for 25% -> 23%
where the time goes in v4:
time: 298 us; the launch traced here: 296 us
  Pallas kernels  94.5 us (32%)
  waiting for transfers between devices  74.4 us (25%)
  starting transfers between devices  68.9 us (23%)
  local copies, waits for them, and re-layouts  23 us (8%)
  other arithmetic  20 us (7%)
  between operations  15.2 us (5%)
    ppermute x51, waiting for transfers between devices, send(): return lax.ppermute(value, BOTH, route)  69.4 us
    ppermute x51, starting transfers between devices, send(): return lax.ppermute(value, BOTH, route)  68.8 us
    pallas_call x2, Pallas kernels, back(): call(attend_back_kernel, [(shape, BF16) for shape in shapes] + [((8, 384)...  20.1 us
    pallas_call x1, Pallas kernels, per_device_paired(): call(attend_kernel, [((2, 384, 256), F32), ((2, 384, 256), BF16), ((2, 8,...  10.5 us
    pallas_call x1, Pallas kernels, per_device_paired(): call(forward_kernel, [((512, 768), F32), ((512, 1), F32), ((512, 768), BF...  10.4 us
    pallas_call x1, Pallas kernels, per_device_paired(): call(project_kernel, [((2, *head_shape), BF16), ((8, *head_shape), BF16),...  9.07 us
    unnamed x80, local copies, waits for them, and re-layouts  8.84 us
    pallas_call x1, Pallas kernels, per_device_paired(): call(projection_grad_kernel, [((448, 768), BF16)] * 4, 10, out_specs=[IN_...  8.81 us
  transfers between devices with their start and end apart: 53, of which 23 were waited for; matrix products, arithmetic and copies ran while one was open for 11% of the time, Pallas kernels for 23%

profile of v4, /device:TPU:0, one launch (start us, length us, event | category | flops | bytes accessed | tf_op | source)
XLA Modules:
  0.0 296.4 jit_solution(5646761674229369357)
XLA Ops:
  21.4 3.6 %collective-permute-done.3 = bf16[56,1536]{1,0:T(8,128)(2,1)S(1)} collective-permute-done((bf16[56,1536]{1,0:T(8,128)(2,1)}, bf16[56,1536]{1,0:T(8,128)(2,1)S(1)}, u32[]{:S(2)}, u32[]{:S(2)}) %collective-permute-start.3) | collective-permute-done | bytes 172064 | tf_op jit(solution)/shard_map/ppermute | solution.py:391
  25.0 9.5 %collective-permute-done.4 = bf16[56,1536]{1,0:T(8,128)(2,1)S(1)} collective-permute-done((bf16[56,1536]{1,0:T(8,128)(2,1)}, bf16[56,1536]{1,0:T(8,128)(2,1)S(1)}, u32[]{:S(2)}, u32[]{:S(2)}) %collective-permute-start.4) | collective-permute-done | bytes 172064 | tf_op jit(solution)/shard_map/ppermute | solution.py:391
  38.8 3.3 %collective-permute-start.6 = (bf16[48,3072]{1,0:T(8,128)(2,1)S(1)}, bf16[48,3072]{1,0:T(8,128)(2,1)S(1)}, u32[]{:S(2)}, u32[]{:S(2)}) collective-permute-start(bf16[48,3072]{1,0:T(8,128)(2,1)S(1)} %pad_maximum_fusion.4), channel_id=1, source_target_pairs={{0,2},{1,3},{2,0},{3,1},{4,6},{5,7},{6,4},{7,5},{8,10},{9,11},{10,... | collective-permute-start | bytes 884744 | tf_op jit(solution)/shard_map/ppermute | solution.py:391
  45.9 7.8 %collective-permute-done.6 = bf16[48,3072]{1,0:T(8,128)(2,1)S(1)} collective-permute-done((bf16[48,3072]{1,0:T(8,128)(2,1)S(1)}, bf16[48,3072]{1,0:T(8,128)(2,1)S(1)}, u32[]{:S(2)}, u32[]{:S(2)}) %collective-permute-start.6) | collective-permute-done | bytes 294944 | tf_op jit(solution)/shard_map/ppermute | solution.py:391
  53.7 11.9 %collective-permute-done.7 = bf16[48,3072]{1,0:T(8,128)(2,1)S(1)} collective-permute-done((bf16[48,3072]{1,0:T(8,128)(2,1)S(1)}, bf16[48,3072]{1,0:T(8,128)(2,1)S(1)}, u32[]{:S(2)}, u32[]{:S(2)}) %collective-permute-start.7) | collective-permute-done | bytes 294944 | tf_op jit(solution)/shard_map/ppermute | solution.py:391
  65.6 6.1 %collective-permute-start.10 = (bf16[2,128,768]{2,1,0:T(8,128)(2,1)}, bf16[2,128,768]{2,1,0:T(8,128)(2,1)S(1)}, u32[]{:S(2)}, u32[]{:S(2)}) collective-permute-start(bf16[2,128,768]{2,1,0:T(8,128)(2,1)} %bitcast.9.refs_0_), channel_id=1, source_target_pairs={{0,4},{1,5},{2,6},{3,7},{4,0},{5,1},{6,2},{7,3},{8,12},{9,13},{10,... | collective-permute-start | bytes 1179656 | tf_op jit(solution)/shard_map/ppermute | solution.py:391
  77.6 5.0 %all-gather.2.cloned.1.call-done.refs_6_.rows_ref = bf16[896,1536]{1,0:T(8,128)(2,1)} async-done(((bf16[224,1536]{1,0:T(8,128)(2,1)}), bf16[896,1536]{1,0:T(8,128)(2,1)}) %all-gather.2.cloned.1.call-update) | async-done | bytes 2752528 | tf_op jit(solution)/shard_map/all_gather | solution.py:442
  97.7 9.1 %shard_map.307 = (bf16[2,2,128,384]{3,2,1,0:T(8,128)(2,1)}, bf16[8,2,128,384]{3,2,1,0:T(8,128)(2,1)}, bf16[8,2,128,384]{3,2,1,0:T(8,128)(2,1)}, bf16[768,1536]{1,0:T(8,128)(2,1)}, bf16[8,2,128,768]{3,2,1,0:T(8,128)(2,1)}) custom-call(bf16[2,128,768]{2,1,0:T(8,128)(2,1)} %bitcast.9.refs_0_, bf16[2,128,768]{2,1,0:T(8,128)(2,1)} %collective-permute-done.2.refs_1_, ...), custom_call_target="tpu_custom_call" | custom-call | flops 2800000000 | bytes 16000000 | tf_op jit(solution)/shard_map/pallas_call | solution.py:1101
  112.1 10.5 %shard_map.308 = (f32[2,384,256]{2,1,0:T(8,128)}, bf16[2,384,256]{2,1,0:T(8,128)(2,1)}, f32[2,8,256]{2,1,0:T(8,128)}, bf16[2,2,128,768]{3,2,1,0:T(8,128)(2,1)}, bf16[384,768]{1,0:T(8,128)(2,1)}) custom-call(bf16[2,2,128,384]{3,2,1,0:T(8,128)(2,1)} %get-tuple-element.164.q_ref, bf16[8,2,128,384]{3,2,1,0:T(8,128)(2,1)} %get-tuple-element.165.k_ref, ...), custom_call_target="tpu_custom_call" | custom-call | flops 1900000000 | bytes 10000000 | tf_op jit(solution)/shard_map/pallas_call | solution.py:1131
  128.4 10.4 %shard_map.309 = (f32[512,768]{1,0:T(8,128)}, f32[512,1]{1,0:T(8,128)}, bf16[512,768]{1,0:T(8,128)(2,1)}, bf16[512,1536]{1,0:T(8,128)(2,1)}, bf16[512,1536]{1,0:...) custom-call(bf16[8,2,128,768]{3,2,1,0:T(8,128)(2,1)} %get-tuple-element.160.refs_0_.x_, ...), custom_call_target="tpu_custom_call" | custom-call | flops 2500000000 | bytes 16000000 | tf_op jit(solution)/shard_map/pallas_call | solution.py:1153
  142.3 5.1 %shard_map.310 = (bf16[256,768]{1,0:T(8,128)(2,1)}, bf16[512,768]{1,0:T(8,128)(2,1)}, f32[512,768]{1,0:T(8,128)}, f32[8,768]{1,0:T(8,128)}) custom-call(f32[512,768]{1,0:T(8,128)} %get-tuple-element.173.n1_ref, bf16[512,768]{1,0:T(8,128)(2,1)} %get-tuple-element.174.own_ref, bf16[512,768]{1,0:T(8,128)(2,1)} %copy-done.8, bf16[2,128,768]{2,1,0:T(8,128)(2,1)} %bitcast.132, ...), custom_call_target="tpu_custom_call" | custom-call | flops 50000000 | bytes 8000000 | tf_op jit(solution)/shard_map/pallas_call | solution.py:1172
  147.4 5.2 %shard_map.311 = (bf16[384,768]{1,0:T(8,128)(2,1)}, bf16[384,768]{1,0:T(8,128)(2,1)}, bf16[384,768]{1,0:T(8,128)(2,1)}, bf16[384,768]{1,0:T(8,128)(2,1)}) custom-call(bf16[512,1536]{1,0:T(8,128)(2,1)} %get-tuple-element.178.act_ref, bf16[512,768]{1,0:T(8,128)(2,1)} %get-tuple-element.183.df_ref), custom_call_target="tpu_custom_call" | custom-call | flops 1200000000 | bytes 6000000 | tf_op jit(solution)/shard_map/pallas_call | solution.py:1182
  156.6 7.7 %shard_map.312 = (bf16[512,1536]{1,0:T(8,128)(2,1)}, bf16[512,768]{1,0:T(8,128)(2,1)}, f32[1,1536]{1,0:T(1,128)}) custom-call(bf16[512,768]{1,0:T(8,128)(2,1)} %get-tuple-element.183.df_ref, bf16[512,1536]{1,0:T(8,128)(2,1)} %get-tuple-element.184.slope_ref, bf16[768,1536]{1,0:T(8,128)(2,1)} %get-tuple-element.185.w1_in, ...), custom_call_target="tpu_custom_call" | custom-call | flops 2400000000 | bytes 9000000 | tf_op jit(solution)/shard_map/pallas_call | solution.py:1191
  165.7 4.7 %shard_map.313 = bf16[768,1536]{1,0:T(8,128)(2,1)} custom-call(bf16[512,768]{1,0:T(8,128)(2,1)} %get-tuple-element.188.low_ref, bf16[512,1536]{1,0:T(8,128)(2,1)} %get-tuple-element.189.du_ref), custom_call_target="tpu_custom_call" | custom-call | flops 1200000000 | bytes 6000000 | tf_op jit(solution)/shard_map/pallas_call | solution.py:1201
  176.0 5.3 %shard_map.314 = (f32[256,768]{1,0:T(8,128)}, bf16[512,768]{1,0:T(8,128)(2,1)}, bf16[512,384]{1,0:T(8,128)(2,1)}, bf16[2,384,256]{2,1,0:T(8,128)(2,1)}, f32[8,768]{1,0:T(8,128)}) custom-call(f32[512,768]{1,0:T(8,128)} %get-tuple-element.176.dz_ref, bf16[512,768]{1,0:T(8,128)(2,1)} %get-tuple-element.194.own_ref, bf16[512,768]{1,0:T(8,128)(2,1)} %copy-done.11, ...), custom_call_target="tpu_custom_call" | custom-call | flops 300000000 | bytes 10000000 | tf_op jit(solution)/shard_map/pallas_call | solution.py:1207
  182.1 10.2 %shard_map.315 = (bf16[2,128,384]{2,1,0:T(8,128)(2,1)}, bf16[8,128,768]{2,1,0:T(8,128)(2,1)}, bf16[4,128,768]{2,1,0:T(8,128)(2,1)}, bf16[4,128,768]{2,1,0:T(8,128)(2,1)}, f32[8,384]{1,0:T(8,128)}) custom-call(bf16[2,2,128,384]{3,2,1,0:T(8,128)(2,1)} %get-tuple-element.164.q_ref, bf16[8,2,128,384]{3,2,1,0:T(8,128)(2,1)} %get-tuple-element.165.k_ref, ...), custom_call_target="tpu_custom_call" | custom-call | flops 3400000000 | bytes 10000000 | tf_op jit(solution)/shard_map/pallas_call | solution.py:1217
  194.7 3.4 %collective-permute-start.29 = (bf16[48,1536]{1,0:T(8,128)(2,1)S(1)}, bf16[48,1536]{1,0:T(8,128)(2,1)S(1)}, u32[]{:S(2)}, u32[]{:S(2)}) collective-permute-start(bf16[48,1536]{1,0:T(8,128)(2,1)S(1)} %pad_maximum_fusion.9), channel_id=1, source_target_pairs={{0,6},{1,7},{2,4},{3,5},{4,2},{5,3},{6,0},{7,1},{8,14},{9,15},{10,... | collective-permute-start | bytes 442376 | tf_op jit(solution)/shard_map/ppermute | solution.py:391
  198.1 4.4 %collective-permute-start.28 = (bf16[48,1536]{1,0:T(8,128)(2,1)S(1)}, bf16[48,1536]{1,0:T(8,128)(2,1)S(1)}, u32[]{:S(2)}, u32[]{:S(2)}) collective-permute-start(bf16[48,1536]{1,0:T(8,128)(2,1)S(1)} %pad_maximum_fusion.8), channel_id=1, source_target_pairs={{0,4},{1,5},{2,6},{3,7},{4,0},{5,1},{6,2},{7,3},{8,12},{9,13},{10,... | collective-permute-start | bytes 442376 | tf_op jit(solution)/shard_map/ppermute | solution.py:391
  202.6 9.9 %shard_map.316 = (bf16[2,128,384]{2,1,0:T(8,128)(2,1)}, bf16[8,128,768]{2,1,0:T(8,128)(2,1)}, bf16[4,128,768]{2,1,0:T(8,128)(2,1)}, bf16[4,128,768]{2,1,0:T(8,128)(2,1)}, f32[8,384]{1,0:T(8,128)}) custom-call(bf16[2,2,128,384]{3,2,1,0:T(8,128)(2,1)} %get-tuple-element.164.q_ref, bf16[8,2,128,384]{3,2,1,0:T(8,128)(2,1)} %get-tuple-element.165.k_ref, ...), custom_call_target="tpu_custom_call" | custom-call | flops 3400000000 | bytes 10000000 | tf_op jit(solution)/shard_map/pallas_call | solution.py:1217
  224.2 8.8 %shard_map.317 = (bf16[448,768]{1,0:T(8,128)(2,1)}, bf16[448,768]{1,0:T(8,128)(2,1)}, bf16[448,768]{1,0:T(8,128)(2,1)}, bf16[448,768]{1,0:T(8,128)(2,1)}) custom-call(bf16[8,2,128,768]{3,2,1,0:T(8,128)(2,1)} %get-tuple-element.160.refs_0_.x_ref, bf16[2,128,384]{2,1,0:T(8,128)(2,1)} %get-tuple-element.202.refs_0_, ...), custom_call_target="tpu_custom_call" | custom-call | flops 3300000000 | bytes 12000000 | tf_op jit(solution)/shard_map/pallas_call | solution.py:1264
  241.2 8.5 %collective-permute-start.41 = (bf16[128,768]{1,0:T(8,128)(2,1)}, bf16[128,768]{1,0:T(8,128)(2,1)S(1)}, u32[]{:S(2)}, u32[]{:S(2)}) collective-permute-start(bf16[128,768]{1,0:T(8,128)(2,1)} %get-tuple-element.318), channel_id=1, source_target_pairs={{0,2},{1,3},{2,0},{3,1},{4,6},{5,7},{6,4},{7,5},{8,10},{9,11},{10,... | collective-permute-start | bytes 589832 | tf_op jit(solution)/shard_map/ppermute | solution.py:391
  257.3 7.6 %collective-permute-done.45 = bf16[224,768]{1,0:T(8,128)(2,1)S(1)} collective-permute-done((bf16[224,768]{1,0:T(8,128)(2,1)S(1)}, bf16[224,768]{1,0:T(8,128)(2,1)S(1)}, u32[]{:S(2)}, u32[]{:S(2)}) %collective-permute-start.45) | collective-permute-done | bytes 344096 | tf_op jit(solution)/shard_map/ppermute | solution.py:391
  267.9 4.3 %collective-permute-start.47 = (bf16[56,1536]{1,0:T(8,128)(2,1)S(1)}, bf16[56,1536]{1,0:T(8,128)(2,1)}, u32[]{:S(2)}, u32[]{:S(2)}) collective-permute-start(bf16[56,1536]{1,0:T(8,128)(2,1)S(1)} %maximum_maximum_fusion.1), channel_id=1, source_target_pairs={{0,4},{1,5},{2,6},{3,7},{4,0},{5,1},{6,2},{7,3},{8,12},{9,13},{10,... | collective-permute-start | bytes 516104 | tf_op jit(solution)/shard_map/ppermute | solution.py:391
  274.2 9.4 %collective-permute-done.47.refs_1_ = bf16[56,1536]{1,0:T(8,128)(2,1)} collective-permute-done((bf16[56,1536]{1,0:T(8,128)(2,1)S(1)}, bf16[56,1536]{1,0:T(8,128)(2,1)}, u32[]{:S(2)}, u32[]{:S(2)}) %collective-permute-start.47) | collective-permute-done | bytes 172064 | tf_op jit(solution)/shard_map/ppermute | solution.py:391
  (291 shorter events, 109.4 us)
Async XLA Ops:
  7.2 75.4 %all-gather.2.cloned.1.call-start = ((), (), s32[]{:S(2)}) async-start(), calls=%async_computation.1 | async-start | bytes 3440640 | tf_op jit(solution)/shard_map/all_gather | solution.py:442
  36.3 182.3 %reduce-scatter.2.cloned.1.call-start = ((), (), s32[]{:S(2)}) async-start(), calls=%async_computation.2 | async-start | bytes 2949120 | tf_op jit(solution)/shard_map/reduce_scatter | solution.py:1202
  42.1 23.5 %collective-permute-start.7 = (bf16[48,3072]{1,0:T(8,128)(2,1)S(1)}, bf16[48,3072]{1,0:T(8,128)(2,1)S(1)}, u32[]{:S(2)}, u32[]{:S(2)}) collective-permute-start(bf16[48,3072]{1,0:T(8,128)(2,1)S(1)} %pad_maximum_fusion.4), channel_id=1, source_target_pairs={{0,4},{1,5},{2,6},{3,7},{4,0},{5,1},{6,2},{7,3},{8,12},{9,13},{10,... | collective-permute-start | bytes 884744 | tf_op jit(solution)/shard_map/ppermute | solution.py:391
  43.1 22.5 %collective-permute-start.8 = (bf16[48,3072]{1,0:T(8,128)(2,1)S(1)}, bf16[48,3072]{1,0:T(8,128)(2,1)S(1)}, u32[]{:S(2)}, u32[]{:S(2)}) collective-permute-start(bf16[48,3072]{1,0:T(8,128)(2,1)S(1)} %pad_maximum_fusion.4), channel_id=1, source_target_pairs={{0,6},{1,7},{2,4},{3,5},{4,2},{5,3},{6,0},{7,1},{8,14},{9,15},{10,... | collective-permute-start | bytes 884744 | tf_op jit(solution)/shard_map/ppermute | solution.py:391
  65.6 23.2 %collective-permute-start.10 = (bf16[2,128,768]{2,1,0:T(8,128)(2,1)}, bf16[2,128,768]{2,1,0:T(8,128)(2,1)S(1)}, u32[]{:S(2)}, u32[]{:S(2)}) collective-permute-start(bf16[2,128,768]{2,1,0:T(8,128)(2,1)} %bitcast.9.refs_0_), channel_id=1, source_target_pairs={{0,4},{1,5},{2,6},{3,7},{4,0},{5,1},{6,2},{7,3},{8,12},{9,13},{10,... | collective-permute-start | bytes 1179656 | tf_op jit(solution)/shard_map/ppermute | solution.py:391
  71.7 18.4 %collective-permute-start.11 = (bf16[2,128,768]{2,1,0:T(8,128)(2,1)}, bf16[2,128,768]{2,1,0:T(8,128)(2,1)}, u32[]{:S(2)}, u32[]{:S(2)}) collective-permute-start(bf16[2,128,768]{2,1,0:T(8,128)(2,1)} %bitcast.9.refs_0_), channel_id=1, source_target_pairs={{2,4},{3,5},{4,2},{5,3},{10,12},{11,13},{12,10},{13,11},{18,20},{1... | collective-permute-start | bytes 1179656 | tf_op jit(solution)/shard_map/ppermute | solution.py:391
  73.1 17.0 %collective-permute-start.9 = (bf16[2,128,768]{2,1,0:T(8,128)(2,1)}, bf16[2,128,768]{2,1,0:T(8,128)(2,1)}, u32[]{:S(2)}, u32[]{:S(2)}) collective-permute-start(bf16[2,128,768]{2,1,0:T(8,128)(2,1)} %bitcast.9.refs_0_), channel_id=1, source_target_pairs={{0,2},{1,3},{2,0},{3,1},{4,6},{5,7},{6,4},{7,5},{8,10},{9,11},{10,... | collective-permute-start | bytes 1179656 | tf_op jit(solution)/shard_map/ppermute | solution.py:391
  74.4 17.0 %collective-permute-start.13 = (bf16[192,1536]{1,0:T(8,128)(2,1)S(1)}, bf16[192,1536]{1,0:T(8,128)(2,1)S(1)}, u32[]{:S(2)}, u32[]{:S(2)}) collective-permute-start(bf16[192,1536]{1,0:T(8,128)(2,1)S(1)} %pad_maximum_fusion.2.refs_9_), channel_id=1, source_target_pairs={{0,16},{1,17},{2,18},{3,19},{4,20},{5,21},{6,22},{7,23},{8,24},{9,... | collective-permute-start | bytes 1769480 | tf_op jit(solution)/shard_map/ppermute | solution.py:391
  152.7 17.8 %collective-permute-start.22 = (bf16[384,768]{1,0:T(8,128)(2,1)}, bf16[384,768]{1,0:T(8,128)(2,1)S(1)}, u32[]{:S(2)}, u32[]{:S(2)}) collective-permute-start(bf16[384,768]{1,0:T(8,128)(2,1)} %get-tuple-element.180), channel_id=1, source_target_pairs={{0,16},{1,17},{2,18},{3,19},{4,20},{5,21},{6,22},{7,23},{8,24},{9,... | collective-permute-start | bytes 1769480 | tf_op jit(solution)/shard_map/ppermute | solution.py:391
  154.2 16.3 %collective-permute-start.23 = (bf16[384,768]{1,0:T(8,128)(2,1)}, bf16[384,768]{1,0:T(8,128)(2,1)S(1)}, u32[]{:S(2)}, u32[]{:S(2)}) collective-permute-start(bf16[384,768]{1,0:T(8,128)(2,1)} %get-tuple-element.182), channel_id=1, source_target_pairs={{0,8},{1,9},{2,10},{3,11},{4,12},{5,13},{6,14},{7,15},{8,0},{9,1},... | collective-permute-start | bytes 1769480 | tf_op jit(solution)/shard_map/ppermute | solution.py:391
  156.6 65.7 %collective-permute-start.31 = (bf16[2,384,256]{2,1,0:T(8,128)(2,1)}, bf16[2,384,256]{2,1,0:T(8,128)(2,1)}, u32[]{:S(2)}, u32[]{:S(2)}) collective-permute-start(bf16[2,384,256]{2,1,0:T(8,128)(2,1)} %get-tuple-element.226), channel_id=1, source_target_pairs={{0,1},{1,0},{2,3},{3,2},{4,5},{5,4},{6,7},{7,6},{8,9},{9,8},{10,11... | collective-permute-start | bytes 1179656 | tf_op jit(solution)/shard_map/ppermute | solution.py:391
  172.3 20.1 %collective-permute-start.26 = (bf16[192,768]{1,0:T(8,128)(2,1)}, bf16[192,768]{1,0:T(8,128)(2,1)}, u32[]{:S(2)}, u32[]{:S(2)}) collective-permute-start(bf16[192,768]{1,0:T(8,128)(2,1)} %add_convert_fusion.6), channel_id=1, source_target_pairs={{0,16},{1,17},{2,18},{3,19},{4,20},{5,21},{6,22},{7,23},{8,24},{9,... | collective-permute-start | bytes 884744 | tf_op jit(solution)/shard_map/ppermute | solution.py:391
  174.4 18.0 %collective-permute-start.25 = (bf16[192,768]{1,0:T(8,128)(2,1)}, bf16[192,768]{1,0:T(8,128)(2,1)}, u32[]{:S(2)}, u32[]{:S(2)}) collective-permute-start(bf16[192,768]{1,0:T(8,128)(2,1)} %add_convert_fusion.7), channel_id=1, source_target_pairs={{0,8},{1,9},{2,10},{3,11},{4,12},{5,13},{6,14},{7,15},{8,0},{9,1},... | collective-permute-start | bytes 884744 | tf_op jit(solution)/shard_map/ppermute | solution.py:391
  192.3 22.5 %collective-permute-start.30 = (bf16[4,128,768]{2,1,0:T(8,128)(2,1)}, bf16[4,128,768]{2,1,0:T(8,128)(2,1)S(1)}, u32[]{:S(2)}, u32[]{:S(2)}) collective-permute-start(bf16[4,128,768]{2,1,0:T(8,128)(2,1)} %get-tuple-element.215), channel_id=1, source_target_pairs={{0,1},{1,0},{2,3},{3,2},{4,5},{5,4},{6,7},{7,6},{8,9},{9,8},{10,11... | collective-permute-start | bytes 2359304 | tf_op jit(solution)/shard_map/ppermute | solution.py:391
  194.7 20.1 %collective-permute-start.29 = (bf16[48,1536]{1,0:T(8,128)(2,1)S(1)}, bf16[48,1536]{1,0:T(8,128)(2,1)S(1)}, u32[]{:S(2)}, u32[]{:S(2)}) collective-permute-start(bf16[48,1536]{1,0:T(8,128)(2,1)S(1)} %pad_maximum_fusion.9), channel_id=1, source_target_pairs={{0,6},{1,7},{2,4},{3,5},{4,2},{5,3},{6,0},{7,1},{8,14},{9,15},{10,... | collective-permute-start | bytes 442376 | tf_op jit(solution)/shard_map/ppermute | solution.py:391
  198.1 16.8 %collective-permute-start.28 = (bf16[48,1536]{1,0:T(8,128)(2,1)S(1)}, bf16[48,1536]{1,0:T(8,128)(2,1)S(1)}, u32[]{:S(2)}, u32[]{:S(2)}) collective-permute-start(bf16[48,1536]{1,0:T(8,128)(2,1)S(1)} %pad_maximum_fusion.8), channel_id=1, source_target_pairs={{0,4},{1,5},{2,6},{3,7},{4,0},{5,1},{6,2},{7,3},{8,12},{9,13},{10,... | collective-permute-start | bytes 442376 | tf_op jit(solution)/shard_map/ppermute | solution.py:391
  214.8 18.3 %collective-permute-start.40 = (bf16[4,128,768]{2,1,0:T(8,128)(2,1)}, bf16[4,128,768]{2,1,0:T(8,128)(2,1)S(1)}, u32[]{:S(2)}, u32[]{:S(2)}) collective-permute-start(bf16[4,128,768]{2,1,0:T(8,128)(2,1)} %get-tuple-element.242), channel_id=1, source_target_pairs={{0,1},{1,0},{2,3},{3,2},{4,5},{5,4},{6,7},{7,6},{8,9},{9,8},{10,11... | collective-permute-start | bytes 2359304 | tf_op jit(solution)/shard_map/ppermute | solution.py:391
  215.8 25.4 %collective-permute-start.34 = (bf16[128,768]{1,0:T(8,128)(2,1)}, bf16[128,768]{1,0:T(8,128)(2,1)S(1)}, u32[]{:S(2)}, u32[]{:S(2)}) collective-permute-start(bf16[128,768]{1,0:T(8,128)(2,1)} %get-tuple-element.323), channel_id=1, source_target_pairs={{0,2},{1,3},{2,0},{3,1},{4,6},{5,7},{6,4},{7,5},{8,10},{9,11},{10,... | collective-permute-start | bytes 589832 | tf_op jit(solution)/shard_map/ppermute | solution.py:391
  233.1 16.7 %collective-permute-start.35 = (bf16[128,768]{1,0:T(8,128)(2,1)}, bf16[128,768]{1,0:T(8,128)(2,1)S(1)}, u32[]{:S(2)}, u32[]{:S(2)}) collective-permute-start(bf16[128,768]{1,0:T(8,128)(2,1)} %get-tuple-element.322), channel_id=1, source_target_pairs={{0,4},{1,5},{2,6},{3,7},{4,0},{5,1},{6,2},{7,3},{8,12},{9,13},{10,... | collective-permute-start | bytes 589832 | tf_op jit(solution)/shard_map/ppermute | solution.py:391
  233.2 18.0 %collective-permute-start.32 = (bf16[448,768]{1,0:T(8,128)(2,1)}, bf16[448,768]{1,0:T(8,128)(2,1)}, u32[]{:S(2)}, u32[]{:S(2)}) collective-permute-start(bf16[448,768]{1,0:T(8,128)(2,1)} %get-tuple-element.234), channel_id=1, source_target_pairs={{0,16},{1,17},{2,18},{3,19},{4,20},{5,21},{6,22},{7,23},{8,24},{9,... | collective-permute-start | bytes 2064392 | tf_op jit(solution)/shard_map/ppermute | solution.py:391
  234.1 17.0 %collective-permute-start.33 = (bf16[448,768]{1,0:T(8,128)(2,1)}, bf16[448,768]{1,0:T(8,128)(2,1)}, u32[]{:S(2)}, u32[]{:S(2)}) collective-permute-start(bf16[448,768]{1,0:T(8,128)(2,1)} %get-tuple-element.236), channel_id=1, source_target_pairs={{0,8},{1,9},{2,10},{3,11},{4,12},{5,13},{6,14},{7,15},{8,0},{9,1},... | collective-permute-start | bytes 2064392 | tf_op jit(solution)/shard_map/ppermute | solution.py:391
  241.2 31.0 %collective-permute-start.41 = (bf16[128,768]{1,0:T(8,128)(2,1)}, bf16[128,768]{1,0:T(8,128)(2,1)S(1)}, u32[]{:S(2)}, u32[]{:S(2)}) collective-permute-start(bf16[128,768]{1,0:T(8,128)(2,1)} %get-tuple-element.318), channel_id=1, source_target_pairs={{0,2},{1,3},{2,0},{3,1},{4,6},{5,7},{6,4},{7,5},{8,10},{9,11},{10,... | collective-permute-start | bytes 589832 | tf_op jit(solution)/shard_map/ppermute | solution.py:391
  249.8 22.5 %collective-permute-start.42 = (bf16[128,768]{1,0:T(8,128)(2,1)}, bf16[128,768]{1,0:T(8,128)(2,1)S(1)}, u32[]{:S(2)}, u32[]{:S(2)}) collective-permute-start(bf16[128,768]{1,0:T(8,128)(2,1)} %get-tuple-element.320), channel_id=1, source_target_pairs={{0,4},{1,5},{2,6},{3,7},{4,0},{5,1},{6,2},{7,3},{8,12},{9,13},{10,... | collective-permute-start | bytes 589832 | tf_op jit(solution)/shard_map/ppermute | solution.py:391
  250.5 21.8 %collective-permute-start.43 = (bf16[128,768]{1,0:T(8,128)(2,1)}, bf16[128,768]{1,0:T(8,128)(2,1)S(1)}, u32[]{:S(2)}, u32[]{:S(2)}) collective-permute-start(bf16[128,768]{1,0:T(8,128)(2,1)} %get-tuple-element.319), channel_id=1, source_target_pairs={{2,4},{3,5},{4,2},{5,3},{10,12},{11,13},{12,10},{13,11},{18,20},{1... | collective-permute-start | bytes 589832 | tf_op jit(solution)/shard_map/ppermute | solution.py:391
  (67 other events, 545.0 us)
Sparse Core Ops, SparseCore 0:
  36.4 46.1 all-gather.1
  170.5 43.7 reduce-scatter.1

commit v5 on v4

--- a/solution.py
+++ b/solution.py
@@ -1202,7 +1202,7 @@
     inner_block = lax.psum_scatter(inner_terms, "dp", scatter_dimension=0, tiled=True)
     outer_hop = after_both(outer_hop, (inner_terms,))
     outer_low = near_terms(outer_hop, 48)
-    dh_own = after(dh_own, inner_terms, *outer_low)
+    dh_own = after(dh_own, inner_terms)
     outer_sent = hop_terms(outer_low)
     dz1, do, do_half, da, sums1 = call(
         first_kernel,
@@ -1238,12 +1238,10 @@
     outer_half = after_both(outer_half, grads0[:1])
     outer_parts = line_parts(outer_half, 48)
     *grads1, dx1, dx_send, sums_q1 = back(1, (dx0, *outer_half))
-    outer_parts, got0, dx0 = after_both((outer_parts, got0, dx0), grads1[:1])
+    outer_parts = after_both(outer_parts, grads1[:1])
     got1 = send(dx_send, CORE)
-    low0 = core_sums(dx0, got0)
-    grads1, _ = lax.optimization_barrier((grads1, (outer_parts, low0, inner_block)))
+    grads1, _ = lax.optimization_barrier((grads1, (outer_parts, inner_block)))
     inner_parts = block_parts(inner_block)
-    sent0 = line_sums(low0)
 
     def widen(value):
         zero = jnp.zeros_like(value)
@@ -1270,7 +1268,8 @@
         cost=(3_300_000_000, 12_000_000),
     )(x_all, grads0[0], grads1[0], grads0[1], grads1[1], mix_low[0], mix_low[1], mix_other, do_half, jnp.concatenate([vec_first, vec_second]))
     square_hop = first_hop(square_terms)
-    inner_parts, got1 = after_both((inner_parts, got1), square_terms)
+    inner_parts, got0, got1 = after_both((inner_parts, got0, got1), square_terms)
+    sent0 = line_sums(core_sums(dx0, got0))
     sent1 = line_sums(core_sums(dx1, got1))
     square_hop, sent0 = after_both((square_hop, sent0), ())
     square_sent = hop_terms(near_terms(square_hop, 56))

time: 298 us -> 297 us (level)
  waiting for transfers between devices: 74.4 us -> 77.4 us
    ppermute x51, waiting for transfers between devices: 69.4 us -> 72.4 us  [send(): return lax.ppermute(value, BOTH, route)]
    unnamed x80 -> x84, local copies, waits for them, and re-layouts: 8.84 us -> 8.74 us
  transfers between devices with their start and end apart: 53 -> 53, of which waited for: 23 -> 24; matrix products, arithmetic and copies ran while one was open for 11% -> 11% of each run, Pallas kernels for 23% -> 23%
where the time goes in v5:
time: 297 us; the launch traced here: 296 us
  Pallas kernels  94.4 us (32%)
  waiting for transfers between devices  77.4 us (26%)
  starting transfers between devices  66 us (22%)
  local copies, waits for them, and re-layouts  23.8 us (8%)
  other arithmetic  18.4 us (6%)
  between operations  15.2 us (5%)
    ppermute x51, waiting for transfers between devices, send(): return lax.ppermute(value, BOTH, route)  72.4 us
    ppermute x51, starting transfers between devices, send(): return lax.ppermute(value, BOTH, route)  65.9 us
    pallas_call x2, Pallas kernels, back(): call(attend_back_kernel, [(shape, BF16) for shape in shapes] + [((8, 384)...  20.2 us
    pallas_call x1, Pallas kernels, per_device_paired(): call(attend_kernel, [((2, 384, 256), F32), ((2, 384, 256), BF16), ((2, 8,...  10.5 us
    pallas_call x1, Pallas kernels, per_device_paired(): call(forward_kernel, [((512, 768), F32), ((512, 1), F32), ((512, 768), BF...  10.4 us
    pallas_call x1, Pallas kernels, per_device_paired(): call(project_kernel, [((2, *head_shape), BF16), ((8, *head_shape), BF16),...  9.07 us
    pallas_call x1, Pallas kernels, per_device_paired(): call(projection_grad_kernel, [((448, 768), BF16)] * 4, 10, out_specs=[IN_...  8.84 us
    unnamed x84, local copies, waits for them, and re-layouts  8.74 us
  transfers between devices with their start and end apart: 53, of which 24 were waited for; matrix products, arithmetic and copies ran while one was open for 11% of the time, Pallas kernels for 23%

profile of v5, /device:TPU:0, one launch (start us, length us, event | category | flops | bytes accessed | tf_op | source)
XLA Modules:
  0.0 295.6 jit_solution(2351526292476589398)
XLA Ops:
  21.4 3.6 %collective-permute-done.3 = bf16[56,1536]{1,0:T(8,128)(2,1)S(1)} collective-permute-done((bf16[56,1536]{1,0:T(8,128)(2,1)}, bf16[56,1536]{1,0:T(8,128)(2,1)S(1)}, u32[]{:S(2)}, u32[]{:S(2)}) %collective-permute-start.3) | collective-permute-done | bytes 172064 | tf_op jit(solution)/shard_map/ppermute | solution.py:391
  25.0 9.5 %collective-permute-done.4 = bf16[56,1536]{1,0:T(8,128)(2,1)S(1)} collective-permute-done((bf16[56,1536]{1,0:T(8,128)(2,1)}, bf16[56,1536]{1,0:T(8,128)(2,1)S(1)}, u32[]{:S(2)}, u32[]{:S(2)}) %collective-permute-start.4) | collective-permute-done | bytes 172064 | tf_op jit(solution)/shard_map/ppermute | solution.py:391
  45.9 7.8 %collective-permute-done.6 = bf16[48,3072]{1,0:T(8,128)(2,1)S(1)} collective-permute-done((bf16[48,3072]{1,0:T(8,128)(2,1)S(1)}, bf16[48,3072]{1,0:T(8,128)(2,1)S(1)}, u32[]{:S(2)}, u32[]{:S(2)}) %collective-permute-start.6) | collective-permute-done | bytes 294944 | tf_op jit(solution)/shard_map/ppermute | solution.py:391
  53.7 11.9 %collective-permute-done.7 = bf16[48,3072]{1,0:T(8,128)(2,1)S(1)} collective-permute-done((bf16[48,3072]{1,0:T(8,128)(2,1)S(1)}, bf16[48,3072]{1,0:T(8,128)(2,1)S(1)}, u32[]{:S(2)}, u32[]{:S(2)}) %collective-permute-start.7) | collective-permute-done | bytes 294944 | tf_op jit(solution)/shard_map/ppermute | solution.py:391
  65.6 6.1 %collective-permute-start.10 = (bf16[2,128,768]{2,1,0:T(8,128)(2,1)}, bf16[2,128,768]{2,1,0:T(8,128)(2,1)S(1)}, u32[]{:S(2)}, u32[]{:S(2)}) collective-permute-start(bf16[2,128,768]{2,1,0:T(8,128)(2,1)} %bitcast.9.refs_0_), channel_id=1, source_target_pairs={{0,4},{1,5},{2,6},{3,7},{4,0},{5,1},{6,2},{7,3},{8,12},{9,13},{10,... | collective-permute-start | bytes 1179656 | tf_op jit(solution)/shard_map/ppermute | solution.py:391
  77.6 5.0 %all-gather.2.cloned.1.call-done.refs_6_.rows_ref = bf16[896,1536]{1,0:T(8,128)(2,1)} async-done(((bf16[224,1536]{1,0:T(8,128)(2,1)}), bf16[896,1536]{1,0:T(8,128)(2,1)}) %all-gather.2.cloned.1.call-update) | async-done | bytes 2752528 | tf_op jit(solution)/shard_map/all_gather | solution.py:442
  97.7 9.1 %shard_map.307 = (bf16[2,2,128,384]{3,2,1,0:T(8,128)(2,1)}, bf16[8,2,128,384]{3,2,1,0:T(8,128)(2,1)}, bf16[8,2,128,384]{3,2,1,0:T(8,128)(2,1)}, bf16[768,1536]{1,0:T(8,128)(2,1)}, bf16[8,2,128,768]{3,2,1,0:T(8,128)(2,1)}) custom-call(bf16[2,128,768]{2,1,0:T(8,128)(2,1)} %bitcast.9.refs_0_, bf16[2,128,768]{2,1,0:T(8,128)(2,1)} %collective-permute-done.2.refs_1_, ...), custom_call_target="tpu_custom_call" | custom-call | flops 2800000000 | bytes 16000000 | tf_op jit(solution)/shard_map/pallas_call | solution.py:1101
  112.1 10.5 %shard_map.308 = (f32[2,384,256]{2,1,0:T(8,128)}, bf16[2,384,256]{2,1,0:T(8,128)(2,1)}, f32[2,8,256]{2,1,0:T(8,128)}, bf16[2,2,128,768]{3,2,1,0:T(8,128)(2,1)}, bf16[384,768]{1,0:T(8,128)(2,1)}) custom-call(bf16[2,2,128,384]{3,2,1,0:T(8,128)(2,1)} %get-tuple-element.163.q_ref, bf16[8,2,128,384]{3,2,1,0:T(8,128)(2,1)} %get-tuple-element.164.k_ref, ...), custom_call_target="tpu_custom_call" | custom-call | flops 1900000000 | bytes 10000000 | tf_op jit(solution)/shard_map/pallas_call | solution.py:1131
  128.4 10.4 %shard_map.309 = (f32[512,768]{1,0:T(8,128)}, f32[512,1]{1,0:T(8,128)}, bf16[512,768]{1,0:T(8,128)(2,1)}, bf16[512,1536]{1,0:T(8,128)(2,1)}, bf16[512,1536]{1,0:...) custom-call(bf16[8,2,128,768]{3,2,1,0:T(8,128)(2,1)} %get-tuple-element.159.refs_0_.x_, ...), custom_call_target="tpu_custom_call" | custom-call | flops 2500000000 | bytes 16000000 | tf_op jit(solution)/shard_map/pallas_call | solution.py:1153
  142.3 5.1 %shard_map.310 = (bf16[256,768]{1,0:T(8,128)(2,1)}, bf16[512,768]{1,0:T(8,128)(2,1)}, f32[512,768]{1,0:T(8,128)}, f32[8,768]{1,0:T(8,128)}) custom-call(f32[512,768]{1,0:T(8,128)} %get-tuple-element.172.n1_ref, bf16[512,768]{1,0:T(8,128)(2,1)} %get-tuple-element.173.own_ref, bf16[512,768]{1,0:T(8,128)(2,1)} %copy-done.8, bf16[2,128,768]{2,1,0:T(8,128)(2,1)} %bitcast.132, ...), custom_call_target="tpu_custom_call" | custom-call | flops 50000000 | bytes 8000000 | tf_op jit(solution)/shard_map/pallas_call | solution.py:1172
  147.4 5.2 %shard_map.311 = (bf16[384,768]{1,0:T(8,128)(2,1)}, bf16[384,768]{1,0:T(8,128)(2,1)}, bf16[384,768]{1,0:T(8,128)(2,1)}, bf16[384,768]{1,0:T(8,128)(2,1)}) custom-call(bf16[512,1536]{1,0:T(8,128)(2,1)} %get-tuple-element.177.act_ref, bf16[512,768]{1,0:T(8,128)(2,1)} %get-tuple-element.182.df_ref), custom_call_target="tpu_custom_call" | custom-call | flops 1200000000 | bytes 6000000 | tf_op jit(solution)/shard_map/pallas_call | solution.py:1182
  156.6 7.6 %shard_map.312 = (bf16[512,1536]{1,0:T(8,128)(2,1)}, bf16[512,768]{1,0:T(8,128)(2,1)}, f32[1,1536]{1,0:T(1,128)}) custom-call(bf16[512,768]{1,0:T(8,128)(2,1)} %get-tuple-element.182.df_ref, bf16[512,1536]{1,0:T(8,128)(2,1)} %get-tuple-element.183.slope_ref, bf16[768,1536]{1,0:T(8,128)(2,1)} %get-tuple-element.184.w1_in, ...), custom_call_target="tpu_custom_call" | custom-call | flops 2400000000 | bytes 9000000 | tf_op jit(solution)/shard_map/pallas_call | solution.py:1191
  164.8 4.7 %shard_map.313 = bf16[768,1536]{1,0:T(8,128)(2,1)} custom-call(bf16[512,768]{1,0:T(8,128)(2,1)} %get-tuple-element.187.low_ref, bf16[512,1536]{1,0:T(8,128)(2,1)} %get-tuple-element.188.du_ref), custom_call_target="tpu_custom_call" | custom-call | flops 1200000000 | bytes 6000000 | tf_op jit(solution)/shard_map/pallas_call | solution.py:1201
  175.2 5.3 %shard_map.314 = (f32[256,768]{1,0:T(8,128)}, bf16[512,768]{1,0:T(8,128)(2,1)}, bf16[512,384]{1,0:T(8,128)(2,1)}, bf16[2,384,256]{2,1,0:T(8,128)(2,1)}, f32[8,768]{1,0:T(8,128)}) custom-call(f32[512,768]{1,0:T(8,128)} %get-tuple-element.175.dz_ref, bf16[512,768]{1,0:T(8,128)(2,1)} %get-tuple-element.189.own_ref, bf16[512,768]{1,0:T(8,128)(2,1)} %copy-done.11, ...), custom_call_target="tpu_custom_call" | custom-call | flops 300000000 | bytes 10000000 | tf_op jit(solution)/shard_map/pallas_call | solution.py:1207
  181.3 10.2 %shard_map.315 = (bf16[2,128,384]{2,1,0:T(8,128)(2,1)}, bf16[8,128,768]{2,1,0:T(8,128)(2,1)}, bf16[4,128,768]{2,1,0:T(8,128)(2,1)}, bf16[4,128,768]{2,1,0:T(8,128)(2,1)}, f32[8,384]{1,0:T(8,128)}) custom-call(bf16[2,2,128,384]{3,2,1,0:T(8,128)(2,1)} %get-tuple-element.163.q_ref, bf16[8,2,128,384]{3,2,1,0:T(8,128)(2,1)} %get-tuple-element.164.k_ref, ...), custom_call_target="tpu_custom_call" | custom-call | flops 3400000000 | bytes 10000000 | tf_op jit(solution)/shard_map/pallas_call | solution.py:1217
  193.8 3.4 %collective-permute-start.29 = (bf16[48,1536]{1,0:T(8,128)(2,1)S(1)}, bf16[48,1536]{1,0:T(8,128)(2,1)S(1)}, u32[]{:S(2)}, u32[]{:S(2)}) collective-permute-start(bf16[48,1536]{1,0:T(8,128)(2,1)S(1)} %pad_maximum_fusion.9), channel_id=1, source_target_pairs={{0,6},{1,7},{2,4},{3,5},{4,2},{5,3},{6,0},{7,1},{8,14},{9,15},{10,... | collective-permute-start | bytes 442376 | tf_op jit(solution)/shard_map/ppermute | solution.py:391
  197.2 4.4 %collective-permute-start.28 = (bf16[48,1536]{1,0:T(8,128)(2,1)S(1)}, bf16[48,1536]{1,0:T(8,128)(2,1)S(1)}, u32[]{:S(2)}, u32[]{:S(2)}) collective-permute-start(bf16[48,1536]{1,0:T(8,128)(2,1)S(1)} %pad_maximum_fusion.8), channel_id=1, source_target_pairs={{0,4},{1,5},{2,6},{3,7},{4,0},{5,1},{6,2},{7,3},{8,12},{9,13},{10,... | collective-permute-start | bytes 442376 | tf_op jit(solution)/shard_map/ppermute | solution.py:391
  201.8 10.0 %shard_map.316 = (bf16[2,128,384]{2,1,0:T(8,128)(2,1)}, bf16[8,128,768]{2,1,0:T(8,128)(2,1)}, bf16[4,128,768]{2,1,0:T(8,128)(2,1)}, bf16[4,128,768]{2,1,0:T(8,128)(2,1)}, f32[8,384]{1,0:T(8,128)}) custom-call(bf16[2,2,128,384]{3,2,1,0:T(8,128)(2,1)} %get-tuple-element.163.q_ref, bf16[8,2,128,384]{3,2,1,0:T(8,128)(2,1)} %get-tuple-element.164.k_ref, ...), custom_call_target="tpu_custom_call" | custom-call | flops 3400000000 | bytes 10000000 | tf_op jit(solution)/shard_map/pallas_call | solution.py:1217
  220.6 8.8 %shard_map.317 = (bf16[448,768]{1,0:T(8,128)(2,1)}, bf16[448,768]{1,0:T(8,128)(2,1)}, bf16[448,768]{1,0:T(8,128)(2,1)}, bf16[448,768]{1,0:T(8,128)(2,1)}) custom-call(bf16[8,2,128,768]{3,2,1,0:T(8,128)(2,1)} %get-tuple-element.159.refs_0_.x_ref, bf16[2,128,384]{2,1,0:T(8,128)(2,1)} %get-tuple-element.197.refs_0_, ...), custom_call_target="tpu_custom_call" | custom-call | flops 3300000000 | bytes 12000000 | tf_op jit(solution)/shard_map/pallas_call | solution.py:1262
  241.5 3.9 %collective-permute-done.38 = bf16[128,768]{1,0:T(8,128)(2,1)S(1)} collective-permute-done((bf16[128,768]{1,0:T(8,128)(2,1)}, bf16[128,768]{1,0:T(8,128)(2,1)S(1)}, u32[]{:S(2)}, u32[]{:S(2)}) %collective-permute-start.38) | collective-permute-done | bytes 196640 | tf_op jit(solution)/shard_map/ppermute | solution.py:391
  245.4 3.9 %collective-permute-done.39 = bf16[128,768]{1,0:T(8,128)(2,1)S(1)} collective-permute-done((bf16[128,768]{1,0:T(8,128)(2,1)}, bf16[128,768]{1,0:T(8,128)(2,1)S(1)}, u32[]{:S(2)}, u32[]{:S(2)}) %collective-permute-start.39) | collective-permute-done | bytes 196640 | tf_op jit(solution)/shard_map/ppermute | solution.py:391
  255.9 7.2 %collective-permute-done.45 = bf16[224,768]{1,0:T(8,128)(2,1)S(1)} collective-permute-done((bf16[224,768]{1,0:T(8,128)(2,1)S(1)}, bf16[224,768]{1,0:T(8,128)(2,1)S(1)}, u32[]{:S(2)}, u32[]{:S(2)}) %collective-permute-start.45) | collective-permute-done | bytes 344096 | tf_op jit(solution)/shard_map/ppermute | solution.py:391
  266.1 9.5 %collective-permute-start.47 = (bf16[56,1536]{1,0:T(8,128)(2,1)S(1)}, bf16[56,1536]{1,0:T(8,128)(2,1)}, u32[]{:S(2)}, u32[]{:S(2)}) collective-permute-start(bf16[56,1536]{1,0:T(8,128)(2,1)S(1)} %maximum_maximum_fusion.1), channel_id=1, source_target_pairs={{0,4},{1,5},{2,6},{3,7},{4,0},{5,1},{6,2},{7,3},{8,12},{9,13},{10,... | collective-permute-start | bytes 516104 | tf_op jit(solution)/shard_map/ppermute | solution.py:391
  277.0 5.8 %collective-permute-done.47.refs_1_ = bf16[56,1536]{1,0:T(8,128)(2,1)} collective-permute-done((bf16[56,1536]{1,0:T(8,128)(2,1)S(1)}, bf16[56,1536]{1,0:T(8,128)(2,1)}, u32[]{:S(2)}, u32[]{:S(2)}) %collective-permute-start.47) | collective-permute-done | bytes 172064 | tf_op jit(solution)/shard_map/ppermute | solution.py:391
  (295 shorter events, 111.4 us)
Async XLA Ops:
  7.2 75.4 %all-gather.2.cloned.1.call-start = ((), (), s32[]{:S(2)}) async-start(), calls=%async_computation.1 | async-start | bytes 3440640 | tf_op jit(solution)/shard_map/all_gather | solution.py:442
  36.3 178.6 %reduce-scatter.2.cloned.1.call-start = ((), (), s32[]{:S(2)}) async-start(), calls=%async_computation.2 | async-start | bytes 2949120 | tf_op jit(solution)/shard_map/reduce_scatter | solution.py:1202
  42.1 23.5 %collective-permute-start.7 = (bf16[48,3072]{1,0:T(8,128)(2,1)S(1)}, bf16[48,3072]{1,0:T(8,128)(2,1)S(1)}, u32[]{:S(2)}, u32[]{:S(2)}) collective-permute-start(bf16[48,3072]{1,0:T(8,128)(2,1)S(1)} %pad_maximum_fusion.4), channel_id=1, source_target_pairs={{0,4},{1,5},{2,6},{3,7},{4,0},{5,1},{6,2},{7,3},{8,12},{9,13},{10,... | collective-permute-start | bytes 884744 | tf_op jit(solution)/shard_map/ppermute | solution.py:391
  43.1 22.5 %collective-permute-start.8 = (bf16[48,3072]{1,0:T(8,128)(2,1)S(1)}, bf16[48,3072]{1,0:T(8,128)(2,1)S(1)}, u32[]{:S(2)}, u32[]{:S(2)}) collective-permute-start(bf16[48,3072]{1,0:T(8,128)(2,1)S(1)} %pad_maximum_fusion.4), channel_id=1, source_target_pairs={{0,6},{1,7},{2,4},{3,5},{4,2},{5,3},{6,0},{7,1},{8,14},{9,15},{10,... | collective-permute-start | bytes 884744 | tf_op jit(solution)/shard_map/ppermute | solution.py:391
  65.6 23.2 %collective-permute-start.10 = (bf16[2,128,768]{2,1,0:T(8,128)(2,1)}, bf16[2,128,768]{2,1,0:T(8,128)(2,1)S(1)}, u32[]{:S(2)}, u32[]{:S(2)}) collective-permute-start(bf16[2,128,768]{2,1,0:T(8,128)(2,1)} %bitcast.9.refs_0_), channel_id=1, source_target_pairs={{0,4},{1,5},{2,6},{3,7},{4,0},{5,1},{6,2},{7,3},{8,12},{9,13},{10,... | collective-permute-start | bytes 1179656 | tf_op jit(solution)/shard_map/ppermute | solution.py:391
  71.7 18.4 %collective-permute-start.11 = (bf16[2,128,768]{2,1,0:T(8,128)(2,1)}, bf16[2,128,768]{2,1,0:T(8,128)(2,1)}, u32[]{:S(2)}, u32[]{:S(2)}) collective-permute-start(bf16[2,128,768]{2,1,0:T(8,128)(2,1)} %bitcast.9.refs_0_), channel_id=1, source_target_pairs={{2,4},{3,5},{4,2},{5,3},{10,12},{11,13},{12,10},{13,11},{18,20},{1... | collective-permute-start | bytes 1179656 | tf_op jit(solution)/shard_map/ppermute | solution.py:391
  73.1 17.0 %collective-permute-start.9 = (bf16[2,128,768]{2,1,0:T(8,128)(2,1)}, bf16[2,128,768]{2,1,0:T(8,128)(2,1)}, u32[]{:S(2)}, u32[]{:S(2)}) collective-permute-start(bf16[2,128,768]{2,1,0:T(8,128)(2,1)} %bitcast.9.refs_0_), channel_id=1, source_target_pairs={{0,2},{1,3},{2,0},{3,1},{4,6},{5,7},{6,4},{7,5},{8,10},{9,11},{10,... | collective-permute-start | bytes 1179656 | tf_op jit(solution)/shard_map/ppermute | solution.py:391
  74.4 17.0 %collective-permute-start.13 = (bf16[192,1536]{1,0:T(8,128)(2,1)S(1)}, bf16[192,1536]{1,0:T(8,128)(2,1)S(1)}, u32[]{:S(2)}, u32[]{:S(2)}) collective-permute-start(bf16[192,1536]{1,0:T(8,128)(2,1)S(1)} %pad_maximum_fusion.2.refs_9_), channel_id=1, source_target_pairs={{0,16},{1,17},{2,18},{3,19},{4,20},{5,21},{6,22},{7,23},{8,24},{9,... | collective-permute-start | bytes 1769480 | tf_op jit(solution)/shard_map/ppermute | solution.py:391
  93.1 15.8 %collective-permute-start.17 = (bf16[192,1536]{1,0:T(8,128)(2,1)S(1)}, bf16[192,1536]{1,0:T(8,128)(2,1)}, u32[]{:S(2)}, u32[]{:S(2)}) collective-permute-start(bf16[192,1536]{1,0:T(8,128)(2,1)S(1)} %pad_maximum_fusion.2.refs_9_), channel_id=1, source_target_pairs={{0,8},{1,9},{2,10},{3,11},{4,12},{5,13},{6,14},{7,15},{8,0},{9,1},... | collective-permute-start | bytes 1769480 | tf_op jit(solution)/shard_map/ppermute | solution.py:391
  152.6 17.8 %collective-permute-start.23 = (bf16[384,768]{1,0:T(8,128)(2,1)}, bf16[384,768]{1,0:T(8,128)(2,1)S(1)}, u32[]{:S(2)}, u32[]{:S(2)}) collective-permute-start(bf16[384,768]{1,0:T(8,128)(2,1)} %get-tuple-element.179), channel_id=1, source_target_pairs={{0,16},{1,17},{2,18},{3,19},{4,20},{5,21},{6,22},{7,23},{8,24},{9,... | collective-permute-start | bytes 1769480 | tf_op jit(solution)/shard_map/ppermute | solution.py:391
  154.1 16.3 %collective-permute-start.24 = (bf16[384,768]{1,0:T(8,128)(2,1)}, bf16[384,768]{1,0:T(8,128)(2,1)S(1)}, u32[]{:S(2)}, u32[]{:S(2)}) collective-permute-start(bf16[384,768]{1,0:T(8,128)(2,1)} %get-tuple-element.181), channel_id=1, source_target_pairs={{0,8},{1,9},{2,10},{3,11},{4,12},{5,13},{6,14},{7,15},{8,0},{9,1},... | collective-permute-start | bytes 1769480 | tf_op jit(solution)/shard_map/ppermute | solution.py:391
  156.6 62.1 %collective-permute-start.30 = (bf16[2,384,256]{2,1,0:T(8,128)(2,1)}, bf16[2,384,256]{2,1,0:T(8,128)(2,1)}, u32[]{:S(2)}, u32[]{:S(2)}) collective-permute-start(bf16[2,384,256]{2,1,0:T(8,128)(2,1)} %get-tuple-element.222), channel_id=1, source_target_pairs={{0,1},{1,0},{2,3},{3,2},{4,5},{5,4},{6,7},{7,6},{8,9},{9,8},{10,11... | collective-permute-start | bytes 1179656 | tf_op jit(solution)/shard_map/ppermute | solution.py:391
  171.5 20.1 %collective-permute-start.26 = (bf16[192,768]{1,0:T(8,128)(2,1)}, bf16[192,768]{1,0:T(8,128)(2,1)}, u32[]{:S(2)}, u32[]{:S(2)}) collective-permute-start(bf16[192,768]{1,0:T(8,128)(2,1)} %add_convert_fusion.6), channel_id=1, source_target_pairs={{0,16},{1,17},{2,18},{3,19},{4,20},{5,21},{6,22},{7,23},{8,24},{9,... | collective-permute-start | bytes 884744 | tf_op jit(solution)/shard_map/ppermute | solution.py:391
  173.6 18.0 %collective-permute-start.25 = (bf16[192,768]{1,0:T(8,128)(2,1)}, bf16[192,768]{1,0:T(8,128)(2,1)}, u32[]{:S(2)}, u32[]{:S(2)}) collective-permute-start(bf16[192,768]{1,0:T(8,128)(2,1)} %add_convert_fusion.7), channel_id=1, source_target_pairs={{0,8},{1,9},{2,10},{3,11},{4,12},{5,13},{6,14},{7,15},{8,0},{9,1},... | collective-permute-start | bytes 884744 | tf_op jit(solution)/shard_map/ppermute | solution.py:391
  191.5 37.9 %collective-permute-start.36 = (bf16[4,128,768]{2,1,0:T(8,128)(2,1)}, bf16[4,128,768]{2,1,0:T(8,128)(2,1)S(1)}, u32[]{:S(2)}, u32[]{:S(2)}) collective-permute-start(bf16[4,128,768]{2,1,0:T(8,128)(2,1)} %get-tuple-element.233), channel_id=1, source_target_pairs={{0,1},{1,0},{2,3},{3,2},{4,5},{5,4},{6,7},{7,6},{8,9},{9,8},{10,11... | collective-permute-start | bytes 2359304 | tf_op jit(solution)/shard_map/ppermute | solution.py:391
  193.8 20.2 %collective-permute-start.29 = (bf16[48,1536]{1,0:T(8,128)(2,1)S(1)}, bf16[48,1536]{1,0:T(8,128)(2,1)S(1)}, u32[]{:S(2)}, u32[]{:S(2)}) collective-permute-start(bf16[48,1536]{1,0:T(8,128)(2,1)S(1)} %pad_maximum_fusion.9), channel_id=1, source_target_pairs={{0,6},{1,7},{2,4},{3,5},{4,2},{5,3},{6,0},{7,1},{8,14},{9,15},{10,... | collective-permute-start | bytes 442376 | tf_op jit(solution)/shard_map/ppermute | solution.py:391
  197.2 16.8 %collective-permute-start.28 = (bf16[48,1536]{1,0:T(8,128)(2,1)S(1)}, bf16[48,1536]{1,0:T(8,128)(2,1)S(1)}, u32[]{:S(2)}, u32[]{:S(2)}) collective-permute-start(bf16[48,1536]{1,0:T(8,128)(2,1)S(1)} %pad_maximum_fusion.8), channel_id=1, source_target_pairs={{0,4},{1,5},{2,6},{3,7},{4,0},{5,1},{6,2},{7,3},{8,12},{9,13},{10,... | collective-permute-start | bytes 442376 | tf_op jit(solution)/shard_map/ppermute | solution.py:391
  214.0 16.3 %collective-permute-start.37 = (bf16[4,128,768]{2,1,0:T(8,128)(2,1)}, bf16[4,128,768]{2,1,0:T(8,128)(2,1)S(1)}, u32[]{:S(2)}, u32[]{:S(2)}) collective-permute-start(bf16[4,128,768]{2,1,0:T(8,128)(2,1)} %get-tuple-element.234), channel_id=1, source_target_pairs={{0,1},{1,0},{2,3},{3,2},{4,5},{5,4},{6,7},{7,6},{8,9},{9,8},{10,11... | collective-permute-start | bytes 2359304 | tf_op jit(solution)/shard_map/ppermute | solution.py:391
  229.4 20.6 %collective-permute-start.31 = (bf16[448,768]{1,0:T(8,128)(2,1)}, bf16[448,768]{1,0:T(8,128)(2,1)}, u32[]{:S(2)}, u32[]{:S(2)}) collective-permute-start(bf16[448,768]{1,0:T(8,128)(2,1)} %get-tuple-element.230), channel_id=1, source_target_pairs={{0,16},{1,17},{2,18},{3,19},{4,20},{5,21},{6,22},{7,23},{8,24},{9,... | collective-permute-start | bytes 2064392 | tf_op jit(solution)/shard_map/ppermute | solution.py:391
  230.3 19.7 %collective-permute-start.32 = (bf16[448,768]{1,0:T(8,128)(2,1)}, bf16[448,768]{1,0:T(8,128)(2,1)}, u32[]{:S(2)}, u32[]{:S(2)}) collective-permute-start(bf16[448,768]{1,0:T(8,128)(2,1)} %get-tuple-element.232), channel_id=1, source_target_pairs={{0,8},{1,9},{2,10},{3,11},{4,12},{5,13},{6,14},{7,15},{8,0},{9,1},... | collective-permute-start | bytes 2064392 | tf_op jit(solution)/shard_map/ppermute | solution.py:391
  245.4 30.3 %collective-permute-start.41 = (bf16[128,768]{1,0:T(8,128)(2,1)}, bf16[128,768]{1,0:T(8,128)(2,1)S(1)}, u32[]{:S(2)}, u32[]{:S(2)}) collective-permute-start(bf16[128,768]{1,0:T(8,128)(2,1)} %get-tuple-element.320), channel_id=1, source_target_pairs={{0,2},{1,3},{2,0},{3,1},{4,6},{5,7},{6,4},{7,5},{8,10},{9,11},{10,... | collective-permute-start | bytes 589832 | tf_op jit(solution)/shard_map/ppermute | solution.py:391
  249.3 26.4 %collective-permute-start.42 = (bf16[128,768]{1,0:T(8,128)(2,1)}, bf16[128,768]{1,0:T(8,128)(2,1)S(1)}, u32[]{:S(2)}, u32[]{:S(2)}) collective-permute-start(bf16[128,768]{1,0:T(8,128)(2,1)} %get-tuple-element.322), channel_id=1, source_target_pairs={{0,4},{1,5},{2,6},{3,7},{4,0},{5,1},{6,2},{7,3},{8,12},{9,13},{10,... | collective-permute-start | bytes 589832 | tf_op jit(solution)/shard_map/ppermute | solution.py:391
  249.3 26.4 %collective-permute-start.43 = (bf16[128,768]{1,0:T(8,128)(2,1)}, bf16[128,768]{1,0:T(8,128)(2,1)S(1)}, u32[]{:S(2)}, u32[]{:S(2)}) collective-permute-start(bf16[128,768]{1,0:T(8,128)(2,1)} %get-tuple-element.321), channel_id=1, source_target_pairs={{2,4},{3,5},{4,2},{5,3},{10,12},{11,13},{12,10},{13,11},{18,20},{1... | collective-permute-start | bytes 589832 | tf_op jit(solution)/shard_map/ppermute | solution.py:391
  266.1 16.7 %collective-permute-start.47 = (bf16[56,1536]{1,0:T(8,128)(2,1)S(1)}, bf16[56,1536]{1,0:T(8,128)(2,1)}, u32[]{:S(2)}, u32[]{:S(2)}) collective-permute-start(bf16[56,1536]{1,0:T(8,128)(2,1)S(1)} %maximum_maximum_fusion.1), channel_id=1, source_target_pairs={{0,4},{1,5},{2,6},{3,7},{4,0},{5,1},{6,2},{7,3},{8,12},{9,13},{10,... | collective-permute-start | bytes 516104 | tf_op jit(solution)/shard_map/ppermute | solution.py:391
  (69 other events, 561.0 us)
Sparse Core Ops, SparseCore 0:
  36.4 46.1 all-gather.1
  169.7 43.7 reduce-scatter.1
